TPU v7x, 32 devices: a whole 2x2x4 slice. The times are simulated.
32 devices in a mesh: row: 16 (over z, y, core), col: 2 (over x).
Axes of the slice: x: 2, y: 2, z: 4, core: 2. Of those that a mesh axis runs over, the one named last changes fastest.
Arguments:
- damping: bfloat16 [1536, 128, 1536], P('col', 'row'), may hold values from -60 to 60
- block_seeds: int32 [32], replicated, may hold values from 1 to 65520
Outputs:
- basis: float32 [32, 1536, 32], P('row', 'col')
All inputs are finite; a program needn't handle non-finite values.
Results may differ from a plain program's by a relative error of at most 0.0057.
Values may be sent and summed in bfloat16 or wider, within the bound.
No kernel may reach another device: no remote copies, remote signals or barrier semaphores. Data moves between devices by JAX's collectives and lax.ppermute only.
A program may use at most 192 MiB of HBM per device.

v0:
```python
import math

import jax
import jax.numpy as jnp
from jax import lax
from jax.sharding import PartitionSpec as P

NF = 128
M = 1536
P_SIZE = 32
NB = 32
NSTEPS = 12


def lag_table():
    lag_idx = jnp.arange(2 * NB, dtype=jnp.float32)[:, None]
    freq_idx = jnp.arange(NF, dtype=jnp.float32)[None, :]
    window = jnp.exp(-math.log(3.0) * lag_idx / NB)
    cos_table = (
        jnp.cos(math.pi * (freq_idx + 0.5) * lag_idx / NF)
        * window
        * math.sqrt(2.0 / NF)
        / math.sqrt(NB * M)
    )
    return cos_table.astype(jnp.bfloat16)


def probe_blocks(block_seeds, start_col, number):
    prime_mod = 65521
    column = (start_col + jnp.arange(number, dtype=jnp.int32))[None, :, None]
    probe_col = jnp.arange(P_SIZE, dtype=jnp.int32)[None, None, :]
    seed_col = block_seeds[:, None, None]
    inner_part = seed_col * (column + 1) % prime_mod * (column + 3) % prime_mod
    phase_val = (
        inner_part * (probe_col + 1) + seed_col * (probe_col + 1) % prime_mod * (probe_col + 2)
    ) % prime_mod
    return jnp.cos(2.0 * math.pi * phase_val.astype(jnp.float32) / prime_mod).astype(jnp.bfloat16)


def hankel_stack(blocks, group_len):
    extent = blocks.shape[0] + group_len - 1
    padded = jnp.pad(blocks, ((group_len - 1, group_len - 1), (0, 0), (0, 0)))
    shifted = [
        padded[group_len - 1 - offset : group_len - 1 - offset + extent]
        for offset in range(group_len)
    ]
    return jnp.stack(shifted, axis=2).reshape(extent, blocks.shape[1], group_len * blocks.shape[2])


def hankel_pass(lag_tiles, stack, shift_by, form, group_len):
    extent = stack.shape[0]
    pieces = []
    for group in range(NB // group_len):
        start_lag = group * group_len + shift_by
        window_lags = lag_tiles[start_lag : start_lag + extent]
        product = jnp.einsum(form, window_lags, stack, preferred_element_type=jnp.float32)
        pieces.append(product.reshape(product.shape[0], group_len, P_SIZE).transpose(1, 0, 2))
    return jnp.concatenate(pieces, axis=0)


def gram_of(blocks):
    return jnp.einsum("bcp,bcq->pq", blocks, blocks, precision=lax.Precision.HIGHEST)


def finish(mine, gram):
    highest = lax.Precision.HIGHEST
    scale = jnp.trace(gram) + 1e-06
    current = gram / scale
    eye_mat = jnp.eye(P_SIZE, dtype=jnp.float32)
    inverse = eye_mat
    for repeat in range(NSTEPS):
        weight = 1.5 * eye_mat - 0.5 * jnp.dot(inverse, current, precision=highest)
        current = jnp.dot(current, weight, precision=highest)
        inverse = jnp.dot(weight, inverse, precision=highest)
    factor = math.sqrt(NB * M) / jnp.sqrt(scale)
    return factor * jnp.einsum("bcp,pq->bcq", mine, inverse, precision=highest)


def shards(damping, block_seeds):
    group_len = min(16, NB)
    tile_cols = damping.shape[0]
    cos_table = lag_table()
    lag_tiles = jnp.einsum(
        "lk,nkr->lrn",
        cos_table,
        lax.all_to_all(damping, "row", split_axis=2, concat_axis=1, tiled=True),
        preferred_element_type=jnp.float32,
    ).astype(jnp.bfloat16)
    local_probes = probe_blocks(block_seeds, lax.axis_index("col") * tile_cols, tile_cols)
    partial_rows = hankel_pass(
        lag_tiles, hankel_stack(local_probes, group_len), 0, "lrc,lcn->rn", group_len
    )
    forward_b = lax.psum(partial_rows, "col").astype(jnp.bfloat16)
    partial_cols = hankel_pass(
        lag_tiles, hankel_stack(forward_b, group_len), 1, "lrc,lrn->cn", group_len
    )
    mine = lax.psum_scatter(partial_cols, "row", scatter_dimension=0, tiled=True)
    gram = lax.psum(gram_of(mine), ("row", "col"))
    return finish(mine, gram)


def solution(mesh):
    return jax.shard_map(
        shards,
        mesh=mesh,
        in_specs=(P("col", "row", None), P()),
        out_specs=P("row", "col", None),
        check_vma=False,
    )
```

profile of v0, /device:TPU:0, one launch (start us, length us, event | category | flops | bytes accessed | tf_op | source)
XLA Modules:
  0.0 696.3 jit_solution(12683558152289276993)
XLA Ops:
  6.5 26.8 %copy.35 = bf16[768,8,1536]{0,1,2:T(8,128)(2,1)} copy(bf16[768,8,1536]{2,1,0:T(8,128)(2,1)} %param.2) | data formatting | bytes 37748736 | tf_op args[0]
  33.3 7.6 %all-to-all-start = ((bf16[768,8,1536]{0,1,2:T(8,128)(2,1)}), bf16[768,8,1536]{0,1,2:T(8,128)(2,1)}, u32[]{:S(2)}, u32[]{:S(2)}) async-start(bf16[768,8,1536]{0,1,2:T(8,128)(2,1)} %copy.35), calls=%async_computation | async-start | bytes 37748736 | tf_op jit(solution)/shard_map/all_to_all | solution.py:86
  41.1 0.2 add_select_fusion.1
  41.3 12.4 %fusion.23 = bf16[32,768,32]{1,2,0:T(8,128)(2,1)S(1)} fusion(s32[32,32]{1,0:T(8,128)S(1)} %fusion.133, s32[32]{0:T(128)S(1)} %get-tuple-element.10, s32[32,768]{1,0:T(8,128)S(1)} %add_select_fusion.1), kind=kLoop, calls=%fused_computation.39 | loop fusion | flops 8650752 | bytes 1675392 | tf_op jit(solution)/shard_map/convert_element_type | solution.py:37
  53.7 1.7 fusion.28
  55.4 1.7 fusion.30
  57.1 1.7 fusion.32
  58.7 1.7 fusion.34
  60.4 1.7 fusion.36
  62.1 1.7 fusion.38
  63.8 1.7 fusion.40
  65.5 1.7 fusion.42
  67.2 1.7 fusion.44
  68.9 1.7 fusion.46
  70.6 1.7 fusion.48
  72.3 1.7 fusion.50
  74.0 1.7 fusion.52
  75.6 1.7 fusion.54
  77.3 1.7 fusion.56
  79.0 1.7 fusion.58
  80.7 293.4 %all-to-all-done = bf16[768,8,1536]{0,1,2:T(8,128)(2,1)} async-done(((bf16[768,8,1536]{0,1,2:T(8,128)(2,1)}), bf16[768,8,1536]{0,1,2:T(8,128)(2,1)}, u32[]{:S(2)}, u32[]{:S(2)}) %all-to-all-start) | async-done | bytes 18874400 | tf_op jit(solution)/shard_map/all_to_all | solution.py:86
  374.1 18.7 %copy.37 = bf16[768,16,8,96]{0,3,2,1:T(8,128)(2,1)} copy(bf16[768,16,8,96]{0,2,3,1:T(8,128)(2,1)} %bitcast.41) | data formatting | bytes 37748736 | tf_op jit(solution)/shard_map/all_to_all | solution.py:86
  392.8 15.6 %convert_bitcast_fusion = bf16[64,96,768]{2,0,1:T(8,128)(2,1)S(1)} fusion(bf16[768,128,96]{0,2,1:T(8,128)(2,1)} %bitcast.321, f32[64]{0:T(128)S(1)} %multiply_exponential_fusion, f32[128]{0:T(128)S(1)} %add_multiply_fusion), kind=kOutput, calls=%fused_computation.6 | convolution fusion | flops 1212719104 | bytes 28312320 | tf_op jit(solution)/shard_map/lk,nkr->lrn/dot_general | solution.py:83
  408.3 8.6 %fusion.147 = (bf16[47,96,768]{2,0,1:T(8,128)(2,1)}, bf16[47,96,768]{2,0,1:T(8,128)(2,1)}, bf16[47,96,768]{2,0,1:T(8,128)(2,1)}, bf16[47,96,768]{2,0,1:T(8,128)(2,1)S(1)}) fusion(bf16[64,96,768]{2,0,1:T(8,128)(2,1)S(1)} %convert_bitcast_fusion), kind=kLoop, calls=%fused_computation.194 | loop fusion | bytes 55443456 | tf_op jit(solution)/shard_map/slice | solution.py:55
  417.0 22.3 %fusion.69 = f32[16,96,32]{1,2,0:T(8,128)S(1)} fusion(bf16[47,768,16,32]{1,3,2,0:T(8,128)(2,1)} %fusion.58, bf16[47,96,768]{2,0,1:T(8,128)(2,1)} %get-tuple-element.7), kind=kOutput, calls=%fused_computation.95 | convolution fusion | flops 3548381184 | bytes 44089344 | tf_op jit(solution)/shard_map/lrc,lcn->rn/dot_general | solution.py:56
  439.2 15.9 %fusion.74 = f32[16,96,32]{1,2,0:T(8,128)S(1)} fusion(bf16[47,768,16,32]{1,3,2,0:T(8,128)(2,1)} %fusion.58, bf16[47,96,768]{2,0,1:T(8,128)(2,1)S(1)} %get-tuple-element.8), kind=kOutput, calls=%fused_computation.96 | convolution fusion | flops 3548381184 | bytes 44089344 | tf_op jit(solution)/shard_map/lrc,lcn->rn/dot_general | solution.py:56
  455.2 19.4 %all-reduce.3 = bf16[32,96,32]{1,2,0:T(8,128)(2,1)S(1)} all-reduce(f32[32,96,32]{1,2,0:T(8,128)S(1)} %pad_maximum_fusion.1), channel_id=1, replica_groups=mesh['row'=16,'col'=2] {'col'}, use_global_device_ids=true, to_apply=%region_0.1 | all-reduce | flops 98304 | bytes 589824 | tf_op jit(solution)/shard_map/psum | solution.py:93
  476.1 16.9 %fusion.59 = f32[16,768,32]{1,2,0:T(8,128)S(1)} fusion(bf16[47,96,16,32]{1,3,0,2:T(8,128)(2,1)S(1)} %fusion.122, bf16[47,96,768]{2,0,1:T(8,128)(2,1)} %get-tuple-element.5), kind=kOutput, calls=%fused_computation.77 | convolution fusion | flops 3548381184 | bytes 13123584 | tf_op jit(solution)/shard_map/lrc,lrn->cn/dot_general | solution.py:56
  493.1 6.2 fusion.64
  499.3 1.9 pad_maximum_fusion
  501.2 138.3 %reduce-scatter.2.cloned.1.call-done = f32[2,768,32]{1,2,0:T(8,128)} async-done(((f32[32,768,32]{1,2,0:T(8,128)}), f32[2,768,32]{1,2,0:T(8,128)}) %reduce-scatter.2.cloned.1.call-update) | async-done | bytes 196624 | tf_op jit(solution)/shard_map/reduce_scatter | solution.py:97
  639.5 1.3 convolution_bitcast_fusion.1
  640.8 39.8 %psum.15 = f32[32,32]{1,0:T(8,128)S(1)} all-reduce(f32[32,32]{1,0:T(8,128)S(1)} %convolution_bitcast_fusion.1), channel_id=1, replica_groups=mesh['row'=16,'col'=2] {'row','col'}, use_global_device_ids=true, to_apply=%region_2.3 | all-reduce | flops 1024 | bytes 8192 | tf_op jit(solution)/shard_map/psum | solution.py:98
  680.6 0.6 select_reduce_fusion
  682.0 0.1 fusion.142
  682.2 0.1 fusion.140
  682.3 0.2 fusion.89
  682.5 0.1 fusion.149
  682.6 0.1 fusion.148
  682.8 0.2 fusion.88
  683.1 0.1 fusion.150
  683.2 0.2 fusion.87
  683.4 0.1 fusion.153
  683.5 0.1 fusion.152
  683.7 0.2 fusion.86
  683.9 0.1 fusion.155
  684.0 0.1 fusion.154
  684.1 0.2 fusion.85
  684.3 0.1 fusion.157
  684.5 0.1 fusion.156
  684.6 0.2 fusion.84
  684.8 0.1 fusion.159
  684.9 0.1 fusion.158
  685.1 0.2 fusion.83
  685.4 0.1 fusion.160
  685.5 0.2 fusion.82
  685.8 0.1 fusion.162
  686.0 0.2 fusion.81
  686.1 0.1 fusion.165
  686.3 0.1 fusion.164
  686.4 0.2 fusion.80
  686.7 0.1 fusion.166
  687.1 0.2 convolution_bitcast_fusion
  687.3 1.9 convolution_multiply_fusion
  (37 shorter events, 2.5 us)
Async XLA Ops:
  33.3 7.7 %copy-start = (s32[32]{0:T(128)S(1)}, s32[32]{0:T(128)}, u32[]{:S(2)}) copy-start(s32[32]{0:T(128)} %param.3) | copy-start | bytes 388
  33.3 340.8 %all-to-all-start = ((bf16[768,8,1536]{0,1,2:T(8,128)(2,1)}), bf16[768,8,1536]{0,1,2:T(8,128)(2,1)}, u32[]{:S(2)}, u32[]{:S(2)}) async-start(bf16[768,8,1536]{0,1,2:T(8,128)(2,1)} %copy.35), calls=%async_computation | async-start | bytes 37748736 | tf_op jit(solution)/shard_map/all_to_all | solution.py:86
  40.9 598.6 %reduce-scatter.2.cloned.1.call-start = ((), (), s32[]{:S(2)}) async-start(), calls=%async_computation.2 | async-start | bytes 3342336 | tf_op jit(solution)/shard_map/reduce_scatter | solution.py:97
  475.6 17.4 %slice-start = ((s8[7077888]{0:T(1024)(128)(4,1)}), s8[4194304]{0:T(1024)(128)(4,1)S(1)}, s32[]{:S(2)}) async-start(s8[7077888]{0:T(1024)(128)(4,1)} %bitcast.322), calls=%async_computation.3 | async-start | bytes 8388608
  476.1 16.9 %slice-start.1 = ((s8[7077888]{0:T(1024)(128)(4,1)}), s8[2883584]{0:T(1024)(128)(4,1)S(1)}, s32[]{:S(2)}) async-start(s8[7077888]{0:T(1024)(128)(4,1)} %bitcast.322), calls=%async_computation.4 | async-start | bytes 5767168
Sparse Core Ops, SparseCore 0:
  501.3 138.1 reduce-scatter.1
where the time goes:
time: 705 us; the launch traced here: 696 us
  waiting for transfers between devices  432 us (61%)
  matrix products  85.3 us (12%)
  local copies, waits for them, and re-layouts  82.6 us (12%)
  blocking collectives  59.2 us (8%)
  other arithmetic  15.2 us (2%)
  between operations  14.6 us (2%)
  starting transfers between devices  7.63 us (1%)
    all_to_all x1, waiting for transfers between devices, shards(): lax.all_to_all(damping, 'row', split_axis=2, concat_axis=1, tiled=True)  293 us
    reduce_scatter x1, waiting for transfers between devices, shards(): lax.psum_scatter(partial_cols, 'row', scatter_dimension=0, tiled=True)  138 us
    dot_general x4, matrix products, hankel_pass(): jnp.einsum(form, window_lags, stack, preferred_element_type=jnp.float32)  61.3 us
    unnamed x37, local copies, waits for them, and re-layouts  53.5 us
    psum x1, blocking collectives, shards(): gram = lax.psum(gram_of(mine), ('row', 'col'))  39.8 us
    psum x1, blocking collectives, shards(): forward_b = lax.psum(partial_rows, 'col').astype(jnp.bfloat16)  19.4 us
    all_to_all x1, local copies, waits for them, and re-layouts, shards(): lax.all_to_all(damping, 'row', split_axis=2, concat_axis=1, tiled=True)  18.7 us
    dot_general x1, matrix products, shards(): jnp.einsum('lk,nkr->lrn', cos_table, lax.all_to_all(damping, 'row', split...  15.6 us
  transfers between devices with their start and end apart: 2, of which 2 were waited for; matrix products, arithmetic and copies ran while one was open for 6% of the time, Pallas kernels for 0%

commit v1 on v0

v1 whole, which is shorter than its diff:
```python
import math

import numpy as np
import jax
import jax.numpy as jnp
from jax import lax
from jax.experimental import pallas as pl
from jax.experimental.pallas import tpu as pltpu
from jax.sharding import PartitionSpec as P

NSTEPS = 12
PRIME = 65521
P_SIZE = 32
BF16 = jnp.bfloat16
F32 = jnp.float32
NT = (((1,), (1,)), ((), ()))


def channel_table(n_freq, freqs, steps, n_blocks):
    angle = math.pi * (np.asarray(freqs)[:, None] + 0.5) / n_freq * np.asarray(steps)[None, :]
    decay = 3.0 ** (-np.asarray(steps) / n_blocks)
    return np.stack([decay * np.cos(angle), decay * np.sin(angle)], axis=1)


def high_low(values):
    high = values.astype(np.float32).astype(jnp.bfloat16)
    low = (values - high.astype(np.float64)).astype(np.float32).astype(jnp.bfloat16)
    return high, low


def cosine_turns(turns):
    u = turns * turns
    out = jnp.full_like(u, COS_COEFS[-1])
    for coef in COS_COEFS[-2::-1]:
        out = out * u + coef
    return out


def _fit_cosine():
    nodes = np.cos(np.pi * (np.arange(64) + 0.5) / 64)
    u = 0.125 * (nodes + 1.0)
    series = np.polynomial.chebyshev.Chebyshev.fit(
        u, np.cos(2 * np.pi * np.sqrt(u)), 8, domain=[0.0, 0.25]
    )
    coefs = series.convert(kind=np.polynomial.Polynomial, domain=[-1, 1], window=[-1, 1]).coef
    return [float(x) for x in coefs]


COS_COEFS = _fit_cosine()


def forward_kernel(n_local, inner_ref, shift_ref, whi_ref, wlo_ref, rep_ref, mask_ref, d_ref, t_ref, probes, acc):
    step = pl.program_id(0)
    n_blocks = inner_ref.shape[0]
    inner = inner_ref[...]
    for p in range(P_SIZE):
        x = inner * float(p + 1) + shift_ref[p]
        turns = (x - jnp.round(x * (1.0 / PRIME)) * float(PRIME)) * (1.0 / PRIME)
        probes[p * n_blocks : (p + 1) * n_blocks, :] = cosine_turns(turns).astype(BF16)
    rows, depth = whi_ref.shape
    parts = []
    for group in range(P_SIZE * n_blocks // depth):
        block = probes[group * depth : (group + 1) * depth, :]
        parts.append(
            jnp.dot(whi_ref[...], block, preferred_element_type=F32)
            + jnp.dot(wlo_ref[...], block, preferred_element_type=F32)
        )
    q = jnp.concatenate(parts, axis=0).astype(BF16)
    spread = jnp.dot(q, rep_ref[...], preferred_element_type=F32).astype(BF16)
    spread = spread * mask_ref[...]
    product = jnp.dot(spread, d_ref[...], preferred_element_type=F32)

    @pl.when(step == 0)
    def _():
        acc[...] = product

    @pl.when(step > 0)
    def _():
        acc[...] += product

    @pl.when(step == pl.num_programs(0) - 1)
    def _():
        t_ref[...] = acc[...].astype(BF16)


def middle_kernel(chi_ref, clo_ref, bhi_ref, blo_ref, x_ref, f_ref):
    x = x_ref[...]
    fwd = jnp.dot(chi_ref[...], x, preferred_element_type=F32) + jnp.dot(
        clo_ref[...], x, preferred_element_type=F32
    )
    high = fwd.astype(BF16)
    low = (fwd - high.astype(F32)).astype(BF16)
    out = (
        jnp.dot(bhi_ref[...], high, preferred_element_type=F32)
        + jnp.dot(bhi_ref[...], low, preferred_element_type=F32)
        + jnp.dot(blo_ref[...], high, preferred_element_type=F32)
    ).astype(BF16)
    n_rows, n_cols, channels, lanes = f_ref.shape
    out = out.reshape(n_rows, channels, lanes)
    for col in range(n_cols):
        f_ref[:, col] = out


def backward_kernel(khi_ref, klo_ref, sel_ref, mask_ref, f_ref, d_ref, keep_ref, send_ref):
    product = lax.dot_general(f_ref[...], d_ref[...], NT, preferred_element_type=F32)
    masked = product.astype(BF16) * mask_ref[...]
    u = jnp.dot(masked, sel_ref[...], preferred_element_type=F32).astype(BF16)
    rows, depth = khi_ref.shape
    half = keep_ref.shape[0]
    p_group = rows // (2 * half)
    for group in range(P_SIZE // p_group):
        block = u[group * depth : (group + 1) * depth, :]
        out = jnp.dot(khi_ref[...], block, preferred_element_type=F32) + jnp.dot(
            klo_ref[...], block, preferred_element_type=F32
        )
        out = out.reshape(2 * half, p_group, out.shape[-1])
        at = slice(group * p_group, (group + 1) * p_group)
        keep_ref[:, at, :] = out[:half]
        send_ref[:, at, :] = out[half:].astype(BF16)


def gram_kernel(x_ref, mine_ref, gram_ref):
    mine = jnp.sum(x_ref[...].astype(F32), axis=0)
    mine_ref[...] = mine
    gram = jnp.zeros((P_SIZE, P_SIZE), F32)
    for j in range(mine.shape[0]):
        gram += lax.dot_general(
            mine[j], mine[j], NT, preferred_element_type=F32, precision=lax.Precision.HIGHEST
        )
    gram_ref[...] = jnp.concatenate([gram[8 * i : 8 * i + 8] for i in range(P_SIZE // 8)], axis=1)


def last_kernel(factor, gram_ref, mine_ref, out_ref):
    total = jnp.sum(gram_ref[...], axis=0)
    gram = jnp.concatenate([total[:, P_SIZE * i : P_SIZE * (i + 1)] for i in range(P_SIZE // 8)], axis=0)
    row = lax.broadcasted_iota(jnp.int32, (P_SIZE, P_SIZE), 0)
    col = lax.broadcasted_iota(jnp.int32, (P_SIZE, P_SIZE), 1)
    eye = jnp.where(row == col, 1.0, 0.0).astype(F32)
    scale = jnp.sum(gram * eye, keepdims=True) + 1e-06

    def dot(a, b):
        return jnp.dot(a, b, preferred_element_type=F32, precision=lax.Precision.HIGHEST)

    current = gram / scale
    inverse = eye
    for _ in range(NSTEPS):
        weight = 1.5 * eye - 0.5 * dot(inverse, current)
        current = dot(current, weight)
        inverse = dot(weight, inverse)
    inverse = inverse * (factor / jnp.sqrt(scale))
    for j in range(mine_ref.shape[0]):
        out_ref[j] = lax.dot_general(
            inverse,
            mine_ref[j],
            (((0,), (0,)), ((), ())),
            preferred_element_type=F32,
            precision=lax.Precision.HIGHEST,
        )


def vmem(n):
    return [pl.BlockSpec(memory_space=pltpu.VMEM)] * n


def shards(damping, block_seeds, n_row, n_col):
    cols, local, m = damping.shape
    n_blocks = block_seeds.shape[0]
    n_freq = local * n_row
    channels = 2 * local
    n_dev = n_row * n_col
    amp = math.sqrt(2.0 / n_freq) / math.sqrt(n_blocks * m)
    row_at, col_at = lax.axis_index("row"), lax.axis_index("col")
    params = pltpu.CompilerParams(vmem_limit_bytes=60 << 20)

    block_c = 128 if cols % 128 == 0 else cols
    wide = block_c * local
    flat = damping.reshape(cols * local, m)

    freqs = np.arange(n_freq)
    steps = np.arange(n_blocks)
    w_all = channel_table(n_freq, freqs, steps, n_blocks)
    sign = np.array([1.0, -1.0])[None, :, None]
    back_all = channel_table(n_freq, freqs, steps + 1, n_blocks) * sign * amp
    per_row = w_all.reshape(n_row, channels, n_blocks)
    back_row = back_all.reshape(n_row, channels, n_blocks).transpose(0, 2, 1)

    def mine_of(table):
        return lax.dynamic_index_in_dim(jnp.asarray(table), row_at, 0, keepdims=False)

    def select(shape, dim, fn):
        r, c = np.indices(shape)
        return jnp.asarray((fn(r) == c) if dim == 0 else (r == fn(c)), BF16)

    pw = max(1, 256 // n_blocks)
    w_rows, w_depth = pw * channels, pw * n_blocks
    r, c = np.indices((w_rows, w_depth))
    w_mask = jnp.asarray(r // channels == c // n_blocks, F32)
    spread_l = select((w_rows, channels), 0, lambda a: a % channels)
    spread_r = select((n_blocks, w_depth), 1, lambda a: a % n_blocks)

    def spread_w(table):
        inner = jnp.dot(mine_of(table), spread_r, preferred_element_type=F32).astype(BF16)
        return (jnp.dot(spread_l, inner, preferred_element_type=F32) * w_mask).astype(BF16)

    w_hi, w_lo = (spread_w(t) for t in high_low(per_row))

    per_owner = n_blocks // n_row
    pk = min(P_SIZE, max(8, 256 // channels))
    k_rows, k_depth = n_blocks * pk, pk * channels
    r, c = np.indices((k_rows, k_depth))
    k_mask = jnp.asarray(r % pk == c // channels, F32)
    k_right = select((channels, k_depth), 1, lambda a: a % channels)
    parity = row_at % 2
    place = np.arange(n_blocks)
    half = n_blocks // 2
    flip = place // half
    chip, within = (place % half) // per_owner, (place % half) % per_owner
    order = (chip * 2) * per_owner + within + ((flip + parity) % 2) * per_owner
    pick = (order[:, None] == jnp.arange(n_blocks)[None, :]).astype(BF16)
    k_left = select((k_rows, n_blocks), 0, lambda a: a // pk)

    def spread_k(table):
        ordered = jnp.dot(pick, mine_of(table), preferred_element_type=F32).astype(BF16)
        inner = jnp.dot(ordered, k_right, preferred_element_type=F32).astype(BF16)
        return (jnp.dot(k_left, inner, preferred_element_type=F32) * k_mask).astype(BF16)

    k_hi, k_lo = (spread_k(t) for t in high_low(back_row))

    n_rows = P_SIZE * channels
    r, c = np.indices((n_rows, wide))
    own = jnp.asarray((r // 2) % local == c % local, BF16)
    repeat = select((block_c, wide), 1, lambda a: a // local)
    gather = select((wide, block_c), 0, lambda a: a // local)

    seeds = block_seeds[:, None]
    column = (col_at * cols + jnp.arange(cols, dtype=jnp.int32))[None, :]
    inner = (seeds * (column + 1) % PRIME * (column + 3) % PRIME).astype(F32)
    pcol = jnp.arange(P_SIZE, dtype=jnp.int32)[:, None]
    shift = (block_seeds[None, :] * (pcol + 1) % PRIME * (pcol + 2) % PRIME).astype(F32)
    shift = jnp.broadcast_to(shift[:, :, None], (P_SIZE, n_blocks, block_c))

    whole = lambda *s: pl.BlockSpec(s, lambda i: (0,) * len(s))
    t = pl.pallas_call(
        lambda *refs: forward_kernel(local, *refs),
        grid=(cols // block_c,),
        out_shape=jax.ShapeDtypeStruct((n_rows, m), BF16),
        in_specs=[
            pl.BlockSpec((n_blocks, block_c), lambda i: (0, i)),
            whole(P_SIZE, n_blocks, block_c),
            whole(w_rows, w_depth),
            whole(w_rows, w_depth),
            whole(block_c, wide),
            whole(n_rows, wide),
            pl.BlockSpec((wide, m), lambda i: (i, 0)),
        ],
        out_specs=whole(n_rows, m),
        scratch_shapes=[
            pltpu.VMEM((P_SIZE * n_blocks, block_c), BF16),
            pltpu.VMEM((n_rows, m), F32),
        ],
        compiler_params=params,
        name="forward",
    )(inner, shift, w_hi, w_lo, repeat, own, flat)

    n_p = math.gcd(P_SIZE, n_dev)
    n_r = n_dev // n_p
    p_own, lanes = P_SIZE // n_p, m // n_r
    t = t.reshape(n_p, p_own * channels, n_r, lanes).transpose(0, 2, 1, 3)
    t = t.reshape(n_dev, p_own * channels, lanes)
    t = lax.all_to_all(t, ("row", "col"), 0, 0, tiled=True)
    t = t.reshape(n_dev, p_own, channels, lanes).transpose(0, 2, 1, 3)
    t = t.reshape(n_dev * channels, p_own * lanes)

    merge = w_all.reshape(n_freq, 2, n_blocks) * sign * amp
    merge = merge.reshape(n_row, 1, channels, n_blocks).repeat(n_col, axis=1)
    merge = merge.reshape(n_dev * channels, n_blocks).T
    c_hi, c_lo = high_low(merge)
    b_hi, b_lo = high_low(w_all.reshape(n_row * channels, n_blocks))
    block_l = 512 if (p_own * lanes) % 512 == 0 else p_own * lanes
    f = pl.pallas_call(
        middle_kernel,
        grid=(p_own * lanes // block_l,),
        out_shape=jax.ShapeDtypeStruct((n_row, n_col, channels, p_own * lanes), BF16),
        in_specs=[
            whole(n_blocks, n_dev * channels),
            whole(n_blocks, n_dev * channels),
            whole(n_row * channels, n_blocks),
            whole(n_row * channels, n_blocks),
            pl.BlockSpec((n_dev * channels, block_l), lambda i: (0, i)),
        ],
        out_specs=pl.BlockSpec((n_row, n_col, channels, block_l), lambda i: (0, 0, 0, i)),
        compiler_params=params,
        name="middle",
    )(*(jnp.asarray(x) for x in (c_hi, c_lo, b_hi, b_lo)), t)
    f = f.reshape(n_dev, channels, p_own, lanes).transpose(0, 2, 1, 3).reshape(n_dev, p_own * channels, lanes)
    f = lax.all_to_all(f, ("row", "col"), 0, 0, tiled=True)
    f = f.reshape(n_p, n_r, p_own * channels, lanes).transpose(0, 2, 1, 3).reshape(n_rows, m)

    keep, send = pl.pallas_call(
        backward_kernel,
        grid=(cols // block_c,),
        out_shape=(
            jax.ShapeDtypeStruct((half, P_SIZE, cols), F32),
            jax.ShapeDtypeStruct((half, P_SIZE, cols), BF16),
        ),
        in_specs=[
            whole(k_rows, k_depth),
            whole(k_rows, k_depth),
            whole(wide, block_c),
            whole(n_rows, wide),
            whole(n_rows, m),
            pl.BlockSpec((wide, m), lambda i: (i, 0)),
        ],
        out_specs=(
            pl.BlockSpec((half, P_SIZE, block_c), lambda i: (0, 0, i)),
            pl.BlockSpec((half, P_SIZE, block_c), lambda i: (0, 0, i)),
        ),
        compiler_params=params,
        name="backward",
    )(k_hi, k_lo, gather, own, f, flat)
    got = lax.ppermute(send, "row", [(i, i ^ 1) for i in range(n_row)])
    summed = (keep + got.astype(F32)).astype(BF16)
    groups = [list(range(core, n_row, 2)) for core in range(2)]
    summed = lax.all_to_all(summed, "row", 0, 0, axis_index_groups=groups, tiled=True)
    summed = summed.reshape(n_row // 2, per_owner, P_SIZE, cols)

    mine, gram = pl.pallas_call(
        gram_kernel,
        out_shape=(
            jax.ShapeDtypeStruct((per_owner, P_SIZE, cols), F32),
            jax.ShapeDtypeStruct((8, 4 * P_SIZE), F32),
        ),
        in_specs=vmem(1),
        out_specs=tuple(vmem(2)),
        compiler_params=params,
        name="gram",
    )(summed)
    gram = jnp.broadcast_to(gram[None], (n_dev, *gram.shape))
    gram = lax.all_to_all(gram, ("row", "col"), 0, 0, tiled=True)
    out = pl.pallas_call(
        lambda *refs: last_kernel(math.sqrt(n_blocks * m), *refs),
        out_shape=jax.ShapeDtypeStruct((per_owner, P_SIZE, cols), F32),
        in_specs=vmem(2),
        out_specs=vmem(1)[0],
        compiler_params=params,
        name="last",
    )(gram, mine)
    return out.transpose(0, 2, 1)


def solution(mesh):
    n_row, n_col = mesh.shape["row"], mesh.shape["col"]
    return jax.shard_map(
        lambda damping, block_seeds: shards(damping, block_seeds, n_row, n_col),
        mesh=mesh,
        in_specs=(P("col", "row", None), P()),
        out_specs=P("row", "col", None),
        check_vma=False,
    )
```

time: 705 us -> 191 us (0.27); the launches traced: 696 us -> 191 us
  waiting for transfers between devices: 432 us -> 36.1 us
  local copies, waits for them, and re-layouts: 82.6 us -> 2.9 us
  matrix products: 85.3 us -> 7.49 us
  Pallas kernels: 0 us -> 55.6 us
  blocking collectives: 59.2 us -> 81 us
  between operations: 14.6 us -> 0.1 us
  other arithmetic: 15.2 us -> 3.88 us
    all_to_all x1, waiting for transfers between devices: 293 us -> 33.6 us  [shards(): f = lax.all_to_all(f, ('row', 'col'), 0, 0, tiled=True)]
    reduce_scatter x1 -> x0, waiting for transfers between devices: 138 us -> none  [shards(): lax.psum_scatter(partial_cols, 'row', scatter_dimension=0, tiled=True)]
    all_to_all x0 -> x3, blocking collectives: none -> 81 us  [the longest x1 44.9 us: shards(): t = lax.all_to_all(t, ('row', 'col'), 0, 0, tiled=True)]
    dot_general x42 -> x6, matrix products: 85.3 us -> 7.49 us  [the longest x2 3.68 us: spread_w(): jnp.dot(spread_l, inner, preferred_element_type=F32) * w_mask]
    psum x2 -> x0, blocking collectives: 59.2 us -> none  [the longest x1 39.8 us: shards(): gram = lax.psum(gram_of(mine), ('row', 'col'))]
    pallas_call x0 -> x5, Pallas kernels: none -> 55.6 us  [the longest x1 21.5 us: shards(): pl.pallas_call(backward_kernel, grid=(cols // block_c,), out_shape=(jax.S...]
    unnamed x37 -> x12, local copies, waits for them, and re-layouts: 53.5 us -> 1.19 us
    all_to_all x1 -> x0, local copies, waits for them, and re-layouts: 18.7 us -> none  [shards(): lax.all_to_all(damping, 'row', split_axis=2, concat_axis=1, tiled=True)]
  transfers between devices with their start and end apart: 2 -> 2, of which waited for: 2 -> 2; matrix products, arithmetic and copies ran while one was open for 6% -> 2% of each run, Pallas kernels for 0% -> 0%
where the time goes in v1:
time: 191 us
  blocking collectives  81 us (42%)
  Pallas kernels  55.6 us (29%)
  waiting for transfers between devices  36.1 us (19%)
  matrix products  7.49 us (4%)
  other arithmetic  3.88 us (2%)
  starting transfers between devices  3.69 us (2%)
  local copies, waits for them, and re-layouts  2.9 us (2%)
    all_to_all x1, blocking collectives, shards(): t = lax.all_to_all(t, ('row', 'col'), 0, 0, tiled=True)  44.9 us
    all_to_all x1, waiting for transfers between devices, shards(): f = lax.all_to_all(f, ('row', 'col'), 0, 0, tiled=True)  33.6 us
    all_to_all x1, blocking collectives, shards(): lax.all_to_all(summed, 'row', 0, 0, axis_index_groups=groups, tiled=True)  24 us
    pallas_call x1, Pallas kernels, shards(): pl.pallas_call(backward_kernel, grid=(cols // block_c,), out_shape=(jax.S...  21.5 us
    pallas_call x1, Pallas kernels, shards(): pl.pallas_call(lambda *refs: forward_kernel(local, *refs), grid=(cols //...  21.4 us
    all_to_all x1, blocking collectives, shards(): gram = lax.all_to_all(gram, ('row', 'col'), 0, 0, tiled=True)  12 us
    pallas_call x1, Pallas kernels, shards(): pl.pallas_call(lambda *refs: last_kernel(math.sqrt(n_blocks * m), *refs),...  6.18 us
    pallas_call x1, Pallas kernels, shards(): pl.pallas_call(middle_kernel, grid=(p_own * lanes // block_l,), out_shape...  4.39 us
  transfers between devices with their start and end apart: 2, of which 2 were waited for; matrix products, arithmetic and copies ran while one was open for 2% of the time, Pallas kernels for 0%

profile of v1, /device:TPU:0, one launch (start us, length us, event | category | flops | bytes accessed | tf_op | source)
XLA Modules:
  0.0 190.7 jit_solution(1619641606548057720)
XLA Ops:
  0.0 1.8 fusion.2.refs_2_
  1.9 1.8 fusion.3.refs_3_
  3.7 0.7 fusion.15
  4.4 1.5 fusion.6.refs_0_
  5.9 1.0 broadcast_in_dim.4.refs_1_
  6.9 21.4 %forward.1 = bf16[512,1536]{1,0:T(8,128)(2,1)} custom-call(f32[32,768]{1,0:T(8,128)} %fusion.6.refs_0_, f32[32,32,128]{2,1,0:T(8,128)} %broadcast_in_dim.4.refs_1_, bf16[128,256]{1,0:T(8,128)(2,1)} %fusion.2.refs_2_, bf16[128,256]{1,0:T(8,128)(2,1)} %fusion.3.refs_3_, bf16[128,1024]{1,0:T(8,128)(2,1)} %constant.124.clone.refs_4_, ...), custom_call_target="tpu_custom_call" | custom-call | tf_op jit(solution)/shard_map/forward/pallas_call | solution.py:243
  28.4 44.9 %all_to_all.20 = bf16[32,16,1536]{2,1,0:T(8,128)(2,1)} all-to-all(bf16[32,16,1536]{2,1,0:T(8,128)(2,1)} %bitcast.36), channel_id=1, replica_groups=mesh['row'=16,'col'=2] {'row','col'}, dimensions={0} | all-to-all | bytes 3145728 | tf_op jit(solution)/shard_map/all_to_all | solution.py:270
  73.2 4.4 %middle.1 = bf16[16,2,16,1536]{3,2,1,0:T(8,128)(2,1)} custom-call(bf16[32,512]{1,0:T(8,128)(2,1)} %constant.126.clone.chi_ref, bf16[32,512]{1,0:T(8,128)(2,1)} %constant.127.clone.clo_ref, bf16[256,32]{1,0:T(8,128)(2,1)} %constant.128.clone.bhi_ref, bf16[256,32]{1,0:T(8,128)(2,1)} %constant.129.clone.blo_ref, bf16[512,1536]{1,0:T(8,128)(2,1)} %bitcast.34), custom_call_target="tpu_custom_call" | custom-call | tf_op jit(solution)/shard_map/middle/pallas_call | solution.py:280
  77.6 0.0 copy-start.4
  77.6 0.0 copy-start.5
  77.6 0.0 copy-start.1
  77.6 0.0 copy-start.2
  77.7 0.0 copy-start.3
  77.7 3.7 %all-to-all-start.1 = ((bf16[32,16,1536]{2,1,0:T(8,128)(2,1)}), bf16[32,16,1536]{2,1,0:T(8,128)(2,1)S(1)}, u32[]{:S(2)}, u32[]{:S(2)}) async-start(bf16[32,16,1536]{2,1,0:T(8,128)(2,1)} %bitcast.33), calls=%async_computation.1 | async-start | bytes 3145728 | tf_op jit(solution)/shard_map/all_to_all | solution.py:296
  81.4 0.0 copy-done.4
  81.4 0.0 copy-done.5
  81.4 0.9 convolution_convert_fusion.4
  82.3 0.9 convolution_convert_fusion.5
  83.2 0.0 copy-done.1
  83.2 0.0 copy-done.2
  83.2 0.0 copy-done.3
  83.2 1.0 fusion.khi_ref
  84.2 1.0 fusion.1.klo_ref
  85.2 33.6 %all-to-all-done.1 = bf16[32,16,1536]{2,1,0:T(8,128)(2,1)S(1)} async-done(((bf16[32,16,1536]{2,1,0:T(8,128)(2,1)}), bf16[32,16,1536]{2,1,0:T(8,128)(2,1)S(1)}, u32[]{:S(2)}, u32[]{:S(2)}) %all-to-all-start.1) | async-done | bytes 1572896 | tf_op jit(solution)/shard_map/all_to_all | solution.py:296
  118.8 0.0 copy-start
  118.8 1.2 copy-done
  120.0 21.5 %backward.1 = (f32[16,32,768]{2,1,0:T(8,128)}, bf16[16,32,768]{2,1,0:T(8,128)(2,1)}) custom-call(bf16[512,256]{1,0:T(8,128)(2,1)} %fusion.khi_ref, bf16[512,256]{1,0:T(8,128)(2,1)} %fusion.1.klo_ref, bf16[1024,128]{1,0:T(8,128)(2,1)} %constant.125.clone.sel_ref, bf16[512,1024]{1,0:T(8,128)(2,1)} %constant.123.clone.refs_5_.mask_ref, ...), custom_call_target="tpu_custom_call" | custom-call | tf_op jit(solution)/shard_map/backward/pallas_call | solution.py:299
  141.5 0.0 collective-permute-start
  141.5 2.5 %collective-permute-done = bf16[16,32,768]{2,1,0:T(8,128)(2,1)S(1)} collective-permute-done((bf16[16,32,768]{2,1,0:T(8,128)(2,1)}, bf16[16,32,768]{2,1,0:T(8,128)(2,1)S(1)}, u32[]{:S(2)}, u32[]{:S(2)}) %collective-permute-start) | collective-permute-done | bytes 786464 | tf_op jit(solution)/shard_map/ppermute | solution.py:321
  144.0 1.6 add_convert_fusion
  145.6 24.0 %all_to_all.21 = bf16[16,32,768]{2,1,0:T(8,128)(2,1)} all-to-all(bf16[16,32,768]{2,1,0:T(8,128)(2,1)S(1)} %add_convert_fusion), channel_id=1, replica_groups={{0,4,8,12,16,20,24,28},{2,6,10,14,18,22,26,30},{1,5,9,13,17,21,25,29},{..., dimensions={0} | all-to-all | bytes 1572864 | tf_op jit(solution)/shard_map/all_to_all | solution.py:324
  169.7 2.1 %gram.1 = (f32[2,32,768]{2,1,0:T(8,128)}, f32[8,128]{1,0:T(8,128)}) custom-call(bf16[8,2,32,768]{3,2,1,0:T(8,128)(2,1)} %bitcast.37), custom_call_target="tpu_custom_call" | custom-call | tf_op jit(solution)/shard_map/gram/pallas_call | solution.py:327
  171.8 0.7 broadcast_in_dim.5
  172.5 12.0 %all_to_all.22.refs_0_ = f32[32,8,128]{2,1,0:T(8,128)} all-to-all(f32[32,8,128]{2,1,0:T(8,128)S(1)} %broadcast_in_dim.5), channel_id=1, replica_groups=mesh['row'=16,'col'=2] {'row','col'}, dimensions={0} | all-to-all | bytes 262144 | tf_op jit(solution)/shard_map/all_to_all | solution.py:339
  184.5 6.2 %last.1 = f32[2,32,768]{2,1,0:T(8,128)} custom-call(f32[32,8,128]{2,1,0:T(8,128)} %all_to_all.22.refs_0_, f32[2,32,768]{2,1,0:T(8,128)} %get-tuple-element.12.refs_1_), custom_call_target="tpu_custom_call" | custom-call | tf_op jit(solution)/shard_map/last/pallas_call | solution.py:340
  (3 shorter events, 0.0 us)
Async XLA Ops:
  77.6 3.7 %copy-start.4 = (s32[32]{0:T(128)S(1)}, s32[32]{0:T(128)}, u32[]{:S(2)}) copy-start(s32[32]{0:T(128)} %constant.119.clone) | copy-start | bytes 388
  77.6 3.8 %copy-start.5 = (s32[32]{0:T(128)S(1)}, s32[32]{0:T(128)}, u32[]{:S(2)}) copy-start(s32[32]{0:T(128)} %constant.118.clone) | copy-start | bytes 388
  77.6 5.6 %copy-start.1 = (f32[512,256]{1,0:T(8,128)S(1)}, f32[512,256]{1,0:T(8,128)}, u32[]{:S(2)}) copy-start(f32[512,256]{1,0:T(8,128)} %constant.116.clone) | copy-start | bytes 1572868
  77.6 5.6 %copy-start.2 = (bf16[512,32]{1,0:T(8,128)(2,1)S(1)}, bf16[512,32]{1,0:T(8,128)(2,1)}, u32[]{:S(2)}) copy-start(bf16[512,32]{1,0:T(8,128)(2,1)} %constant.120.clone) | copy-start | bytes 98308
  77.7 5.5 %copy-start.3 = (bf16[16,256]{1,0:T(8,128)(2,1)S(1)}, bf16[16,256]{1,0:T(8,128)(2,1)}, u32[]{:S(2)}) copy-start(bf16[16,256]{1,0:T(8,128)(2,1)} %constant.117.clone) | copy-start | bytes 24580
  77.7 41.1 %all-to-all-start.1 = ((bf16[32,16,1536]{2,1,0:T(8,128)(2,1)}), bf16[32,16,1536]{2,1,0:T(8,128)(2,1)S(1)}, u32[]{:S(2)}, u32[]{:S(2)}) async-start(bf16[32,16,1536]{2,1,0:T(8,128)(2,1)} %bitcast.33), calls=%async_computation.1 | async-start | bytes 3145728 | tf_op jit(solution)/shard_map/all_to_all | solution.py:296
  118.8 1.2 copy-start
  141.5 2.5 %collective-permute-start = (bf16[16,32,768]{2,1,0:T(8,128)(2,1)}, bf16[16,32,768]{2,1,0:T(8,128)(2,1)S(1)}, u32[]{:S(2)}, u32[]{:S(2)}) collective-permute-start(bf16[16,32,768]{2,1,0:T(8,128)(2,1)} %get-tuple-element.10), channel_id=1, source_target_pairs={{0,2},{2,0},{4,6},{6,4},{8,10},{10,8},{12,14},{14,12},{16,18},{18,... | collective-permute-start | bytes 2359304 | tf_op jit(solution)/shard_map/ppermute | solution.py:321

commit v2 on v1

--- a/solution.py
+++ b/solution.py
@@ -49,38 +49,94 @@
 COS_COEFS = _fit_cosine()
 
 
-def forward_kernel(n_local, inner_ref, shift_ref, whi_ref, wlo_ref, rep_ref, mask_ref, d_ref, t_ref, probes, acc):
-    step = pl.program_id(0)
-    n_blocks = inner_ref.shape[0]
-    inner = inner_ref[...]
+def place(rows, cols, test):
+    r = lax.broadcasted_iota(jnp.int32, (rows, cols), 0)
+    c = lax.broadcasted_iota(jnp.int32, (rows, cols), 1)
+    return test(r, c).astype(F32)
+
+
+def less_turns(x):
+    return x - (x.astype(F32) * (1.0 / PRIME)).astype(jnp.int32) * PRIME
+
+
+def forward_kernel(local, seeds_ref, table_ref, d_ref, t_ref, held, wide, acc, probes, shift, spread, q_all, sems):
+    n_chunks, rows, m = held.shape
+    block_c = rows // local
+    channels = 2 * local
+    n_blocks, lanes = seeds_ref.shape
+    group = 8
+    tiles = P_SIZE // 8
+    lane_w = wide.shape[-1]
+    per_pass = wide.shape[1]
+
+    def copy(b):
+        return pltpu.make_async_copy(d_ref.at[pl.ds(b * rows, rows)], held.at[b], sems.at[b])
+
+    for b in range(n_chunks):
+        copy(b).start()
+    start = lax.axis_index("col") * (n_chunks * block_c)
+    table = table_ref[lax.axis_index("row")]
+    left = place(channels * group, channels, lambda r, c: r // group == c)
+    right = place(n_blocks, group * n_blocks, lambda r, c: r == c % n_blocks)
+    same = place(channels * group, group * n_blocks, lambda r, c: r % group == c // n_blocks)
+    for part in range(2):
+        w = jnp.dot(table[part * channels : (part + 1) * channels], right, preferred_element_type=F32)
+        spread[part] = (jnp.dot(left, w, preferred_element_type=F32) * same).astype(BF16)
+    seeds = seeds_ref[...]
     for p in range(P_SIZE):
-        x = inner * float(p + 1) + shift_ref[p]
-        turns = (x - jnp.round(x * (1.0 / PRIME)) * float(PRIME)) * (1.0 / PRIME)
-        probes[p * n_blocks : (p + 1) * n_blocks, :] = cosine_turns(turns).astype(BF16)
-    rows, depth = whi_ref.shape
-    parts = []
-    for group in range(P_SIZE * n_blocks // depth):
-        block = probes[group * depth : (group + 1) * depth, :]
-        parts.append(
-            jnp.dot(whi_ref[...], block, preferred_element_type=F32)
-            + jnp.dot(wlo_ref[...], block, preferred_element_type=F32)
-        )
-    q = jnp.concatenate(parts, axis=0).astype(BF16)
-    spread = jnp.dot(q, rep_ref[...], preferred_element_type=F32).astype(BF16)
-    spread = spread * mask_ref[...]
-    product = jnp.dot(spread, d_ref[...], preferred_element_type=F32)
-
-    @pl.when(step == 0)
-    def _():
-        acc[...] = product
-
-    @pl.when(step > 0)
-    def _():
-        acc[...] += product
-
-    @pl.when(step == pl.num_programs(0) - 1)
-    def _():
-        t_ref[...] = acc[...].astype(BF16)
+        x = (seeds * (p + 1)).astype(F32)
+        shift[p] = (x - jnp.round(x * (1.0 / PRIME)) * float(PRIME)) * float(p + 2)
+    acc[...] = jnp.zeros_like(acc)
+
+    @pl.loop(0, n_chunks)
+    def _(b):
+        lane = lax.broadcasted_iota(jnp.int32, (n_blocks, lanes), 1)
+        for at in range(0, block_c, lanes):
+            column = start + b * block_c + at + lane
+            inner = less_turns(less_turns(seeds * (column + 1)) * (column + 3)).astype(F32)
+            for p in range(P_SIZE):
+                x = inner * float(p + 1) + shift[p]
+                turns = (x - jnp.round(x * (1.0 / PRIME)) * float(PRIME)) * (1.0 / PRIME)
+                probes[p * n_blocks : (p + 1) * n_blocks, at : at + lanes] = cosine_turns(turns).astype(BF16)
+        for g in range(P_SIZE // group):
+            block = probes[g * group * n_blocks : (g + 1) * group * n_blocks, :]
+            q = jnp.dot(spread[0], block, preferred_element_type=F32) + jnp.dot(
+                spread[1], block, preferred_element_type=F32
+            )
+            q_all[:, g * group : (g + 1) * group, :] = q.reshape(channels, group, block_c)
+        copy(b).wait()
+        for i in range(m // (per_pass * lane_w)):
+            for l in range(per_pass):
+                at = (i * per_pass + l) * lane_w
+                wide[i % 2, l] = held[b, :, at : at + lane_w].astype(F32)
+            for k in range(local):
+                s = jnp.concatenate(
+                    [wide[i % 2, l, pl.ds(k, block_c, stride=local), :] for l in range(per_pass)], axis=1
+                ).astype(BF16)
+                q = jnp.concatenate([q_all[k], q_all[local + k]], axis=0).astype(BF16)
+                o = jnp.dot(q, s, preferred_element_type=F32)
+                for l in range(per_pass):
+                    for t in range(2 * tiles):
+                        acc[i * per_pass + l, t, k * 8 : k * 8 + 8, :] += o[
+                            t * 8 : t * 8 + 8, l * lane_w : (l + 1) * lane_w
+                        ]
+
+    for l in range(m // lane_w):
+        for p in range(P_SIZE):
+            t = jnp.concatenate(
+                [acc[l, part * tiles + p // 8, pl.ds(p % 8, local, stride=8), :] for part in range(2)], axis=0
+            )
+            t_ref[p, :, l * lane_w : (l + 1) * lane_w] = t.astype(BF16)
+
+
+def separate_kernel(local, d_ref, o_ref, wide):
+    rows, m = d_ref.shape
+    lane_w = wide.shape[-1]
+    for l in range(m // lane_w):
+        at = slice(l * lane_w, (l + 1) * lane_w)
+        wide[l % 2] = d_ref[:, at].astype(F32)
+        for k in range(local):
+            o_ref[k, at, :] = wide[l % 2, pl.ds(k, rows // local, stride=local), :].T.astype(BF16)
 
 
 def middle_kernel(chi_ref, clo_ref, bhi_ref, blo_ref, x_ref, f_ref):
@@ -101,20 +157,44 @@
         f_ref[:, col] = out
 
 
-def backward_kernel(khi_ref, klo_ref, sel_ref, mask_ref, f_ref, d_ref, keep_ref, send_ref):
-    product = lax.dot_general(f_ref[...], d_ref[...], NT, preferred_element_type=F32)
-    masked = product.astype(BF16) * mask_ref[...]
-    u = jnp.dot(masked, sel_ref[...], preferred_element_type=F32).astype(BF16)
-    rows, depth = khi_ref.shape
+def backward_kernel(khi_ref, klo_ref, f_ref, d_ref, keep_ref, send_ref, wide, f_by):
+    local, m, _ = d_ref.shape
+    channels = 2 * local
+    tiles = P_SIZE // 8
+    lane_w = wide.shape[-1]
+
+    @pl.when(pl.program_id(0) == 0)
+    def _():
+        for l in range(m // lane_w):
+            at = slice(l * lane_w, (l + 1) * lane_w)
+            for p in range(P_SIZE):
+                x = f_ref[p * channels : (p + 1) * channels, at].astype(F32)
+                for part in range(2):
+                    wide[l % 2, part * tiles + p // 8, (p % 8) * local : (p % 8 + 1) * local, :] = x[
+                        part * local : (part + 1) * local
+                    ]
+            for k in range(local):
+                f_by[k, :, at] = jnp.concatenate(
+                    [wide[l % 2, t, pl.ds(k, 8, stride=local), :] for t in range(2 * tiles)], axis=0
+                ).astype(BF16)
+
+    u = [jnp.dot(f_by[k], d_ref[k], preferred_element_type=F32).astype(BF16) for k in range(local)]
     half = keep_ref.shape[0]
-    p_group = rows // (2 * half)
-    for group in range(P_SIZE // p_group):
-        block = u[group * depth : (group + 1) * depth, :]
+    group = khi_ref.shape[0] // (2 * half)
+    for g in range(P_SIZE // group):
+        block = jnp.concatenate(
+            [
+                u[k][part * P_SIZE + g * group : part * P_SIZE + (g + 1) * group]
+                for k in range(local)
+                for part in range(2)
+            ],
+            axis=0,
+        )
         out = jnp.dot(khi_ref[...], block, preferred_element_type=F32) + jnp.dot(
             klo_ref[...], block, preferred_element_type=F32
         )
-        out = out.reshape(2 * half, p_group, out.shape[-1])
-        at = slice(group * p_group, (group + 1) * p_group)
+        out = out.reshape(2 * half, group, out.shape[-1])
+        at = slice(g * group, (g + 1) * group)
         keep_ref[:, at, :] = out[:half]
         send_ref[:, at, :] = out[half:].astype(BF16)
 
@@ -172,8 +252,10 @@
     row_at, col_at = lax.axis_index("row"), lax.axis_index("col")
     params = pltpu.CompilerParams(vmem_limit_bytes=60 << 20)
 
-    block_c = 128 if cols % 128 == 0 else cols
-    wide = block_c * local
+    block_c = 256 if cols % 256 == 0 else cols
+    lanes_c = 128 if block_c % 128 == 0 else block_c
+    lane_w = 128 if m % 128 == 0 else m
+    per_pass = 2 if m % (2 * lane_w) == 0 else 1
     flat = damping.reshape(cols * local, m)
 
     freqs = np.arange(n_freq)
@@ -181,8 +263,14 @@
     w_all = channel_table(n_freq, freqs, steps, n_blocks)
     sign = np.array([1.0, -1.0])[None, :, None]
     back_all = channel_table(n_freq, freqs, steps + 1, n_blocks) * sign * amp
-    per_row = w_all.reshape(n_row, channels, n_blocks)
     back_row = back_all.reshape(n_row, channels, n_blocks).transpose(0, 2, 1)
+
+    def by_channel(table):
+        table = table.reshape(n_row, local, 2, n_blocks)
+        return table.transpose(0, 2, 1, 3).reshape(n_row, channels, n_blocks)
+
+    w_row = by_channel(w_all)
+    w_parts = np.concatenate([x.astype(np.float32) for x in high_low(w_row)], axis=1)
 
     def mine_of(table):
         return lax.dynamic_index_in_dim(jnp.asarray(table), row_at, 0, keepdims=False)
@@ -191,25 +279,12 @@
         r, c = np.indices(shape)
         return jnp.asarray((fn(r) == c) if dim == 0 else (r == fn(c)), BF16)
 
-    pw = max(1, 256 // n_blocks)
-    w_rows, w_depth = pw * channels, pw * n_blocks
-    r, c = np.indices((w_rows, w_depth))
-    w_mask = jnp.asarray(r // channels == c // n_blocks, F32)
-    spread_l = select((w_rows, channels), 0, lambda a: a % channels)
-    spread_r = select((n_blocks, w_depth), 1, lambda a: a % n_blocks)
-
-    def spread_w(table):
-        inner = jnp.dot(mine_of(table), spread_r, preferred_element_type=F32).astype(BF16)
-        return (jnp.dot(spread_l, inner, preferred_element_type=F32) * w_mask).astype(BF16)
-
-    w_hi, w_lo = (spread_w(t) for t in high_low(per_row))
-
     per_owner = n_blocks // n_row
-    pk = min(P_SIZE, max(8, 256 // channels))
+    pk = 16
     k_rows, k_depth = n_blocks * pk, pk * channels
     r, c = np.indices((k_rows, k_depth))
-    k_mask = jnp.asarray(r % pk == c // channels, F32)
-    k_right = select((channels, k_depth), 1, lambda a: a % channels)
+    k_mask = jnp.asarray(r % pk == c % pk, F32)
+    k_right = select((channels, k_depth), 1, lambda a: a // pk)
     parity = row_at % 2
     place = np.arange(n_blocks)
     half = n_blocks // 2
@@ -227,40 +302,43 @@
     k_hi, k_lo = (spread_k(t) for t in high_low(back_row))
 
     n_rows = P_SIZE * channels
-    r, c = np.indices((n_rows, wide))
-    own = jnp.asarray((r // 2) % local == c % local, BF16)
-    repeat = select((block_c, wide), 1, lambda a: a // local)
-    gather = select((wide, block_c), 0, lambda a: a // local)
-
-    seeds = block_seeds[:, None]
-    column = (col_at * cols + jnp.arange(cols, dtype=jnp.int32))[None, :]
-    inner = (seeds * (column + 1) % PRIME * (column + 3) % PRIME).astype(F32)
-    pcol = jnp.arange(P_SIZE, dtype=jnp.int32)[:, None]
-    shift = (block_seeds[None, :] * (pcol + 1) % PRIME * (pcol + 2) % PRIME).astype(F32)
-    shift = jnp.broadcast_to(shift[:, :, None], (P_SIZE, n_blocks, block_c))
+    seeds = jnp.broadcast_to(block_seeds[:, None], (n_blocks, lanes_c))
 
     whole = lambda *s: pl.BlockSpec(s, lambda i: (0,) * len(s))
+    v_one = pl.BlockSpec(memory_space=pltpu.VMEM)
+    work = 2 * cols * local * m
     t = pl.pallas_call(
         lambda *refs: forward_kernel(local, *refs),
-        grid=(cols // block_c,),
-        out_shape=jax.ShapeDtypeStruct((n_rows, m), BF16),
-        in_specs=[
-            pl.BlockSpec((n_blocks, block_c), lambda i: (0, i)),
-            whole(P_SIZE, n_blocks, block_c),
-            whole(w_rows, w_depth),
-            whole(w_rows, w_depth),
-            whole(block_c, wide),
-            whole(n_rows, wide),
-            pl.BlockSpec((wide, m), lambda i: (i, 0)),
+        out_shape=jax.ShapeDtypeStruct((P_SIZE, channels, m), BF16),
+        in_specs=[v_one, v_one, pl.BlockSpec(memory_space=pl.ANY)],
+        out_specs=v_one,
+        scratch_shapes=[
+            pltpu.VMEM((cols // block_c, block_c * local, m), BF16),
+            pltpu.VMEM((2, per_pass, block_c * local, lane_w), F32),
+            pltpu.VMEM((m // lane_w, P_SIZE // 4, 8 * local, lane_w), F32),
+            pltpu.VMEM((P_SIZE * n_blocks, block_c), BF16),
+            pltpu.VMEM((P_SIZE, n_blocks, lanes_c), F32),
+            pltpu.VMEM((2, channels * 8, 8 * n_blocks), BF16),
+            pltpu.VMEM((channels, P_SIZE, block_c), F32),
+            pltpu.SemaphoreType.DMA((cols // block_c,)),
         ],
-        out_specs=whole(n_rows, m),
-        scratch_shapes=[
-            pltpu.VMEM((P_SIZE * n_blocks, block_c), BF16),
-            pltpu.VMEM((n_rows, m), F32),
-        ],
-        compiler_params=params,
+        compiler_params=params,
+        cost_estimate=pl.CostEstimate(flops=64 * work, bytes_accessed=work, transcendentals=0),
         name="forward",
-    )(inner, shift, w_hi, w_lo, repeat, own, flat)
+    )(seeds, jnp.asarray(w_parts), flat)
+    t, flat = lax.optimization_barrier((t, flat))
+    block_s = 128 if cols % 128 == 0 else cols
+    by_freq = pl.pallas_call(
+        lambda *refs: separate_kernel(local, *refs),
+        grid=(cols // block_s,),
+        out_shape=jax.ShapeDtypeStruct((local, m, cols), BF16),
+        in_specs=[pl.BlockSpec((block_s * local, m), lambda i: (i, 0))],
+        out_specs=pl.BlockSpec((local, m, block_s), lambda i: (0, 0, i)),
+        scratch_shapes=[pltpu.VMEM((2, block_s * local, lane_w), F32)],
+        compiler_params=params,
+        cost_estimate=pl.CostEstimate(flops=work, bytes_accessed=2 * work, transcendentals=0),
+        name="separate",
+    )(flat)
 
     n_p = math.gcd(P_SIZE, n_dev)
     n_r = n_dev // n_p
@@ -271,11 +349,11 @@
     t = t.reshape(n_dev, p_own, channels, lanes).transpose(0, 2, 1, 3)
     t = t.reshape(n_dev * channels, p_own * lanes)
 
-    merge = w_all.reshape(n_freq, 2, n_blocks) * sign * amp
+    merge = by_channel(w_all * sign * amp)
     merge = merge.reshape(n_row, 1, channels, n_blocks).repeat(n_col, axis=1)
     merge = merge.reshape(n_dev * channels, n_blocks).T
     c_hi, c_lo = high_low(merge)
-    b_hi, b_lo = high_low(w_all.reshape(n_row * channels, n_blocks))
+    b_hi, b_lo = high_low(w_row.reshape(n_row * channels, n_blocks))
     block_l = 512 if (p_own * lanes) % 512 == 0 else p_own * lanes
     f = pl.pallas_call(
         middle_kernel,
@@ -298,7 +376,7 @@
 
     keep, send = pl.pallas_call(
         backward_kernel,
-        grid=(cols // block_c,),
+        grid=(cols // block_s,),
         out_shape=(
             jax.ShapeDtypeStruct((half, P_SIZE, cols), F32),
             jax.ShapeDtypeStruct((half, P_SIZE, cols), BF16),
@@ -306,18 +384,21 @@
         in_specs=[
             whole(k_rows, k_depth),
             whole(k_rows, k_depth),
-            whole(wide, block_c),
-            whole(n_rows, wide),
             whole(n_rows, m),
-            pl.BlockSpec((wide, m), lambda i: (i, 0)),
+            pl.BlockSpec((local, m, block_s), lambda i: (0, 0, i)),
         ],
         out_specs=(
-            pl.BlockSpec((half, P_SIZE, block_c), lambda i: (0, 0, i)),
-            pl.BlockSpec((half, P_SIZE, block_c), lambda i: (0, 0, i)),
+            pl.BlockSpec((half, P_SIZE, block_s), lambda i: (0, 0, i)),
+            pl.BlockSpec((half, P_SIZE, block_s), lambda i: (0, 0, i)),
         ),
-        compiler_params=params,
+        scratch_shapes=[
+            pltpu.VMEM((2, P_SIZE // 4, 8 * local, lane_w), F32),
+            pltpu.VMEM((local, 2 * P_SIZE, m), BF16),
+        ],
+        compiler_params=params,
+        cost_estimate=pl.CostEstimate(flops=64 * work, bytes_accessed=work, transcendentals=0),
         name="backward",
-    )(k_hi, k_lo, gather, own, f, flat)
+    )(k_hi, k_lo, f, by_freq)
     got = lax.ppermute(send, "row", [(i, i ^ 1) for i in range(n_row)])
     summed = (keep + got.astype(F32)).astype(BF16)
     groups = [list(range(core, n_row, 2)) for core in range(2)]

time: 191 us -> 173 us (0.906)
  waiting for transfers between devices: 36.1 us -> 17.6 us
  Pallas kernels: 55.6 us -> 61 us
  matrix products: 7.49 us -> 3.83 us
  other arithmetic: 3.88 us -> 1.65 us
    all_to_all x1, waiting for transfers between devices: 33.6 us -> 15.1 us  [shards(): f = lax.all_to_all(f, ('row', 'col'), 0, 0, tiled=True)]
    pallas_call x2 -> x3, Pallas kernels: 42.9 us -> 48.3 us  [the longest x1 18.4 us: shards(): pl.pallas_call(lambda *refs: separate_kernel(local, *refs), grid=(cols //...]
    dot_general x2 -> x0, matrix products: 3.68 us -> none  [spread_w(): jnp.dot(spread_l, inner, preferred_element_type=F32) * w_mask]
    convert_element_type x2 -> x0, other arithmetic: 2.23 us -> none  [the longest x1 1.48 us: shards(): inner = (seeds * (column + 1) % PRIME * (column + 3) % PRIME).astype(F32)]
  transfers between devices with their start and end apart: 2 -> 2, of which waited for: 2 -> 2; matrix products, arithmetic and copies ran while one was open for 2% -> 2% of each run, Pallas kernels for 0% -> 11%
where the time goes in v2:
time: 173 us; the launch traced here: 172 us
  blocking collectives  81 us (47%)
  Pallas kernels  61 us (35%)
  waiting for transfers between devices  17.6 us (10%)
  matrix products  3.83 us (2%)
  starting transfers between devices  3.67 us (2%)
  local copies, waits for them, and re-layouts  3.24 us (2%)
    all_to_all x1, blocking collectives, shards(): t = lax.all_to_all(t, ('row', 'col'), 0, 0, tiled=True)  44.9 us
    all_to_all x1, blocking collectives, shards(): lax.all_to_all(summed, 'row', 0, 0, axis_index_groups=groups, tiled=True)  24 us
    pallas_call x1, Pallas kernels, shards(): pl.pallas_call(lambda *refs: separate_kernel(local, *refs), grid=(cols //...  18.4 us
    pallas_call x1, Pallas kernels, shards(): pl.pallas_call(lambda *refs: forward_kernel(local, *refs), out_shape=jax....  17.1 us
    all_to_all x1, waiting for transfers between devices, shards(): f = lax.all_to_all(f, ('row', 'col'), 0, 0, tiled=True)  15.1 us
    pallas_call x1, Pallas kernels, shards(): pl.pallas_call(backward_kernel, grid=(cols // block_s,), out_shape=(jax.S...  12.7 us
    all_to_all x1, blocking collectives, shards(): gram = lax.all_to_all(gram, ('row', 'col'), 0, 0, tiled=True)  12 us
    pallas_call x1, Pallas kernels, shards(): pl.pallas_call(lambda *refs: last_kernel(math.sqrt(n_blocks * m), *refs),...  6.17 us
  transfers between devices with their start and end apart: 2, of which 2 were waited for; matrix products, arithmetic and copies ran while one was open for 2% of the time, Pallas kernels for 11%

profile of v2, /device:TPU:0, one launch (start us, length us, event | category | flops | bytes accessed | tf_op | source)
XLA Modules:
  0.0 172.0 jit_solution(14085427998837405150)
XLA Ops:
  0.0 1.3 broadcast_in_dim.4.refs_0_
  1.3 17.1 %forward.1 = bf16[32,16,1536]{2,1,0:T(8,128)(2,1)} custom-call(s32[32,128]{1,0:T(8,128)} %broadcast_in_dim.4.refs_0_, f32[16,32,32]{2,1,0:T(8,128)} %constant.66.clone.refs_1_, bf16[6144,1536]{1,0:T(8,128)(2,1)} %bitcast.18), custom_call_target="tpu_custom_call" | custom-call | flops 1207959552 | bytes 18874368 | tf_op jit(solution)/shard_map/forward/pallas_call | solution.py:310
  18.5 44.9 %all_to_all.20 = bf16[32,16,1536]{2,1,0:T(8,128)(2,1)} all-to-all(bf16[32,16,1536]{2,1,0:T(8,128)(2,1)} %forward.1), channel_id=1, replica_groups=mesh['row'=16,'col'=2] {'row','col'}, dimensions={0} | all-to-all | bytes 3145728 | tf_op jit(solution)/shard_map/all_to_all | solution.py:348
  63.4 4.4 %middle.1 = bf16[16,2,16,1536]{3,2,1,0:T(8,128)(2,1)} custom-call(bf16[32,512]{1,0:T(8,128)(2,1)} %constant.67.clone.chi_ref, bf16[32,512]{1,0:T(8,128)(2,1)} %constant.68.clone.clo_ref, bf16[256,32]{1,0:T(8,128)(2,1)} %constant.69.clone.bhi_ref, bf16[256,32]{1,0:T(8,128)(2,1)} %constant.70.clone.blo_ref, bf16[512,1536]{1,0:T(8,128)(2,1)} %bitcast.22), custom_call_target="tpu_custom_call" | custom-call | tf_op jit(solution)/shard_map/middle/pallas_call | solution.py:358
  67.7 3.7 %all-to-all-start.1 = ((bf16[32,16,1536]{2,1,0:T(8,128)(2,1)}), bf16[32,16,1536]{2,1,0:T(8,128)(2,1)S(1)}, u32[]{:S(2)}, u32[]{:S(2)}) async-start(bf16[32,16,1536]{2,1,0:T(8,128)(2,1)} %bitcast.21), calls=%async_computation.1 | async-start | bytes 3145728 | tf_op jit(solution)/shard_map/all_to_all | solution.py:374
  71.4 0.0 copy-start.4
  71.4 0.0 copy-start.5
  71.4 0.0 copy-start.1
  71.5 0.0 copy-start.2
  71.5 0.0 copy-start.3
  71.5 18.4 %separate.1.d_ref = bf16[8,1536,768]{2,1,0:T(8,128)(2,1)} custom-call(bf16[6144,1536]{1,0:T(8,128)(2,1)} %bitcast.19), custom_call_target="tpu_custom_call" | custom-call | flops 18874368 | bytes 37748736 | tf_op jit(solution)/shard_map/separate/pallas_call | solution.py:331
  89.9 0.0 copy-done.4
  89.9 0.0 copy-done.5
  89.9 0.9 convolution_convert_fusion.2
  90.8 0.9 convolution_convert_fusion.3
  91.7 0.0 copy-done.1
  91.7 0.0 copy-done.2
  91.7 0.0 copy-done.3
  91.7 1.0 fusion.khi_ref
  92.7 1.0 fusion.1.klo_ref
  93.8 15.1 %all-to-all-done.1 = bf16[32,16,1536]{2,1,0:T(8,128)(2,1)S(1)} async-done(((bf16[32,16,1536]{2,1,0:T(8,128)(2,1)}), bf16[32,16,1536]{2,1,0:T(8,128)(2,1)S(1)}, u32[]{:S(2)}, u32[]{:S(2)}) %all-to-all-start.1) | async-done | bytes 1572896 | tf_op jit(solution)/shard_map/all_to_all | solution.py:374
  108.8 0.0 copy-start
  108.9 1.2 copy-done
  110.0 12.7 %backward.1 = (f32[16,32,768]{2,1,0:T(8,128)}, bf16[16,32,768]{2,1,0:T(8,128)(2,1)}) custom-call(bf16[512,256]{1,0:T(8,128)(2,1)} %fusion.khi_ref, bf16[512,256]{1,0:T(8,128)(2,1)} %fusion.1.klo_ref, bf16[512,1536]{1,0:T(8,128)(2,1)} %bitcast.20, bf16[8,1536,768]{2,1,0:T(8,128)(2,1)} %separate.1.d_ref), custom_call_target="tpu_custom_call" | custom-call | flops 1207959552 | bytes 18874368 | tf_op jit(solution)/shard_map/backward/pallas_call | solution.py:377
  122.8 0.0 collective-permute-start
  122.8 2.5 %collective-permute-done = bf16[16,32,768]{2,1,0:T(8,128)(2,1)S(1)} collective-permute-done((bf16[16,32,768]{2,1,0:T(8,128)(2,1)}, bf16[16,32,768]{2,1,0:T(8,128)(2,1)S(1)}, u32[]{:S(2)}, u32[]{:S(2)}) %collective-permute-start) | collective-permute-done | bytes 786464 | tf_op jit(solution)/shard_map/ppermute | solution.py:402
  125.3 1.6 add_convert_fusion
  126.9 24.0 %all_to_all.21 = bf16[16,32,768]{2,1,0:T(8,128)(2,1)} all-to-all(bf16[16,32,768]{2,1,0:T(8,128)(2,1)S(1)} %add_convert_fusion), channel_id=1, replica_groups={{0,4,8,12,16,20,24,28},{2,6,10,14,18,22,26,30},{1,5,9,13,17,21,25,29},{..., dimensions={0} | all-to-all | bytes 1572864 | tf_op jit(solution)/shard_map/all_to_all | solution.py:405
  151.0 2.1 %gram.1 = (f32[2,32,768]{2,1,0:T(8,128)}, f32[8,128]{1,0:T(8,128)}) custom-call(bf16[8,2,32,768]{3,2,1,0:T(8,128)(2,1)} %bitcast.23), custom_call_target="tpu_custom_call" | custom-call | tf_op jit(solution)/shard_map/gram/pallas_call | solution.py:408
  153.1 0.7 broadcast_in_dim.5
  153.8 12.0 %all_to_all.22.refs_0_ = f32[32,8,128]{2,1,0:T(8,128)} all-to-all(f32[32,8,128]{2,1,0:T(8,128)S(1)} %broadcast_in_dim.5), channel_id=1, replica_groups=mesh['row'=16,'col'=2] {'row','col'}, dimensions={0} | all-to-all | bytes 262144 | tf_op jit(solution)/shard_map/all_to_all | solution.py:420
  165.8 6.2 %last.1 = f32[2,32,768]{2,1,0:T(8,128)} custom-call(f32[32,8,128]{2,1,0:T(8,128)} %all_to_all.22.refs_0_, f32[2,32,768]{2,1,0:T(8,128)} %get-tuple-element.16.refs_1_), custom_call_target="tpu_custom_call" | custom-call | tf_op jit(solution)/shard_map/last/pallas_call | solution.py:421
  (1 shorter events, 0.0 us)
Async XLA Ops:
  67.7 41.1 %all-to-all-start.1 = ((bf16[32,16,1536]{2,1,0:T(8,128)(2,1)}), bf16[32,16,1536]{2,1,0:T(8,128)(2,1)S(1)}, u32[]{:S(2)}, u32[]{:S(2)}) async-start(bf16[32,16,1536]{2,1,0:T(8,128)(2,1)} %bitcast.21), calls=%async_computation.1 | async-start | bytes 3145728 | tf_op jit(solution)/shard_map/all_to_all | solution.py:374
  71.4 18.5 %copy-start.4 = (s32[32]{0:T(128)S(1)}, s32[32]{0:T(128)}, u32[]{:S(2)}) copy-start(s32[32]{0:T(128)} %constant.62.clone) | copy-start | bytes 388
  71.4 18.5 %copy-start.5 = (s32[32]{0:T(128)S(1)}, s32[32]{0:T(128)}, u32[]{:S(2)}) copy-start(s32[32]{0:T(128)} %constant.61.clone) | copy-start | bytes 388
  71.4 20.2 %copy-start.1 = (f32[512,256]{1,0:T(8,128)S(1)}, f32[512,256]{1,0:T(8,128)}, u32[]{:S(2)}) copy-start(f32[512,256]{1,0:T(8,128)} %constant.59.clone) | copy-start | bytes 1572868
  71.5 20.2 %copy-start.2 = (bf16[512,32]{1,0:T(8,128)(2,1)S(1)}, bf16[512,32]{1,0:T(8,128)(2,1)}, u32[]{:S(2)}) copy-start(bf16[512,32]{1,0:T(8,128)(2,1)} %constant.63.clone) | copy-start | bytes 98308
  71.5 20.2 %copy-start.3 = (bf16[16,256]{1,0:T(8,128)(2,1)S(1)}, bf16[16,256]{1,0:T(8,128)(2,1)}, u32[]{:S(2)}) copy-start(bf16[16,256]{1,0:T(8,128)(2,1)} %constant.60.clone) | copy-start | bytes 24580
  108.8 1.2 copy-start
  122.8 2.5 %collective-permute-start = (bf16[16,32,768]{2,1,0:T(8,128)(2,1)}, bf16[16,32,768]{2,1,0:T(8,128)(2,1)S(1)}, u32[]{:S(2)}, u32[]{:S(2)}) collective-permute-start(bf16[16,32,768]{2,1,0:T(8,128)(2,1)} %get-tuple-element.14), channel_id=1, source_target_pairs={{0,2},{2,0},{4,6},{6,4},{8,10},{10,8},{12,14},{14,12},{16,18},{18,... | collective-permute-start | bytes 2359304 | tf_op jit(solution)/shard_map/ppermute | solution.py:402

commit v3 on v2

--- a/solution.py
+++ b/solution.py
@@ -139,22 +139,40 @@
             o_ref[k, at, :] = wide[l % 2, pl.ds(k, rows // local, stride=local), :].T.astype(BF16)
 
 
-def middle_kernel(chi_ref, clo_ref, bhi_ref, blo_ref, x_ref, f_ref):
-    x = x_ref[...]
-    fwd = jnp.dot(chi_ref[...], x, preferred_element_type=F32) + jnp.dot(
-        clo_ref[...], x, preferred_element_type=F32
-    )
-    high = fwd.astype(BF16)
-    low = (fwd - high.astype(F32)).astype(BF16)
-    out = (
-        jnp.dot(bhi_ref[...], high, preferred_element_type=F32)
-        + jnp.dot(bhi_ref[...], low, preferred_element_type=F32)
-        + jnp.dot(blo_ref[...], high, preferred_element_type=F32)
-    ).astype(BF16)
-    n_rows, n_cols, channels, lanes = f_ref.shape
-    out = out.reshape(n_rows, channels, lanes)
-    for col in range(n_cols):
-        f_ref[:, col] = out
+def half_of(n_row):
+    return lax.axis_index("row") // (n_row // 2)
+
+
+def gather_kernel(n_row, c_ref, x_ref, keep_ref, send_ref):
+    n_src, p_own, channels, lanes = x_ref.shape
+    table = c_ref[half_of(n_row)]
+    n = table.shape[0] // 2
+    for p in range(p_own):
+        x = x_ref[:, p].reshape(n_src * channels, lanes)
+        both = jnp.dot(table, x, preferred_element_type=F32)
+        out = both[:n] + both[n:]
+        keep_ref[p] = out
+        send_ref[p] = out.astype(BF16)
+
+
+def scatter_kernel(n_row, b_ref, keep_ref, got_ref, f_ref):
+    n_rows, n_cols, p_own, channels, lanes = f_ref.shape
+    table = b_ref[half_of(n_row)]
+    for p in range(p_own):
+        forward = keep_ref[p] + got_ref[p].astype(F32)
+        high = forward.astype(BF16)
+        low = (forward - high.astype(F32)).astype(BF16)
+        out = jnp.dot(table, jnp.concatenate([high, low, high], axis=0), preferred_element_type=F32)
+        out = out.astype(BF16).reshape(n_rows, channels, lanes)
+        for col in range(n_cols):
+            f_ref[:, col, p] = out
+
+
+def join_kernel(x_ref, keep_ref, send_ref):
+    x = x_ref[...].astype(F32)
+    total = jnp.sum(x, axis=0)
+    keep_ref[...] = total[0]
+    send_ref[...] = total[1].astype(BF16)
 
 
 def backward_kernel(khi_ref, klo_ref, f_ref, d_ref, keep_ref, send_ref, wide, f_by):
@@ -199,15 +217,17 @@
         send_ref[:, at, :] = out[half:].astype(BF16)
 
 
-def gram_kernel(x_ref, mine_ref, gram_ref):
-    mine = jnp.sum(x_ref[...].astype(F32), axis=0)
+def gram_kernel(keep_ref, got_ref, mine_ref, gram_ref):
+    mine = keep_ref[...] + got_ref[...].astype(F32)
     mine_ref[...] = mine
     gram = jnp.zeros((P_SIZE, P_SIZE), F32)
     for j in range(mine.shape[0]):
         gram += lax.dot_general(
             mine[j], mine[j], NT, preferred_element_type=F32, precision=lax.Precision.HIGHEST
         )
-    gram_ref[...] = jnp.concatenate([gram[8 * i : 8 * i + 8] for i in range(P_SIZE // 8)], axis=1)
+    gram = jnp.concatenate([gram[8 * i : 8 * i + 8] for i in range(P_SIZE // 8)], axis=1)
+    for i in range(gram_ref.shape[0]):
+        gram_ref[i] = gram
 
 
 def last_kernel(factor, gram_ref, mine_ref, out_ref):
@@ -250,7 +270,7 @@
     n_dev = n_row * n_col
     amp = math.sqrt(2.0 / n_freq) / math.sqrt(n_blocks * m)
     row_at, col_at = lax.axis_index("row"), lax.axis_index("col")
-    params = pltpu.CompilerParams(vmem_limit_bytes=60 << 20)
+    large, params = (pltpu.CompilerParams(vmem_limit_bytes=x << 20) for x in (40, 20))
 
     block_c = 256 if cols % 256 == 0 else cols
     lanes_c = 128 if block_c % 128 == 0 else block_c
@@ -288,9 +308,11 @@
     parity = row_at % 2
     place = np.arange(n_blocks)
     half = n_blocks // 2
-    flip = place // half
-    chip, within = (place % half) // per_owner, (place % half) % per_owner
-    order = (chip * 2) * per_owner + within + ((flip + parity) % 2) * per_owner
+    quarter = n_row // 4
+    flip, rest = place // half, place % half
+    spot, far, within = rest // (2 * per_owner), rest // per_owner % 2, rest % per_owner
+    chip = spot + quarter * ((far + half_of(n_row)) % 2)
+    order = (2 * chip + (flip + parity) % 2) * per_owner + within
     pick = (order[:, None] == jnp.arange(n_blocks)[None, :]).astype(BF16)
     k_left = select((k_rows, n_blocks), 0, lambda a: a // pk)
 
@@ -322,7 +344,7 @@
             pltpu.VMEM((channels, P_SIZE, block_c), F32),
             pltpu.SemaphoreType.DMA((cols // block_c,)),
         ],
-        compiler_params=params,
+        compiler_params=large,
         cost_estimate=pl.CostEstimate(flops=64 * work, bytes_accessed=work, transcendentals=0),
         name="forward",
     )(seeds, jnp.asarray(w_parts), flat)
@@ -340,38 +362,44 @@
         name="separate",
     )(flat)
 
-    n_p = math.gcd(P_SIZE, n_dev)
-    n_r = n_dev // n_p
+    n_grp = n_dev // 2
+    n_p = math.gcd(P_SIZE, n_grp)
+    n_r = n_grp // n_p
     p_own, lanes = P_SIZE // n_p, m // n_r
+    halves = [list(range(n_grp)), list(range(n_grp, n_dev))]
+    across = [(i, (i + n_row // 2) % n_row) for i in range(n_row)]
     t = t.reshape(n_p, p_own * channels, n_r, lanes).transpose(0, 2, 1, 3)
-    t = t.reshape(n_dev, p_own * channels, lanes)
-    t = lax.all_to_all(t, ("row", "col"), 0, 0, tiled=True)
-    t = t.reshape(n_dev, p_own, channels, lanes).transpose(0, 2, 1, 3)
-    t = t.reshape(n_dev * channels, p_own * lanes)
-
-    merge = by_channel(w_all * sign * amp)
-    merge = merge.reshape(n_row, 1, channels, n_blocks).repeat(n_col, axis=1)
-    merge = merge.reshape(n_dev * channels, n_blocks).T
-    c_hi, c_lo = high_low(merge)
-    b_hi, b_lo = high_low(w_row.reshape(n_row * channels, n_blocks))
-    block_l = 512 if (p_own * lanes) % 512 == 0 else p_own * lanes
+    t = t.reshape(n_grp, p_own * channels, lanes)
+    t = lax.all_to_all(t, ("row", "col"), 0, 0, axis_index_groups=halves, tiled=True)
+    t = t.reshape(n_grp, p_own, channels, lanes)
+
+    merge = by_channel(w_all * sign * amp).reshape(2, n_row // 2, 1, channels, n_blocks).repeat(n_col, axis=2)
+    merge = merge.reshape(2, n_grp * channels, n_blocks).transpose(0, 2, 1)
+    merge = np.concatenate(high_low(merge), axis=1)
+    b_hi, b_lo = high_low(w_row.reshape(2, n_row // 2 * channels, n_blocks))
+    fan = np.concatenate([b_hi, b_hi, b_lo], axis=2)
+    keep, send = pl.pallas_call(
+        lambda *refs: gather_kernel(n_row, *refs),
+        out_shape=(
+            jax.ShapeDtypeStruct((p_own, n_blocks, lanes), F32),
+            jax.ShapeDtypeStruct((p_own, n_blocks, lanes), BF16),
+        ),
+        in_specs=vmem(2),
+        out_specs=tuple(vmem(2)),
+        compiler_params=params,
+        name="gather",
+    )(jnp.asarray(merge), t)
+    got = lax.ppermute(send, "row", across)
     f = pl.pallas_call(
-        middle_kernel,
-        grid=(p_own * lanes // block_l,),
-        out_shape=jax.ShapeDtypeStruct((n_row, n_col, channels, p_own * lanes), BF16),
-        in_specs=[
-            whole(n_blocks, n_dev * channels),
-            whole(n_blocks, n_dev * channels),
-            whole(n_row * channels, n_blocks),
-            whole(n_row * channels, n_blocks),
-            pl.BlockSpec((n_dev * channels, block_l), lambda i: (0, i)),
-        ],
-        out_specs=pl.BlockSpec((n_row, n_col, channels, block_l), lambda i: (0, 0, 0, i)),
-        compiler_params=params,
-        name="middle",
-    )(*(jnp.asarray(x) for x in (c_hi, c_lo, b_hi, b_lo)), t)
-    f = f.reshape(n_dev, channels, p_own, lanes).transpose(0, 2, 1, 3).reshape(n_dev, p_own * channels, lanes)
-    f = lax.all_to_all(f, ("row", "col"), 0, 0, tiled=True)
+        lambda *refs: scatter_kernel(n_row, *refs),
+        out_shape=jax.ShapeDtypeStruct((n_row // 2, n_col, p_own, channels, lanes), BF16),
+        in_specs=vmem(3),
+        out_specs=v_one,
+        compiler_params=params,
+        name="scatter",
+    )(jnp.asarray(fan), keep, got)
+    f = f.reshape(n_grp, p_own * channels, lanes)
+    f = lax.all_to_all(f, ("row", "col"), 0, 0, axis_index_groups=halves, tiled=True)
     f = f.reshape(n_p, n_r, p_own * channels, lanes).transpose(0, 2, 1, 3).reshape(n_rows, m)
 
     keep, send = pl.pallas_call(
@@ -401,22 +429,33 @@
     )(k_hi, k_lo, f, by_freq)
     got = lax.ppermute(send, "row", [(i, i ^ 1) for i in range(n_row)])
     summed = (keep + got.astype(F32)).astype(BF16)
-    groups = [list(range(core, n_row, 2)) for core in range(2)]
+    groups = [[core + 2 * (i + quarter * h) for i in range(quarter)] for h in range(2) for core in range(2)]
     summed = lax.all_to_all(summed, "row", 0, 0, axis_index_groups=groups, tiled=True)
-    summed = summed.reshape(n_row // 2, per_owner, P_SIZE, cols)
+    summed = summed.reshape(quarter, 2, per_owner, P_SIZE, cols)
+    keep, send = pl.pallas_call(
+        join_kernel,
+        out_shape=(
+            jax.ShapeDtypeStruct((per_owner, P_SIZE, cols), F32),
+            jax.ShapeDtypeStruct((per_owner, P_SIZE, cols), BF16),
+        ),
+        in_specs=vmem(1),
+        out_specs=tuple(vmem(2)),
+        compiler_params=params,
+        name="join",
+    )(summed)
+    got = lax.ppermute(send, "row", across)
 
     mine, gram = pl.pallas_call(
         gram_kernel,
         out_shape=(
             jax.ShapeDtypeStruct((per_owner, P_SIZE, cols), F32),
-            jax.ShapeDtypeStruct((8, 4 * P_SIZE), F32),
+            jax.ShapeDtypeStruct((n_dev, 8, 4 * P_SIZE), F32),
         ),
-        in_specs=vmem(1),
+        in_specs=vmem(2),
         out_specs=tuple(vmem(2)),
         compiler_params=params,
         name="gram",
-    )(summed)
-    gram = jnp.broadcast_to(gram[None], (n_dev, *gram.shape))
+    )(keep, got)
     gram = lax.all_to_all(gram, ("row", "col"), 0, 0, tiled=True)
     out = pl.pallas_call(
         lambda *refs: last_kernel(math.sqrt(n_blocks * m), *refs),

time: 173 us -> 145 us (0.84)
  blocking collectives: 81 us -> 54.1 us
  Pallas kernels: 61 us -> 47.8 us
  local copies, waits for them, and re-layouts: 3.24 us -> 14.6 us
  starting transfers between devices: 3.67 us -> 8.6 us
    all_to_all x1, blocking collectives: 44.9 us -> 26.6 us  [shards(): lax.all_to_all(t, ('row', 'col'), 0, 0, axis_index_groups=halves, tiled=T...]
    all_to_all x1, waiting for transfers between devices: 15.1 us -> 0.01 us  [shards(): lax.all_to_all(f, ('row', 'col'), 0, 0, axis_index_groups=halves, tiled=T...]
    ppermute x0 -> x2, waiting for transfers between devices: none -> 14.5 us  [shards(): got = lax.ppermute(send, 'row', across)]
    unnamed x12 -> x24, local copies, waits for them, and re-layouts: 1.21 us -> 13.8 us
    all_to_all x1, blocking collectives: 24 us -> 15.5 us  [shards(): lax.all_to_all(summed, 'row', 0, 0, axis_index_groups=groups, tiled=True)]
    ppermute x0 -> x2, starting transfers between devices: none -> 4.55 us  [shards(): got = lax.ppermute(send, 'row', across)]
    pallas_call x1, Pallas kernels: 18.4 us -> 14.5 us  [shards(): pl.pallas_call(lambda *refs: separate_kernel(local, *refs), grid=(cols //...]
    pallas_call x1 -> x3, Pallas kernels: 4.37 us -> 1.99 us  [the longest x1 1.5 us: shards(): pl.pallas_call(lambda *refs: scatter_kernel(n_row, *refs), out_shape=jax....]
  transfers between devices with their start and end apart: 2 -> 4, of which waited for: 2 -> 3; matrix products, arithmetic and copies ran while one was open for 2% -> 2% of each run, Pallas kernels for 11% -> 10%
where the time goes in v3:
time: 145 us
  blocking collectives  54.1 us (37%)
  Pallas kernels  47.8 us (33%)
  waiting for transfers between devices  16.5 us (11%)
  local copies, waits for them, and re-layouts  14.6 us (10%)
  starting transfers between devices  8.6 us (6%)
  matrix products  2.42 us (2%)
    all_to_all x1, blocking collectives, shards(): lax.all_to_all(t, ('row', 'col'), 0, 0, axis_index_groups=halves, tiled=T...  26.6 us
    all_to_all x1, blocking collectives, shards(): lax.all_to_all(summed, 'row', 0, 0, axis_index_groups=groups, tiled=True)  15.5 us
    pallas_call x1, Pallas kernels, shards(): pl.pallas_call(lambda *refs: forward_kernel(local, *refs), out_shape=jax....  15 us
    pallas_call x1, Pallas kernels, shards(): pl.pallas_call(lambda *refs: separate_kernel(local, *refs), grid=(cols //...  14.5 us
    ppermute x2, waiting for transfers between devices, shards(): got = lax.ppermute(send, 'row', across)  14.5 us
    unnamed x24, local copies, waits for them, and re-layouts  13.8 us
    all_to_all x1, blocking collectives, shards(): gram = lax.all_to_all(gram, ('row', 'col'), 0, 0, tiled=True)  12.1 us
    pallas_call x1, Pallas kernels, shards(): pl.pallas_call(backward_kernel, grid=(cols // block_s,), out_shape=(jax.S...  10.7 us
  transfers between devices with their start and end apart: 4, of which 3 were waited for; matrix products, arithmetic and copies ran while one was open for 2% of the time, Pallas kernels for 10%

profile of v3, /device:TPU:0, one launch (start us, length us, event | category | flops | bytes accessed | tf_op | source)
XLA Modules:
  0.0 144.5 jit_solution(11570736113723891629)
XLA Ops:
  0.0 0.7 broadcast_in_dim.2.refs_0_
  0.7 0.0 copy-start.2
  0.7 0.9 copy-done.2
  1.7 15.0 %forward.1 = bf16[32,16,1536]{2,1,0:T(8,128)(2,1)S(1)} custom-call(s32[32,128]{1,0:T(8,128)S(1)} %broadcast_in_dim.2.refs_0_, f32[16,32,32]{2,1,0:T(8,128)S(1)} %copy-done.2, bf16[6144,1536]{1,0:T(8,128)(2,1)} %bitcast.23), custom_call_target="tpu_custom_call" | custom-call | flops 1207959552 | bytes 18874368 | tf_op jit(solution)/shard_map/forward/pallas_call | solution.py:332
  16.7 0.0 copy-start.4
  16.7 26.6 %all_to_all.20 = bf16[16,32,1536]{2,1,0:T(8,128)(2,1)S(1)} all-to-all(bf16[16,32,1536]{2,1,0:T(8,128)(2,1)S(1)} %bitcast.21), channel_id=1, replica_groups={{0,1,2,3,4,5,6,7,8,9,10,11,12,13,14,15},{16,17,18,19,20,21,22,23,24,25,..., dimensions={0} | all-to-all | bytes 3145728 | tf_op jit(solution)/shard_map/all_to_all | solution.py:373
  43.3 0.0 copy-start.3
  43.3 0.0 copy-done.4
  43.3 0.4 gather.1
  43.7 2.6 %collective-permute-start = (bf16[2,32,1536]{2,1,0:T(8,128)(2,1)S(1)}, bf16[2,32,1536]{2,1,0:T(8,128)(2,1)S(1)}, u32[]{:S(2)}, u32[]{:S(2)}) collective-permute-start(bf16[2,32,1536]{2,1,0:T(8,128)(2,1)S(1)} %get-tuple-element.17), channel_id=1, source_target_pairs={{0,16},{2,18},{4,20},{6,22},{8,24},{10,26},{12,28},{14,30},{16,0},... | collective-permute-start | bytes 589832 | tf_op jit(solution)/shard_map/ppermute | solution.py:392
  46.4 9.8 %collective-permute-done.refs_2_ = bf16[2,32,1536]{2,1,0:T(8,128)(2,1)S(1)} collective-permute-done((bf16[2,32,1536]{2,1,0:T(8,128)(2,1)S(1)}, bf16[2,32,1536]{2,1,0:T(8,128)(2,1)S(1)}, u32[]{:S(2)}, u32[]{:S(2)}) %collective-permute-start) | collective-permute-done | bytes 196640 | tf_op jit(solution)/shard_map/ppermute | solution.py:392
  56.1 0.0 copy-done.3
  56.1 1.5 %scatter.1 = bf16[8,2,2,16,1536]{4,3,2,1,0:T(8,128)(2,1)} custom-call(bf16[2,128,96]{2,1,0:T(8,128)(2,1)S(1)} %copy-done.3, f32[2,32,1536]{2,1,0:T(8,128)S(1)} %get-tuple-element.16.refs_1_, bf16[2,32,1536]{2,1,0:T(8,128)(2,1)S(1)} %collective-permute-done.refs_2_), custom_call_target="tpu_custom_call" | custom-call | tf_op jit(solution)/shard_map/scatter/pallas_call | solution.py:393
  57.7 3.7 %all-to-all-start.1 = ((bf16[16,32,1536]{2,1,0:T(8,128)(2,1)}), bf16[16,32,1536]{2,1,0:T(8,128)(2,1)S(1)}, u32[]{:S(2)}, u32[]{:S(2)}) async-start(bf16[16,32,1536]{2,1,0:T(8,128)(2,1)} %bitcast.5), calls=%async_computation.1 | async-start | bytes 3145728 | tf_op jit(solution)/shard_map/all_to_all | solution.py:402
  61.4 0.0 copy-start.8
  61.4 0.0 copy-start.9
  61.4 0.0 copy-start.10
  61.4 0.0 copy-start.11
  61.4 0.0 copy-start.5
  61.5 0.0 copy-start.6
  61.5 0.0 copy-start.7
  61.5 14.5 %separate.1.d_ref = bf16[8,1536,768]{2,1,0:T(8,128)(2,1)S(1)} custom-call(bf16[6144,1536]{1,0:T(8,128)(2,1)} %bitcast.24), custom_call_target="tpu_custom_call" | custom-call | flops 18874368 | bytes 37748736 | tf_op jit(solution)/shard_map/separate/pallas_call | solution.py:353
  76.0 0.0 copy-start
  76.0 6.5 %copy-done = bf16[8,1536,768]{2,1,0:T(8,128)(2,1)} copy-done((bf16[8,1536,768]{2,1,0:T(8,128)(2,1)}, bf16[8,1536,768]{2,1,0:T(8,128)(2,1)S(1)}, u32[]{:S(2)}) %copy-start) | copy-done | bytes 18874392
  82.5 0.0 copy-done.8
  82.5 0.0 copy-done.9
  82.5 0.0 copy-done.10
  82.5 0.0 copy-done.11
  82.5 0.9 convolution_convert_fusion.2
  83.4 0.9 convolution_convert_fusion.3
  84.3 0.0 copy-done.5
  84.3 0.0 copy-done.6
  84.3 0.0 copy-done.7
  84.3 0.3 fusion.khi_ref
  84.6 0.3 fusion.1.klo_ref
  85.0 0.0 all-to-all-done.1
  85.0 0.0 copy-start.1
  85.0 6.4 %copy-done.1 = bf16[8,1536,768]{2,1,0:T(8,128)(2,1)S(1)} copy-done((bf16[8,1536,768]{2,1,0:T(8,128)(2,1)S(1)}, bf16[8,1536,768]{2,1,0:T(8,128)(2,1)}, u32[]{:S(2)}) %copy-start.1) | copy-done | bytes 18874392
  91.3 10.7 %backward.1 = (f32[16,32,768]{2,1,0:T(8,128)S(1)}, bf16[16,32,768]{2,1,0:T(8,128)(2,1)S(1)}) custom-call(bf16[512,256]{1,0:T(8,128)(2,1)S(1)} %fusion.khi_ref, bf16[512,256]{1,0:T(8,128)(2,1)S(1)} %fusion.1.klo_ref, bf16[512,1536]{1,0:T(8,128)(2,1)S(1)} %bitcast.19, bf16[8,1536,768]{2,1,0:T(8,128)(2,1)S(1)} %copy-done.1), custom_call_target="tpu_custom_call" | custom-call | flops 1207959552 | bytes 18874368 | tf_op jit(solution)/shard_map/backward/pallas_call | solution.py:405
  102.1 0.3 collective-permute-start.1
  102.4 2.0 %collective-permute-done.1 = bf16[16,32,768]{2,1,0:T(8,128)(2,1)S(1)} collective-permute-done((bf16[16,32,768]{2,1,0:T(8,128)(2,1)S(1)}, bf16[16,32,768]{2,1,0:T(8,128)(2,1)S(1)}, u32[]{:S(2)}, u32[]{:S(2)}) %collective-permute-start.1) | collective-permute-done | bytes 786464 | tf_op jit(solution)/shard_map/ppermute | solution.py:430
  104.4 0.2 add_convert_fusion
  104.7 15.5 %all_to_all.21 = bf16[16,32,768]{2,1,0:T(8,128)(2,1)S(1)} all-to-all(bf16[16,32,768]{2,1,0:T(8,128)(2,1)S(1)} %add_convert_fusion), channel_id=1, replica_groups={{0,4,8,12},{2,6,10,14},{16,20,24,28},{18,22,26,30},{1,5,9,13},{3,7,11,1..., dimensions={0} | all-to-all | bytes 1572864 | tf_op jit(solution)/shard_map/all_to_all | solution.py:433
  120.1 0.1 join.1
  120.2 1.9 %collective-permute-start.2 = (bf16[2,32,768]{2,1,0:T(8,128)(2,1)S(1)}, bf16[2,32,768]{2,1,0:T(8,128)(2,1)S(1)}, u32[]{:S(2)}, u32[]{:S(2)}) collective-permute-start(bf16[2,32,768]{2,1,0:T(8,128)(2,1)S(1)} %get-tuple-element.22), channel_id=1, source_target_pairs={{0,16},{2,18},{4,20},{6,22},{8,24},{10,26},{12,28},{14,30},{16,0},... | collective-permute-start | bytes 294920 | tf_op jit(solution)/shard_map/ppermute | solution.py:446
  122.1 4.7 %collective-permute-done.2.got_ref = bf16[2,32,768]{2,1,0:T(8,128)(2,1)S(1)} collective-permute-done((bf16[2,32,768]{2,1,0:T(8,128)(2,1)S(1)}, bf16[2,32,768]{2,1,0:T(8,128)(2,1)S(1)}, u32[]{:S(2)}, u32[]{:S(2)}) %collective-permute-start.2) | collective-permute-done | bytes 98336 | tf_op jit(solution)/shard_map/ppermute | solution.py:446
  126.9 0.4 gram.1
  127.2 12.1 %all_to_all.22.refs_0_ = f32[32,8,128]{2,1,0:T(8,128)S(1)} all-to-all(f32[32,8,128]{2,1,0:T(8,128)S(1)} %get-tuple-element.23), channel_id=1, replica_groups=mesh['row'=16,'col'=2] {'row','col'}, dimensions={0} | all-to-all | bytes 262144 | tf_op jit(solution)/shard_map/all_to_all | solution.py:459
  139.3 5.2 %last.1 = f32[2,32,768]{2,1,0:T(8,128)} custom-call(f32[32,8,128]{2,1,0:T(8,128)S(1)} %all_to_all.22.refs_0_, f32[2,32,768]{2,1,0:T(8,128)S(1)} %get-tuple-element.24.refs_1_), custom_call_target="tpu_custom_call" | custom-call | tf_op jit(solution)/shard_map/last/pallas_call | solution.py:460
  (1 shorter events, 0.0 us)
Async XLA Ops:
  0.7 1.0 copy-start.2
  16.7 26.6 %copy-start.4 = (bf16[2,64,256]{2,1,0:T(8,128)(2,1)S(1)}, bf16[2,64,256]{2,1,0:T(8,128)(2,1)}, u32[]{:S(2)}) copy-start(bf16[2,64,256]{2,1,0:T(8,128)(2,1)} %constant.90.clone.refs_0_) | copy-start | bytes 196612
  43.3 12.8 %copy-start.3 = (bf16[2,128,96]{2,1,0:T(8,128)(2,1)S(1)}, bf16[2,128,96]{2,1,0:T(8,128)(2,1)}, u32[]{:S(2)}) copy-start(bf16[2,128,96]{2,1,0:T(8,128)(2,1)} %constant.91.clone.refs_0_) | copy-start | bytes 147460
  43.7 12.4 %collective-permute-start = (bf16[2,32,1536]{2,1,0:T(8,128)(2,1)S(1)}, bf16[2,32,1536]{2,1,0:T(8,128)(2,1)S(1)}, u32[]{:S(2)}, u32[]{:S(2)}) collective-permute-start(bf16[2,32,1536]{2,1,0:T(8,128)(2,1)S(1)} %get-tuple-element.17), channel_id=1, source_target_pairs={{0,16},{2,18},{4,20},{6,22},{8,24},{10,26},{12,28},{14,30},{16,0},... | collective-permute-start | bytes 589832 | tf_op jit(solution)/shard_map/ppermute | solution.py:392
  57.7 27.3 %all-to-all-start.1 = ((bf16[16,32,1536]{2,1,0:T(8,128)(2,1)}), bf16[16,32,1536]{2,1,0:T(8,128)(2,1)S(1)}, u32[]{:S(2)}, u32[]{:S(2)}) async-start(bf16[16,32,1536]{2,1,0:T(8,128)(2,1)} %bitcast.5), calls=%async_computation.1 | async-start | bytes 3145728 | tf_op jit(solution)/shard_map/all_to_all | solution.py:402
  61.4 21.1 %copy-start.8 = (s32[32]{0:T(128)S(1)}, s32[32]{0:T(128)}, u32[]{:S(2)}) copy-start(s32[32]{0:T(128)} %constant.85.clone) | copy-start | bytes 388
  61.4 21.1 %copy-start.9 = (s32[32]{0:T(128)S(1)}, s32[32]{0:T(128)}, u32[]{:S(2)}) copy-start(s32[32]{0:T(128)} %constant.84.clone) | copy-start | bytes 388
  61.4 21.1 %copy-start.10 = (s32[32]{0:T(128)S(1)}, s32[32]{0:T(128)}, u32[]{:S(2)}) copy-start(s32[32]{0:T(128)} %constant.83.clone) | copy-start | bytes 388
  61.4 21.1 %copy-start.11 = (s32[32]{0:T(128)S(1)}, s32[32]{0:T(128)}, u32[]{:S(2)}) copy-start(s32[32]{0:T(128)} %constant.82.clone) | copy-start | bytes 388
  61.4 22.9 %copy-start.5 = (f32[512,256]{1,0:T(8,128)S(1)}, f32[512,256]{1,0:T(8,128)}, u32[]{:S(2)}) copy-start(f32[512,256]{1,0:T(8,128)} %constant.80.clone) | copy-start | bytes 1572868
  61.5 22.9 %copy-start.6 = (bf16[512,32]{1,0:T(8,128)(2,1)S(1)}, bf16[512,32]{1,0:T(8,128)(2,1)}, u32[]{:S(2)}) copy-start(bf16[512,32]{1,0:T(8,128)(2,1)} %constant.86.clone) | copy-start | bytes 98308
  61.5 22.8 %copy-start.7 = (bf16[16,256]{1,0:T(8,128)(2,1)S(1)}, bf16[16,256]{1,0:T(8,128)(2,1)}, u32[]{:S(2)}) copy-start(bf16[16,256]{1,0:T(8,128)(2,1)} %constant.81.clone) | copy-start | bytes 24580
  76.0 6.5 %copy-start = (bf16[8,1536,768]{2,1,0:T(8,128)(2,1)}, bf16[8,1536,768]{2,1,0:T(8,128)(2,1)S(1)}, u32[]{:S(2)}) copy-start(bf16[8,1536,768]{2,1,0:T(8,128)(2,1)S(1)} %separate.1.d_ref) | copy-start | bytes 56623108
  85.0 6.4 %copy-start.1 = (bf16[8,1536,768]{2,1,0:T(8,128)(2,1)S(1)}, bf16[8,1536,768]{2,1,0:T(8,128)(2,1)}, u32[]{:S(2)}) copy-start(bf16[8,1536,768]{2,1,0:T(8,128)(2,1)} %copy-done) | copy-start | bytes 56623108
  102.1 2.4 %collective-permute-start.1 = (bf16[16,32,768]{2,1,0:T(8,128)(2,1)S(1)}, bf16[16,32,768]{2,1,0:T(8,128)(2,1)S(1)}, u32[]{:S(2)}, u32[]{:S(2)}) collective-permute-start(bf16[16,32,768]{2,1,0:T(8,128)(2,1)S(1)} %get-tuple-element.20), channel_id=1, source_target_pairs={{0,2},{2,0},{4,6},{6,4},{8,10},{10,8},{12,14},{14,12},{16,18},{18,... | collective-permute-start | bytes 2359304 | tf_op jit(solution)/shard_map/ppermute | solution.py:430
  120.2 6.6 %collective-permute-start.2 = (bf16[2,32,768]{2,1,0:T(8,128)(2,1)S(1)}, bf16[2,32,768]{2,1,0:T(8,128)(2,1)S(1)}, u32[]{:S(2)}, u32[]{:S(2)}) collective-permute-start(bf16[2,32,768]{2,1,0:T(8,128)(2,1)S(1)} %get-tuple-element.22), channel_id=1, source_target_pairs={{0,16},{2,18},{4,20},{6,22},{8,24},{10,26},{12,28},{14,30},{16,0},... | collective-permute-start | bytes 294920 | tf_op jit(solution)/shard_map/ppermute | solution.py:446

commit v4 on v3

--- a/solution.py
+++ b/solution.py
@@ -59,11 +59,11 @@
     return x - (x.astype(F32) * (1.0 / PRIME)).astype(jnp.int32) * PRIME
 
 
-def forward_kernel(local, seeds_ref, table_ref, d_ref, t_ref, held, wide, acc, probes, shift, spread, q_all, sems):
+def forward_kernel(local, seeds_ref, table_ref, d_ref, t_ref, held, wide, acc, probes, shift, spread, q_all, own, sems, sem):
     n_chunks, rows, m = held.shape
     block_c = rows // local
     channels = 2 * local
-    n_blocks, lanes = seeds_ref.shape
+    n_blocks, lanes = shift.shape[1:]
     group = 8
     tiles = P_SIZE // 8
     lane_w = wide.shape[-1]
@@ -72,21 +72,27 @@
     def copy(b):
         return pltpu.make_async_copy(d_ref.at[pl.ds(b * rows, rows)], held.at[b], sems.at[b])
 
+    fetch = pltpu.make_async_copy(table_ref.at[lax.axis_index("row")], own, sem)
+    fetch.start()
     for b in range(n_chunks):
         copy(b).start()
     start = lax.axis_index("col") * (n_chunks * block_c)
-    table = table_ref[lax.axis_index("row")]
+    line = lax.broadcasted_iota(jnp.int32, (n_blocks, lanes), 0)
+    seeds = jnp.zeros((n_blocks, lanes), jnp.int32)
+    for j in range(n_blocks):
+        seeds = jnp.where(line == j, seeds_ref[j], seeds)
+    for p in range(P_SIZE):
+        x = (seeds * (p + 1)).astype(F32)
+        shift[p] = (x - jnp.round(x * (1.0 / PRIME)) * float(PRIME)) * float(p + 2)
+    acc[...] = jnp.zeros_like(acc)
+    fetch.wait()
+    table = own[...]
     left = place(channels * group, channels, lambda r, c: r // group == c)
     right = place(n_blocks, group * n_blocks, lambda r, c: r == c % n_blocks)
     same = place(channels * group, group * n_blocks, lambda r, c: r % group == c // n_blocks)
     for part in range(2):
         w = jnp.dot(table[part * channels : (part + 1) * channels], right, preferred_element_type=F32)
         spread[part] = (jnp.dot(left, w, preferred_element_type=F32) * same).astype(BF16)
-    seeds = seeds_ref[...]
-    for p in range(P_SIZE):
-        x = (seeds * (p + 1)).astype(F32)
-        shift[p] = (x - jnp.round(x * (1.0 / PRIME)) * float(PRIME)) * float(p + 2)
-    acc[...] = jnp.zeros_like(acc)
 
     @pl.loop(0, n_chunks)
     def _(b):
@@ -129,9 +135,32 @@
             t_ref[p, :, l * lane_w : (l + 1) * lane_w] = t.astype(BF16)
 
 
-def separate_kernel(local, d_ref, o_ref, wide):
+def separate_kernel(local, n_row, group, d_ref, table_ref, o_ref, khi_ref, klo_ref, wide):
     rows, m = d_ref.shape
     lane_w = wide.shape[-1]
+
+    @pl.when(pl.program_id(0) == 0)
+    def _():
+        row_at = lax.axis_index("row")
+        table = table_ref[row_at]
+        channels = 2 * local
+        n_blocks = table.shape[0] // 2
+        half, own, quarter = n_blocks // 2, n_blocks // n_row, n_row // 4
+
+        def is_owner(r, c):
+            rest = r % half
+            chip = rest // (2 * own) + quarter * ((rest // own + half_of(n_row)) % 2)
+            return (2 * chip + (r // half + row_at) % 2) * own + rest % own == c
+
+        pick = place(n_blocks, n_blocks, is_owner)
+        right = place(channels, channels * group, lambda r, c: r == c // 32 * 2 + c // 8 % 2)
+        left = place(n_blocks * group, n_blocks, lambda r, c: r // group == c)
+        same = place(n_blocks * group, channels * group, lambda r, c: r % group == c // 16 % 2 * 8 + c % 8)
+        for part, out_ref in enumerate((khi_ref, klo_ref)):
+            k = jnp.dot(pick, table[part * n_blocks : (part + 1) * n_blocks], preferred_element_type=F32)
+            k = jnp.dot(left, jnp.dot(k, right, preferred_element_type=F32), preferred_element_type=F32)
+            out_ref[...] = (k * same).astype(BF16)
+
     for l in range(m // lane_w):
         at = slice(l * lane_w, (l + 1) * lane_w)
         wide[l % 2] = d_ref[:, at].astype(F32)
@@ -175,46 +204,39 @@
     send_ref[...] = total[1].astype(BF16)
 
 
-def backward_kernel(khi_ref, klo_ref, f_ref, d_ref, keep_ref, send_ref, wide, f_by):
-    local, m, _ = d_ref.shape
+def backward_kernel(local, khi_ref, klo_ref, f_ref, d_ref, keep_ref, send_ref, held, f_by, sems):
+    n_chunks, _, m, block_c = held.shape
+    rows = f_ref.shape[0] // 4
     channels = 2 * local
-    tiles = P_SIZE // 8
-    lane_w = wide.shape[-1]
-
-    @pl.when(pl.program_id(0) == 0)
-    def _():
-        for l in range(m // lane_w):
-            at = slice(l * lane_w, (l + 1) * lane_w)
-            for p in range(P_SIZE):
-                x = f_ref[p * channels : (p + 1) * channels, at].astype(F32)
-                for part in range(2):
-                    wide[l % 2, part * tiles + p // 8, (p % 8) * local : (p % 8 + 1) * local, :] = x[
-                        part * local : (part + 1) * local
-                    ]
-            for k in range(local):
-                f_by[k, :, at] = jnp.concatenate(
-                    [wide[l % 2, t, pl.ds(k, 8, stride=local), :] for t in range(2 * tiles)], axis=0
-                ).astype(BF16)
-
-    u = [jnp.dot(f_by[k], d_ref[k], preferred_element_type=F32).astype(BF16) for k in range(local)]
+
+    def copy(b):
+        at = pl.ds(pl.multiple_of(b * block_c, block_c), block_c) if n_chunks > 1 else slice(None)
+        return pltpu.make_async_copy(d_ref.at[:, :, at], held.at[b], sems.at[b])
+
+    for b in range(n_chunks):
+        copy(b).start()
+
+    swap = place(rows, rows, lambda r, c: (r % 8 * 2 + r // 8 % 2) * local + r // 16 == c).astype(BF16)
+    for g in range(4):
+        out = jnp.dot(swap, f_ref[g * rows : (g + 1) * rows, :], preferred_element_type=F32).astype(BF16)
+        for k in range(local):
+            f_by[k, g * 16 : g * 16 + 16, :] = out[k * 16 : k * 16 + 16]
+
     half = keep_ref.shape[0]
-    group = khi_ref.shape[0] // (2 * half)
-    for g in range(P_SIZE // group):
-        block = jnp.concatenate(
-            [
-                u[k][part * P_SIZE + g * group : part * P_SIZE + (g + 1) * group]
-                for k in range(local)
-                for part in range(2)
-            ],
-            axis=0,
-        )
-        out = jnp.dot(khi_ref[...], block, preferred_element_type=F32) + jnp.dot(
-            klo_ref[...], block, preferred_element_type=F32
-        )
-        out = out.reshape(2 * half, group, out.shape[-1])
-        at = slice(g * group, (g + 1) * group)
-        keep_ref[:, at, :] = out[:half]
-        send_ref[:, at, :] = out[half:].astype(BF16)
+
+    @pl.loop(0, n_chunks)
+    def _(b):
+        copy(b).wait()
+        at = pl.ds(pl.multiple_of(b * block_c, block_c), block_c) if n_chunks > 1 else slice(None)
+        u = [jnp.dot(f_by[k], held[b, k], preferred_element_type=F32).astype(BF16) for k in range(local)]
+        for g in range(2):
+            block = jnp.concatenate([x[g * 32 : g * 32 + 32] for x in u], axis=0)
+            out = jnp.dot(khi_ref[...], block, preferred_element_type=F32) + jnp.dot(
+                klo_ref[...], block, preferred_element_type=F32
+            )
+            out = out.reshape(2 * half, 16, block_c)
+            keep_ref[:, g * 16 : g * 16 + 16, at] = out[:half]
+            send_ref[:, g * 16 : g * 16 + 16, at] = out[half:].astype(BF16)
 
 
 def gram_kernel(keep_ref, got_ref, mine_ref, gram_ref):
@@ -269,8 +291,7 @@
     channels = 2 * local
     n_dev = n_row * n_col
     amp = math.sqrt(2.0 / n_freq) / math.sqrt(n_blocks * m)
-    row_at, col_at = lax.axis_index("row"), lax.axis_index("col")
-    large, params = (pltpu.CompilerParams(vmem_limit_bytes=x << 20) for x in (40, 20))
+    most, large, params = (pltpu.CompilerParams(vmem_limit_bytes=x << 20) for x in (54, 40, 20))
 
     block_c = 256 if cols % 256 == 0 else cols
     lanes_c = 128 if block_c % 128 == 0 else block_c
@@ -292,47 +313,17 @@
     w_row = by_channel(w_all)
     w_parts = np.concatenate([x.astype(np.float32) for x in high_low(w_row)], axis=1)
 
-    def mine_of(table):
-        return lax.dynamic_index_in_dim(jnp.asarray(table), row_at, 0, keepdims=False)
-
-    def select(shape, dim, fn):
-        r, c = np.indices(shape)
-        return jnp.asarray((fn(r) == c) if dim == 0 else (r == fn(c)), BF16)
-
-    per_owner = n_blocks // n_row
-    pk = 16
-    k_rows, k_depth = n_blocks * pk, pk * channels
-    r, c = np.indices((k_rows, k_depth))
-    k_mask = jnp.asarray(r % pk == c % pk, F32)
-    k_right = select((channels, k_depth), 1, lambda a: a // pk)
-    parity = row_at % 2
-    place = np.arange(n_blocks)
-    half = n_blocks // 2
-    quarter = n_row // 4
-    flip, rest = place // half, place % half
-    spot, far, within = rest // (2 * per_owner), rest // per_owner % 2, rest % per_owner
-    chip = spot + quarter * ((far + half_of(n_row)) % 2)
-    order = (2 * chip + (flip + parity) % 2) * per_owner + within
-    pick = (order[:, None] == jnp.arange(n_blocks)[None, :]).astype(BF16)
-    k_left = select((k_rows, n_blocks), 0, lambda a: a // pk)
-
-    def spread_k(table):
-        ordered = jnp.dot(pick, mine_of(table), preferred_element_type=F32).astype(BF16)
-        inner = jnp.dot(ordered, k_right, preferred_element_type=F32).astype(BF16)
-        return (jnp.dot(k_left, inner, preferred_element_type=F32) * k_mask).astype(BF16)
-
-    k_hi, k_lo = (spread_k(t) for t in high_low(back_row))
-
+    k_parts = np.concatenate([x.astype(np.float32) for x in high_low(back_row)], axis=1)
+    per_owner, half, quarter = n_blocks // n_row, n_blocks // 2, n_row // 4
+    group = 16
     n_rows = P_SIZE * channels
-    seeds = jnp.broadcast_to(block_seeds[:, None], (n_blocks, lanes_c))
-
     whole = lambda *s: pl.BlockSpec(s, lambda i: (0,) * len(s))
     v_one = pl.BlockSpec(memory_space=pltpu.VMEM)
     work = 2 * cols * local * m
     t = pl.pallas_call(
         lambda *refs: forward_kernel(local, *refs),
         out_shape=jax.ShapeDtypeStruct((P_SIZE, channels, m), BF16),
-        in_specs=[v_one, v_one, pl.BlockSpec(memory_space=pl.ANY)],
+        in_specs=[pl.BlockSpec(memory_space=pltpu.SMEM)] + [pl.BlockSpec(memory_space=pltpu.HBM)] * 2,
         out_specs=v_one,
         scratch_shapes=[
             pltpu.VMEM((cols // block_c, block_c * local, m), BF16),
@@ -342,25 +333,32 @@
             pltpu.VMEM((P_SIZE, n_blocks, lanes_c), F32),
             pltpu.VMEM((2, channels * 8, 8 * n_blocks), BF16),
             pltpu.VMEM((channels, P_SIZE, block_c), F32),
+            pltpu.VMEM((2 * channels, n_blocks), F32),
             pltpu.SemaphoreType.DMA((cols // block_c,)),
+            pltpu.SemaphoreType.DMA,
         ],
         compiler_params=large,
         cost_estimate=pl.CostEstimate(flops=64 * work, bytes_accessed=work, transcendentals=0),
         name="forward",
-    )(seeds, jnp.asarray(w_parts), flat)
+    )(block_seeds, jnp.asarray(w_parts), flat)
     t, flat = lax.optimization_barrier((t, flat))
     block_s = 128 if cols % 128 == 0 else cols
-    by_freq = pl.pallas_call(
-        lambda *refs: separate_kernel(local, *refs),
+    k_shape = (n_blocks * group, channels * group)
+    by_freq, k_hi, k_lo = pl.pallas_call(
+        lambda *refs: separate_kernel(local, n_row, group, *refs),
         grid=(cols // block_s,),
-        out_shape=jax.ShapeDtypeStruct((local, m, cols), BF16),
-        in_specs=[pl.BlockSpec((block_s * local, m), lambda i: (i, 0))],
-        out_specs=pl.BlockSpec((local, m, block_s), lambda i: (0, 0, i)),
+        out_shape=(
+            jax.ShapeDtypeStruct((local, m, cols), BF16),
+            jax.ShapeDtypeStruct(k_shape, BF16),
+            jax.ShapeDtypeStruct(k_shape, BF16),
+        ),
+        in_specs=[pl.BlockSpec((block_s * local, m), lambda i: (i, 0)), whole(*k_parts.shape)],
+        out_specs=(pl.BlockSpec((local, m, block_s), lambda i: (0, 0, i)), whole(*k_shape), whole(*k_shape)),
         scratch_shapes=[pltpu.VMEM((2, block_s * local, lane_w), F32)],
-        compiler_params=params,
+        compiler_params=most,
         cost_estimate=pl.CostEstimate(flops=work, bytes_accessed=2 * work, transcendentals=0),
         name="separate",
-    )(flat)
+    )(flat, jnp.asarray(k_parts))
 
     n_grp = n_dev // 2
     n_p = math.gcd(P_SIZE, n_grp)
@@ -403,27 +401,19 @@
     f = f.reshape(n_p, n_r, p_own * channels, lanes).transpose(0, 2, 1, 3).reshape(n_rows, m)
 
     keep, send = pl.pallas_call(
-        backward_kernel,
-        grid=(cols // block_s,),
+        lambda *refs: backward_kernel(local, *refs),
         out_shape=(
             jax.ShapeDtypeStruct((half, P_SIZE, cols), F32),
             jax.ShapeDtypeStruct((half, P_SIZE, cols), BF16),
         ),
-        in_specs=[
-            whole(k_rows, k_depth),
-            whole(k_rows, k_depth),
-            whole(n_rows, m),
-            pl.BlockSpec((local, m, block_s), lambda i: (0, 0, i)),
+        in_specs=vmem(3) + [pl.BlockSpec(memory_space=pl.ANY)],
+        out_specs=tuple(vmem(2)),
+        scratch_shapes=[
+            pltpu.VMEM((cols // block_s, local, m, block_s), BF16),
+            pltpu.VMEM((local, 2 * P_SIZE, m), BF16),
+            pltpu.SemaphoreType.DMA((cols // block_s,)),
         ],
-        out_specs=(
-            pl.BlockSpec((half, P_SIZE, block_s), lambda i: (0, 0, i)),
-            pl.BlockSpec((half, P_SIZE, block_s), lambda i: (0, 0, i)),
-        ),
-        scratch_shapes=[
-            pltpu.VMEM((2, P_SIZE // 4, 8 * local, lane_w), F32),
-            pltpu.VMEM((local, 2 * P_SIZE, m), BF16),
-        ],
-        compiler_params=params,
+        compiler_params=large,
         cost_estimate=pl.CostEstimate(flops=64 * work, bytes_accessed=work, transcendentals=0),
         name="backward",
     )(k_hi, k_lo, f, by_freq)

time: 145 us -> 136 us (0.938)
  local copies, waits for them, and re-layouts: 14.6 us -> 3.51 us
  Pallas kernels: 47.8 us -> 50.9 us
  matrix products: 2.42 us -> 0 us
  waiting for transfers between devices: 16.5 us -> 18.6 us
    unnamed x24 -> x12, local copies, waits for them, and re-layouts: 13.8 us -> 3.51 us
    pallas_call x2, Pallas kernels: 25.2 us -> 27.8 us  [the longest x1 18.9 us: shards(): pl.pallas_call(lambda *refs: separate_kernel(local, n_row, group, *refs),...]
    dot_general x4 -> x0, matrix products: 2.42 us -> none  [the longest x2 1.78 us: spread_k(): jnp.dot(pick, mine_of(table), preferred_element_type=F32).astype(BF16)]
    all_to_all x1, waiting for transfers between devices: 0.01 us -> 1.89 us  [shards(): lax.all_to_all(f, ('row', 'col'), 0, 0, axis_index_groups=halves, tiled=T...]
  transfers between devices with their start and end apart: 4 -> 4, of which waited for: 3 -> 4; matrix products, arithmetic and copies ran while one was open for 2% -> 0% of each run, Pallas kernels for 10% -> 14%
where the time goes in v4:
time: 136 us
  blocking collectives  54 us (40%)
  Pallas kernels  50.9 us (37%)
  waiting for transfers between devices  18.6 us (14%)
  starting transfers between devices  8.38 us (6%)
  local copies, waits for them, and re-layouts  3.51 us (3%)
    all_to_all x1, blocking collectives, shards(): lax.all_to_all(t, ('row', 'col'), 0, 0, axis_index_groups=halves, tiled=T...  26.6 us
    pallas_call x1, Pallas kernels, shards(): pl.pallas_call(lambda *refs: separate_kernel(local, n_row, group, *refs),...  18.9 us
    all_to_all x1, blocking collectives, shards(): lax.all_to_all(summed, 'row', 0, 0, axis_index_groups=groups, tiled=True)  15.9 us
    pallas_call x1, Pallas kernels, shards(): pl.pallas_call(lambda *refs: forward_kernel(local, *refs), out_shape=jax....  15.6 us
    ppermute x2, waiting for transfers between devices, shards(): got = lax.ppermute(send, 'row', across)  14.5 us
    all_to_all x1, blocking collectives, shards(): gram = lax.all_to_all(gram, ('row', 'col'), 0, 0, tiled=True)  11.5 us
    pallas_call x1, Pallas kernels, shards(): pl.pallas_call(lambda *refs: backward_kernel(local, *refs), out_shape=(ja...  8.84 us
    pallas_call x1, Pallas kernels, shards(): pl.pallas_call(lambda *refs: last_kernel(math.sqrt(n_blocks * m), *refs),...  5.19 us
  transfers between devices with their start and end apart: 4, of which 4 were waited for; matrix products, arithmetic and copies ran while one was open for 0% of the time, Pallas kernels for 14%

profile of v4, /device:TPU:0, one launch (start us, length us, event | category | flops | bytes accessed | tf_op | source)
XLA Modules:
  0.0 135.8 jit_solution(9376190800286326381)
XLA Ops:
  0.0 0.0 copy-start.2
  0.0 0.9 copy-done.2
  1.0 0.0 copy-start.5
  1.0 0.7 copy-done.5
  1.6 15.6 %forward.1 = bf16[32,16,1536]{2,1,0:T(8,128)(2,1)S(1)} custom-call(s32[32]{0:T(128)S(1)} %copy-done.5, f32[16,32,32]{2,1,0:T(8,128)S(1)} %copy-done.2, bf16[6144,1536]{1,0:T(8,128)(2,1)} %bitcast.11), custom_call_target="tpu_custom_call" | custom-call | flops 1207959552 | bytes 18874368 | tf_op jit(solution)/shard_map/forward/pallas_call | solution.py:323
  17.2 0.0 copy-start.4
  17.2 26.6 %all_to_all.20 = bf16[16,32,1536]{2,1,0:T(8,128)(2,1)S(1)} all-to-all(bf16[16,32,1536]{2,1,0:T(8,128)(2,1)S(1)} %bitcast.9), channel_id=1, replica_groups={{0,1,2,3,4,5,6,7,8,9,10,11,12,13,14,15},{16,17,18,19,20,21,22,23,24,25,..., dimensions={0} | all-to-all | bytes 3145728 | tf_op jit(solution)/shard_map/all_to_all | solution.py:371
  43.8 0.0 copy-start.3
  43.8 0.0 copy-done.4
  43.8 0.4 gather.1
  44.2 2.6 %collective-permute-start = (bf16[2,32,1536]{2,1,0:T(8,128)(2,1)S(1)}, bf16[2,32,1536]{2,1,0:T(8,128)(2,1)S(1)}, u32[]{:S(2)}, u32[]{:S(2)}) collective-permute-start(bf16[2,32,1536]{2,1,0:T(8,128)(2,1)S(1)} %get-tuple-element.23), channel_id=1, source_target_pairs={{0,16},{2,18},{4,20},{6,22},{8,24},{10,26},{12,28},{14,30},{16,0},... | collective-permute-start | bytes 589832 | tf_op jit(solution)/shard_map/ppermute | solution.py:390
  46.8 9.8 %collective-permute-done.refs_2_ = bf16[2,32,1536]{2,1,0:T(8,128)(2,1)S(1)} collective-permute-done((bf16[2,32,1536]{2,1,0:T(8,128)(2,1)S(1)}, bf16[2,32,1536]{2,1,0:T(8,128)(2,1)S(1)}, u32[]{:S(2)}, u32[]{:S(2)}) %collective-permute-start) | collective-permute-done | bytes 196640 | tf_op jit(solution)/shard_map/ppermute | solution.py:390
  56.6 0.0 copy-done.3
  56.6 1.5 %scatter.1 = bf16[8,2,2,16,1536]{4,3,2,1,0:T(8,128)(2,1)} custom-call(bf16[2,128,96]{2,1,0:T(8,128)(2,1)S(1)} %copy-done.3, f32[2,32,1536]{2,1,0:T(8,128)S(1)} %get-tuple-element.22.refs_1_, bf16[2,32,1536]{2,1,0:T(8,128)(2,1)S(1)} %collective-permute-done.refs_2_), custom_call_target="tpu_custom_call" | custom-call | tf_op jit(solution)/shard_map/scatter/pallas_call | solution.py:391
  58.2 3.7 %all-to-all-start.1 = ((bf16[16,32,1536]{2,1,0:T(8,128)(2,1)}), bf16[16,32,1536]{2,1,0:T(8,128)(2,1)S(1)}, u32[]{:S(2)}, u32[]{:S(2)}) async-start(bf16[16,32,1536]{2,1,0:T(8,128)(2,1)} %bitcast.3), calls=%async_computation.1 | async-start | bytes 3145728 | tf_op jit(solution)/shard_map/all_to_all | solution.py:400
  61.9 18.9 %separate.1 = (bf16[8,1536,768]{2,1,0:T(8,128)(2,1)}, bf16[512,256]{1,0:T(8,128)(2,1)}, bf16[512,256]{1,0:T(8,128)(2,1)}) custom-call(bf16[6144,1536]{1,0:T(8,128)(2,1)} %bitcast.12, f32[16,64,16]{2,1,0:T(8,128)} %constant.9.clone.refs_1_), custom_call_target="tpu_custom_call" | custom-call | flops 18874368 | bytes 37748736 | tf_op jit(solution)/shard_map/separate/pallas_call | solution.py:347
  80.8 1.9 %all-to-all-done.1 = bf16[16,32,1536]{2,1,0:T(8,128)(2,1)S(1)} async-done(((bf16[16,32,1536]{2,1,0:T(8,128)(2,1)}), bf16[16,32,1536]{2,1,0:T(8,128)(2,1)S(1)}, u32[]{:S(2)}, u32[]{:S(2)}) %all-to-all-start.1) | async-done | bytes 1572896 | tf_op jit(solution)/shard_map/all_to_all | solution.py:400
  82.7 0.0 copy-start
  82.7 0.9 copy-done
  83.7 0.0 copy-start.1
  83.7 0.9 copy-done.1
  84.6 8.8 %backward.1 = (f32[16,32,768]{2,1,0:T(8,128)S(1)}, bf16[16,32,768]{2,1,0:T(8,128)(2,1)S(1)}) custom-call(bf16[512,256]{1,0:T(8,128)(2,1)S(1)} %copy-done, bf16[512,256]{1,0:T(8,128)(2,1)S(1)} %copy-done.1, bf16[512,1536]{1,0:T(8,128)(2,1)S(1)} %bitcast.7, bf16[8,1536,768]{2,1,0:T(8,128)(2,1)} %get-tuple-element.24.refs_3_), custom_call_target="tpu_custom_call" | custom-call | flops 1207959552 | bytes 18874368 | tf_op jit(solution)/shard_map/backward/pallas_call | solution.py:403
  93.5 0.1 collective-permute-start.1
  93.5 2.3 %collective-permute-done.1 = bf16[16,32,768]{2,1,0:T(8,128)(2,1)S(1)} collective-permute-done((bf16[16,32,768]{2,1,0:T(8,128)(2,1)S(1)}, bf16[16,32,768]{2,1,0:T(8,128)(2,1)S(1)}, u32[]{:S(2)}, u32[]{:S(2)}) %collective-permute-start.1) | collective-permute-done | bytes 786464 | tf_op jit(solution)/shard_map/ppermute | solution.py:420
  95.8 0.2 add_convert_fusion
  96.0 15.9 %all_to_all.21 = bf16[16,32,768]{2,1,0:T(8,128)(2,1)S(1)} all-to-all(bf16[16,32,768]{2,1,0:T(8,128)(2,1)S(1)} %add_convert_fusion), channel_id=1, replica_groups={{0,4,8,12},{2,6,10,14},{16,20,24,28},{18,22,26,30},{1,5,9,13},{3,7,11,1..., dimensions={0} | all-to-all | bytes 1572864 | tf_op jit(solution)/shard_map/all_to_all | solution.py:423
  111.9 0.1 join.1
  112.0 2.0 %collective-permute-start.2 = (bf16[2,32,768]{2,1,0:T(8,128)(2,1)S(1)}, bf16[2,32,768]{2,1,0:T(8,128)(2,1)S(1)}, u32[]{:S(2)}, u32[]{:S(2)}) collective-permute-start(bf16[2,32,768]{2,1,0:T(8,128)(2,1)S(1)} %get-tuple-element.28), channel_id=1, source_target_pairs={{0,16},{2,18},{4,20},{6,22},{8,24},{10,26},{12,28},{14,30},{16,0},... | collective-permute-start | bytes 294920 | tf_op jit(solution)/shard_map/ppermute | solution.py:436
  114.0 4.7 %collective-permute-done.2.got_ref = bf16[2,32,768]{2,1,0:T(8,128)(2,1)S(1)} collective-permute-done((bf16[2,32,768]{2,1,0:T(8,128)(2,1)S(1)}, bf16[2,32,768]{2,1,0:T(8,128)(2,1)S(1)}, u32[]{:S(2)}, u32[]{:S(2)}) %collective-permute-start.2) | collective-permute-done | bytes 98336 | tf_op jit(solution)/shard_map/ppermute | solution.py:436
  118.7 0.4 gram.1
  119.1 11.5 %all_to_all.22.refs_0_ = f32[32,8,128]{2,1,0:T(8,128)S(1)} all-to-all(f32[32,8,128]{2,1,0:T(8,128)S(1)} %get-tuple-element.29), channel_id=1, replica_groups=mesh['row'=16,'col'=2] {'row','col'}, dimensions={0} | all-to-all | bytes 262144 | tf_op jit(solution)/shard_map/all_to_all | solution.py:449
  130.6 5.2 %last.1 = f32[2,32,768]{2,1,0:T(8,128)} custom-call(f32[32,8,128]{2,1,0:T(8,128)S(1)} %all_to_all.22.refs_0_, f32[2,32,768]{2,1,0:T(8,128)S(1)} %get-tuple-element.30.refs_1_), custom_call_target="tpu_custom_call" | custom-call | tf_op jit(solution)/shard_map/last/pallas_call | solution.py:450
Async XLA Ops:
  0.0 0.9 copy-start.2
  1.0 0.7 copy-start.5
  17.2 26.6 %copy-start.4 = (bf16[2,64,256]{2,1,0:T(8,128)(2,1)S(1)}, bf16[2,64,256]{2,1,0:T(8,128)(2,1)}, u32[]{:S(2)}) copy-start(bf16[2,64,256]{2,1,0:T(8,128)(2,1)} %constant.10.clone.refs_0_) | copy-start | bytes 196612
  43.8 12.8 %copy-start.3 = (bf16[2,128,96]{2,1,0:T(8,128)(2,1)S(1)}, bf16[2,128,96]{2,1,0:T(8,128)(2,1)}, u32[]{:S(2)}) copy-start(bf16[2,128,96]{2,1,0:T(8,128)(2,1)} %constant.11.clone.refs_0_) | copy-start | bytes 147460
  44.2 12.4 %collective-permute-start = (bf16[2,32,1536]{2,1,0:T(8,128)(2,1)S(1)}, bf16[2,32,1536]{2,1,0:T(8,128)(2,1)S(1)}, u32[]{:S(2)}, u32[]{:S(2)}) collective-permute-start(bf16[2,32,1536]{2,1,0:T(8,128)(2,1)S(1)} %get-tuple-element.23), channel_id=1, source_target_pairs={{0,16},{2,18},{4,20},{6,22},{8,24},{10,26},{12,28},{14,30},{16,0},... | collective-permute-start | bytes 589832 | tf_op jit(solution)/shard_map/ppermute | solution.py:390
  58.2 24.6 %all-to-all-start.1 = ((bf16[16,32,1536]{2,1,0:T(8,128)(2,1)}), bf16[16,32,1536]{2,1,0:T(8,128)(2,1)S(1)}, u32[]{:S(2)}, u32[]{:S(2)}) async-start(bf16[16,32,1536]{2,1,0:T(8,128)(2,1)} %bitcast.3), calls=%async_computation.1 | async-start | bytes 3145728 | tf_op jit(solution)/shard_map/all_to_all | solution.py:400
  82.7 1.0 copy-start
  83.7 0.9 copy-start.1
  93.5 2.4 %collective-permute-start.1 = (bf16[16,32,768]{2,1,0:T(8,128)(2,1)S(1)}, bf16[16,32,768]{2,1,0:T(8,128)(2,1)S(1)}, u32[]{:S(2)}, u32[]{:S(2)}) collective-permute-start(bf16[16,32,768]{2,1,0:T(8,128)(2,1)S(1)} %get-tuple-element.26), channel_id=1, source_target_pairs={{0,2},{2,0},{4,6},{6,4},{8,10},{10,8},{12,14},{14,12},{16,18},{18,... | collective-permute-start | bytes 2359304 | tf_op jit(solution)/shard_map/ppermute | solution.py:420
  112.0 6.7 %collective-permute-start.2 = (bf16[2,32,768]{2,1,0:T(8,128)(2,1)S(1)}, bf16[2,32,768]{2,1,0:T(8,128)(2,1)S(1)}, u32[]{:S(2)}, u32[]{:S(2)}) collective-permute-start(bf16[2,32,768]{2,1,0:T(8,128)(2,1)S(1)} %get-tuple-element.28), channel_id=1, source_target_pairs={{0,16},{2,18},{4,20},{6,22},{8,24},{10,26},{12,28},{14,30},{16,0},... | collective-permute-start | bytes 294920 | tf_op jit(solution)/shard_map/ppermute | solution.py:436

commit v5 on v4

--- a/solution.py
+++ b/solution.py
@@ -28,25 +28,55 @@
     return high, low
 
 
-def cosine_turns(turns):
-    u = turns * turns
-    out = jnp.full_like(u, COS_COEFS[-1])
-    for coef in COS_COEFS[-2::-1]:
+def _fit(fn, degree):
+    nodes = np.cos(np.pi * (np.arange(64) + 0.5) / 64)
+    u = (nodes + 1.0) / 128
+    series = np.polynomial.chebyshev.Chebyshev.fit(u, fn(np.sqrt(u)), degree, domain=[0.0, 1 / 64])
+    return [float(x) for x in series.convert(kind=np.polynomial.Polynomial, domain=[-1, 1], window=[-1, 1]).coef]
+
+
+COS_COEFS = _fit(lambda t: np.cos(2 * np.pi * t), 5)
+SIN_COEFS = _fit(lambda t: np.sin(2 * np.pi * t) / t, 5)
+
+
+def polynomial(coefs, u):
+    out = jnp.full_like(u, coefs[-1])
+    for coef in coefs[-2::-1]:
         out = out * u + coef
     return out
 
 
-def _fit_cosine():
-    nodes = np.cos(np.pi * (np.arange(64) + 0.5) / 64)
-    u = 0.125 * (nodes + 1.0)
-    series = np.polynomial.chebyshev.Chebyshev.fit(
-        u, np.cos(2 * np.pi * np.sqrt(u)), 8, domain=[0.0, 0.25]
-    )
-    coefs = series.convert(kind=np.polynomial.Polynomial, domain=[-1, 1], window=[-1, 1]).coef
-    return [float(x) for x in coefs]
-
-
-COS_COEFS = _fit_cosine()
+def cos_sin(turns):
+    quarter = jnp.round(turns * 4.0)
+    rest = turns - quarter * 0.25
+    u = rest * rest
+    cos, sin = polynomial(COS_COEFS, u), polynomial(SIN_COEFS, u) * rest
+    odd = jnp.abs(quarter) == 1.0
+    far = jnp.abs(quarter) == 2.0
+    flip_cos = jnp.logical_or(quarter == 1.0, far)
+    flip_sin = jnp.logical_or(quarter == -1.0, far)
+    out_cos, out_sin = jnp.where(odd, sin, cos), jnp.where(odd, cos, sin)
+    return jnp.where(flip_cos, -out_cos, out_cos), jnp.where(flip_sin, -out_sin, out_sin)
+
+
+def mod_turns(x):
+    return (x - jnp.round(x * (1.0 / PRIME)) * float(PRIME)) * (1.0 / PRIME)
+
+
+def channel_values(n_freq, n_blocks, freq, step, sine):
+    turns = ((2 * freq + 1) * step % (4 * n_freq)).astype(F32) * (0.25 / n_freq)
+    cos, sin = cos_sin(turns - jnp.round(turns))
+    values = jnp.where(sine, sin, cos) * jnp.exp(step.astype(F32) * (-math.log(3.0) / n_blocks))
+    return values
+
+
+def split(values):
+    high = values.astype(BF16).astype(F32)
+    return high, values - high
+
+
+def iotas(rows, cols):
+    return (lax.broadcasted_iota(jnp.int32, (rows, cols), d) for d in range(2))
 
 
 def place(rows, cols, test):
@@ -59,59 +89,90 @@
     return x - (x.astype(F32) * (1.0 / PRIME)).astype(jnp.int32) * PRIME
 
 
-def forward_kernel(local, seeds_ref, table_ref, d_ref, t_ref, held, wide, acc, probes, shift, spread, q_all, own, sems, sem):
+def forward_kernel(local, n_freq, seeds_ref, d_ref, t_ref, held, wide, acc, probes, cos_shift, sin_shift, state, spread, q_all, own, sems, sem):
     n_chunks, rows, m = held.shape
     block_c = rows // local
     channels = 2 * local
-    n_blocks, lanes = shift.shape[1:]
+    n_blocks, lanes = cos_shift.shape[1:]
     group = 8
     tiles = P_SIZE // 8
-    lane_w = wide.shape[-1]
-    per_pass = wide.shape[1]
-
-    def copy(b):
-        return pltpu.make_async_copy(d_ref.at[pl.ds(b * rows, rows)], held.at[b], sems.at[b])
-
-    fetch = pltpu.make_async_copy(table_ref.at[lax.axis_index("row")], own, sem)
+    per_pass, lane_w = wide.shape[1], wide.shape[3]
+    passes = m // (per_pass * lane_w)
+
+    width = per_pass * lane_w
+
+    def copy(b, i):
+        part = (slice(b * rows, (b + 1) * rows), slice(i * width, (i + 1) * width))
+        return pltpu.make_async_copy(d_ref.at[part], held.at[b, :, part[1]], sems.at[b, i])
+
+    fetch = pltpu.make_async_copy(seeds_ref, own, sem)
     fetch.start()
     for b in range(n_chunks):
-        copy(b).start()
-    start = lax.axis_index("col") * (n_chunks * block_c)
-    line = lax.broadcasted_iota(jnp.int32, (n_blocks, lanes), 0)
-    seeds = jnp.zeros((n_blocks, lanes), jnp.int32)
-    for j in range(n_blocks):
-        seeds = jnp.where(line == j, seeds_ref[j], seeds)
-    for p in range(P_SIZE):
-        x = (seeds * (p + 1)).astype(F32)
-        shift[p] = (x - jnp.round(x * (1.0 / PRIME)) * float(PRIME)) * float(p + 2)
-    acc[...] = jnp.zeros_like(acc)
-    fetch.wait()
-    table = own[...]
+        for i in range(passes):
+            copy(b, i).start()
+
+    row, col = iotas(channels, n_blocks)
+    table = channel_values(n_freq, n_blocks, lax.axis_index("row") * local + row % local, col, row >= local)
     left = place(channels * group, channels, lambda r, c: r // group == c)
     right = place(n_blocks, group * n_blocks, lambda r, c: r == c % n_blocks)
     same = place(channels * group, group * n_blocks, lambda r, c: r % group == c // n_blocks)
-    for part in range(2):
-        w = jnp.dot(table[part * channels : (part + 1) * channels], right, preferred_element_type=F32)
+    for part, w in enumerate(split(table)):
+        w = jnp.dot(w, right, preferred_element_type=F32)
         spread[part] = (jnp.dot(left, w, preferred_element_type=F32) * same).astype(BF16)
 
-    @pl.loop(0, n_chunks)
-    def _(b):
-        lane = lax.broadcasted_iota(jnp.int32, (n_blocks, lanes), 1)
-        for at in range(0, block_c, lanes):
+    fetch.wait()
+    line, lane = iotas(n_blocks, lanes)
+    seeds = jnp.zeros((n_blocks, lanes), jnp.int32)
+    for j in range(n_blocks):
+        seeds = jnp.where(line == j, own[j], seeds)
+    steps = (lane + 1).astype(F32)
+    shift = mod_turns(seeds.astype(F32) * steps) * float(PRIME)
+    shift_parts = cos_sin(mod_turns(jnp.round(shift) * (steps + 1.0)))
+    for p in range(P_SIZE):
+        for part, out in zip(shift_parts, (cos_shift, sin_shift)):
+            out[p] = jnp.broadcast_to(part[:, p : p + 1], (n_blocks, lanes))
+
+    start = lax.axis_index("col") * (n_chunks * block_c)
+    spans = [(at, p) for at in range(0, block_c, lanes) for p in range(0, P_SIZE, 8)]
+
+    def make_probes(b, span):
+        at, first = span
+        if first == 0:
             column = start + b * block_c + at + lane
             inner = less_turns(less_turns(seeds * (column + 1)) * (column + 3)).astype(F32)
-            for p in range(P_SIZE):
-                x = inner * float(p + 1) + shift[p]
-                turns = (x - jnp.round(x * (1.0 / PRIME)) * float(PRIME)) * (1.0 / PRIME)
-                probes[p * n_blocks : (p + 1) * n_blocks, at : at + lanes] = cosine_turns(turns).astype(BF16)
+            turn_cos, turn_sin = cos_sin(mod_turns(inner))
+            cos, sin = turn_cos, turn_sin
+        else:
+            cos, sin, turn_cos, turn_sin = (state[i] for i in range(4))
+        for p in range(first, first + 8):
+            value = cos * cos_shift[p] - sin * sin_shift[p]
+            probes[p * n_blocks : (p + 1) * n_blocks, at : at + lanes] = value.astype(BF16)
+            cos, sin = cos * turn_cos - sin * turn_sin, sin * turn_cos + cos * turn_sin
+        for i, x in enumerate((cos, sin, turn_cos, turn_sin)):
+            state[i] = x
+
+    def make_channels(b):
         for g in range(P_SIZE // group):
             block = probes[g * group * n_blocks : (g + 1) * group * n_blocks, :]
             q = jnp.dot(spread[0], block, preferred_element_type=F32) + jnp.dot(
                 spread[1], block, preferred_element_type=F32
             )
-            q_all[:, g * group : (g + 1) * group, :] = q.reshape(channels, group, block_c)
-        copy(b).wait()
-        for i in range(m // (per_pass * lane_w)):
+            q = q.astype(BF16)
+            for part in range(2):
+                for k in range(local):
+                    at = (part * local + k) * group
+                    to = part * P_SIZE + g * group
+                    q_all[b % 2, k, to : to + group, :] = q[at : at + group]
+
+    for span in spans:
+        make_probes(0, span)
+    make_channels(0)
+    for b in range(n_chunks):
+        for i in range(passes):
+            copy(b, i).wait()
+            if b + 1 < n_chunks:
+                for span in spans[len(spans) * i // passes : len(spans) * (i + 1) // passes]:
+                    make_probes(b + 1, span)
             for l in range(per_pass):
                 at = (i * per_pass + l) * lane_w
                 wide[i % 2, l] = held[b, :, at : at + lane_w].astype(F32)
@@ -119,48 +180,28 @@
                 s = jnp.concatenate(
                     [wide[i % 2, l, pl.ds(k, block_c, stride=local), :] for l in range(per_pass)], axis=1
                 ).astype(BF16)
-                q = jnp.concatenate([q_all[k], q_all[local + k]], axis=0).astype(BF16)
-                o = jnp.dot(q, s, preferred_element_type=F32)
+                o = jnp.dot(q_all[b % 2, k], s, preferred_element_type=F32)
                 for l in range(per_pass):
                     for t in range(2 * tiles):
-                        acc[i * per_pass + l, t, k * 8 : k * 8 + 8, :] += o[
-                            t * 8 : t * 8 + 8, l * lane_w : (l + 1) * lane_w
-                        ]
-
-    for l in range(m // lane_w):
-        for p in range(P_SIZE):
-            t = jnp.concatenate(
-                [acc[l, part * tiles + p // 8, pl.ds(p % 8, local, stride=8), :] for part in range(2)], axis=0
-            )
-            t_ref[p, :, l * lane_w : (l + 1) * lane_w] = t.astype(BF16)
-
-
-def separate_kernel(local, n_row, group, d_ref, table_ref, o_ref, khi_ref, klo_ref, wide):
+                        piece = o[t * 8 : t * 8 + 8, l * lane_w : (l + 1) * lane_w]
+                        if b > 0:
+                            piece += acc[i * per_pass + l, t, k * 8 : k * 8 + 8, :]
+                        acc[i * per_pass + l, t, k * 8 : k * 8 + 8, :] = piece
+            if b + 1 == n_chunks:
+                for l in range(i * per_pass, (i + 1) * per_pass):
+                    for p in range(P_SIZE):
+                        t = jnp.concatenate(
+                            [acc[l, part * tiles + p // 8, pl.ds(p % 8, local, stride=8), :] for part in range(2)],
+                            axis=0,
+                        )
+                        t_ref[p, :, l * lane_w : (l + 1) * lane_w] = t.astype(BF16)
+        if b + 1 < n_chunks:
+            make_channels(b + 1)
+
+
+def separate_kernel(local, d_ref, o_ref, wide):
     rows, m = d_ref.shape
     lane_w = wide.shape[-1]
-
-    @pl.when(pl.program_id(0) == 0)
-    def _():
-        row_at = lax.axis_index("row")
-        table = table_ref[row_at]
-        channels = 2 * local
-        n_blocks = table.shape[0] // 2
-        half, own, quarter = n_blocks // 2, n_blocks // n_row, n_row // 4
-
-        def is_owner(r, c):
-            rest = r % half
-            chip = rest // (2 * own) + quarter * ((rest // own + half_of(n_row)) % 2)
-            return (2 * chip + (r // half + row_at) % 2) * own + rest % own == c
-
-        pick = place(n_blocks, n_blocks, is_owner)
-        right = place(channels, channels * group, lambda r, c: r == c // 32 * 2 + c // 8 % 2)
-        left = place(n_blocks * group, n_blocks, lambda r, c: r // group == c)
-        same = place(n_blocks * group, channels * group, lambda r, c: r % group == c // 16 % 2 * 8 + c % 8)
-        for part, out_ref in enumerate((khi_ref, klo_ref)):
-            k = jnp.dot(pick, table[part * n_blocks : (part + 1) * n_blocks], preferred_element_type=F32)
-            k = jnp.dot(left, jnp.dot(k, right, preferred_element_type=F32), preferred_element_type=F32)
-            out_ref[...] = (k * same).astype(BF16)
-
     for l in range(m // lane_w):
         at = slice(l * lane_w, (l + 1) * lane_w)
         wide[l % 2] = d_ref[:, at].astype(F32)
@@ -204,7 +245,7 @@
     send_ref[...] = total[1].astype(BF16)
 
 
-def backward_kernel(local, khi_ref, klo_ref, f_ref, d_ref, keep_ref, send_ref, held, f_by, sems):
+def backward_kernel(local, n_row, n_blocks, amp, f_ref, d_ref, keep_ref, send_ref, held, f_by, k_parts, sems):
     n_chunks, _, m, block_c = held.shape
     rows = f_ref.shape[0] // 4
     channels = 2 * local
@@ -215,14 +256,28 @@
 
     for b in range(n_chunks):
         copy(b).start()
+
+    row_at = lax.axis_index("row")
+    half, per_owner, quarter = n_blocks // 2, n_blocks // n_row, n_row // 4
+    r, c = iotas(n_blocks, channels)
+    rest = r % half
+    chip = rest // (2 * per_owner) + quarter * ((rest // per_owner + half_of(n_row)) % 2)
+    block_at = (2 * chip + (r // half + row_at) % 2) * per_owner + rest % per_owner
+    sine = c % 2 == 1
+    table = channel_values(local * n_row, n_blocks, row_at * local + c // 2, block_at + 1, sine)
+    table = table * jnp.where(sine, -amp, amp)
+    left = place(n_blocks * 16, n_blocks, lambda r, c: r // 16 == c)
+    right = place(channels, channels * 16, lambda r, c: r == c // 32 * 2 + c // 8 % 2)
+    same = place(n_blocks * 16, channels * 16, lambda r, c: r % 16 == c // 16 % 2 * 8 + c % 8)
+    for part, k in enumerate(split(table)):
+        k = jnp.dot(left, jnp.dot(k, right, preferred_element_type=F32), preferred_element_type=F32)
+        k_parts[part] = (k * same).astype(BF16)
 
     swap = place(rows, rows, lambda r, c: (r % 8 * 2 + r // 8 % 2) * local + r // 16 == c).astype(BF16)
     for g in range(4):
         out = jnp.dot(swap, f_ref[g * rows : (g + 1) * rows, :], preferred_element_type=F32).astype(BF16)
         for k in range(local):
             f_by[k, g * 16 : g * 16 + 16, :] = out[k * 16 : k * 16 + 16]
-
-    half = keep_ref.shape[0]
 
     @pl.loop(0, n_chunks)
     def _(b):
@@ -231,8 +286,8 @@
         u = [jnp.dot(f_by[k], held[b, k], preferred_element_type=F32).astype(BF16) for k in range(local)]
         for g in range(2):
             block = jnp.concatenate([x[g * 32 : g * 32 + 32] for x in u], axis=0)
-            out = jnp.dot(khi_ref[...], block, preferred_element_type=F32) + jnp.dot(
-                klo_ref[...], block, preferred_element_type=F32
+            out = jnp.dot(k_parts[0], block, preferred_element_type=F32) + jnp.dot(
+                k_parts[1], block, preferred_element_type=F32
             )
             out = out.reshape(2 * half, 16, block_c)
             keep_ref[:, g * 16 : g * 16 + 16, at] = out[:half]
@@ -261,7 +316,7 @@
     scale = jnp.sum(gram * eye, keepdims=True) + 1e-06
 
     def dot(a, b):
-        return jnp.dot(a, b, preferred_element_type=F32, precision=lax.Precision.HIGHEST)
+        return jnp.dot(a, b, preferred_element_type=F32, precision=lax.Precision.HIGH)
 
     current = gram / scale
     inverse = eye
@@ -299,31 +354,19 @@
     per_pass = 2 if m % (2 * lane_w) == 0 else 1
     flat = damping.reshape(cols * local, m)
 
-    freqs = np.arange(n_freq)
-    steps = np.arange(n_blocks)
-    w_all = channel_table(n_freq, freqs, steps, n_blocks)
-    sign = np.array([1.0, -1.0])[None, :, None]
-    back_all = channel_table(n_freq, freqs, steps + 1, n_blocks) * sign * amp
-    back_row = back_all.reshape(n_row, channels, n_blocks).transpose(0, 2, 1)
-
-    def by_channel(table):
-        table = table.reshape(n_row, local, 2, n_blocks)
-        return table.transpose(0, 2, 1, 3).reshape(n_row, channels, n_blocks)
-
-    w_row = by_channel(w_all)
-    w_parts = np.concatenate([x.astype(np.float32) for x in high_low(w_row)], axis=1)
-
-    k_parts = np.concatenate([x.astype(np.float32) for x in high_low(back_row)], axis=1)
+    w_row = channel_table(n_freq, np.arange(n_freq), np.arange(n_blocks), n_blocks)
+    w_row = w_row.reshape(n_row, local, 2, n_blocks).transpose(0, 2, 1, 3)
+    sign = np.array([1.0, -1.0])[None, :, None, None] * amp
     per_owner, half, quarter = n_blocks // n_row, n_blocks // 2, n_row // 4
-    group = 16
+
     n_rows = P_SIZE * channels
     whole = lambda *s: pl.BlockSpec(s, lambda i: (0,) * len(s))
     v_one = pl.BlockSpec(memory_space=pltpu.VMEM)
     work = 2 * cols * local * m
     t = pl.pallas_call(
-        lambda *refs: forward_kernel(local, *refs),
+        lambda *refs: forward_kernel(local, n_freq, *refs),
         out_shape=jax.ShapeDtypeStruct((P_SIZE, channels, m), BF16),
-        in_specs=[pl.BlockSpec(memory_space=pltpu.SMEM)] + [pl.BlockSpec(memory_space=pltpu.HBM)] * 2,
+        in_specs=[pl.BlockSpec(memory_space=pl.ANY)] * 2,
         out_specs=v_one,
         scratch_shapes=[
             pltpu.VMEM((cols // block_c, block_c * local, m), BF16),
@@ -331,34 +374,31 @@
             pltpu.VMEM((m // lane_w, P_SIZE // 4, 8 * local, lane_w), F32),
             pltpu.VMEM((P_SIZE * n_blocks, block_c), BF16),
             pltpu.VMEM((P_SIZE, n_blocks, lanes_c), F32),
+            pltpu.VMEM((P_SIZE, n_blocks, lanes_c), F32),
+            pltpu.VMEM((4, n_blocks, lanes_c), F32),
             pltpu.VMEM((2, channels * 8, 8 * n_blocks), BF16),
-            pltpu.VMEM((channels, P_SIZE, block_c), F32),
-            pltpu.VMEM((2 * channels, n_blocks), F32),
-            pltpu.SemaphoreType.DMA((cols // block_c,)),
+            pltpu.VMEM((2, local, 2 * P_SIZE, block_c), BF16),
+            pltpu.SMEM((n_blocks,), jnp.int32),
+            pltpu.SemaphoreType.DMA((cols // block_c, m // (per_pass * lane_w))),
             pltpu.SemaphoreType.DMA,
         ],
         compiler_params=large,
         cost_estimate=pl.CostEstimate(flops=64 * work, bytes_accessed=work, transcendentals=0),
         name="forward",
-    )(block_seeds, jnp.asarray(w_parts), flat)
+    )(block_seeds, flat)
     t, flat = lax.optimization_barrier((t, flat))
     block_s = 128 if cols % 128 == 0 else cols
-    k_shape = (n_blocks * group, channels * group)
-    by_freq, k_hi, k_lo = pl.pallas_call(
-        lambda *refs: separate_kernel(local, n_row, group, *refs),
+    by_freq = pl.pallas_call(
+        lambda *refs: separate_kernel(local, *refs),
         grid=(cols // block_s,),
-        out_shape=(
-            jax.ShapeDtypeStruct((local, m, cols), BF16),
-            jax.ShapeDtypeStruct(k_shape, BF16),
-            jax.ShapeDtypeStruct(k_shape, BF16),
-        ),
-        in_specs=[pl.BlockSpec((block_s * local, m), lambda i: (i, 0)), whole(*k_parts.shape)],
-        out_specs=(pl.BlockSpec((local, m, block_s), lambda i: (0, 0, i)), whole(*k_shape), whole(*k_shape)),
+        out_shape=jax.ShapeDtypeStruct((local, m, cols), BF16),
+        in_specs=[pl.BlockSpec((block_s * local, m), lambda i: (i, 0))],
+        out_specs=pl.BlockSpec((local, m, block_s), lambda i: (0, 0, i)),
         scratch_shapes=[pltpu.VMEM((2, block_s * local, lane_w), F32)],
         compiler_params=most,
         cost_estimate=pl.CostEstimate(flops=work, bytes_accessed=2 * work, transcendentals=0),
         name="separate",
-    )(flat, jnp.asarray(k_parts))
+    )(flat)
 
     n_grp = n_dev // 2
     n_p = math.gcd(P_SIZE, n_grp)
@@ -369,9 +409,10 @@
     t = t.reshape(n_p, p_own * channels, n_r, lanes).transpose(0, 2, 1, 3)
     t = t.reshape(n_grp, p_own * channels, lanes)
     t = lax.all_to_all(t, ("row", "col"), 0, 0, axis_index_groups=halves, tiled=True)
+    t, by_freq = lax.optimization_barrier((t, by_freq))
     t = t.reshape(n_grp, p_own, channels, lanes)
 
-    merge = by_channel(w_all * sign * amp).reshape(2, n_row // 2, 1, channels, n_blocks).repeat(n_col, axis=2)
+    merge = (w_row * sign).reshape(2, n_row // 2, 1, channels, n_blocks).repeat(n_col, axis=2)
     merge = merge.reshape(2, n_grp * channels, n_blocks).transpose(0, 2, 1)
     merge = np.concatenate(high_low(merge), axis=1)
     b_hi, b_lo = high_low(w_row.reshape(2, n_row // 2 * channels, n_blocks))
@@ -401,22 +442,23 @@
     f = f.reshape(n_p, n_r, p_own * channels, lanes).transpose(0, 2, 1, 3).reshape(n_rows, m)
 
     keep, send = pl.pallas_call(
-        lambda *refs: backward_kernel(local, *refs),
+        lambda *refs: backward_kernel(local, n_row, n_blocks, amp, *refs),
         out_shape=(
             jax.ShapeDtypeStruct((half, P_SIZE, cols), F32),
             jax.ShapeDtypeStruct((half, P_SIZE, cols), BF16),
         ),
-        in_specs=vmem(3) + [pl.BlockSpec(memory_space=pl.ANY)],
+        in_specs=vmem(1) + [pl.BlockSpec(memory_space=pl.ANY)],
         out_specs=tuple(vmem(2)),
         scratch_shapes=[
             pltpu.VMEM((cols // block_s, local, m, block_s), BF16),
             pltpu.VMEM((local, 2 * P_SIZE, m), BF16),
+            pltpu.VMEM((2, n_blocks * 16, channels * 16), BF16),
             pltpu.SemaphoreType.DMA((cols // block_s,)),
         ],
         compiler_params=large,
         cost_estimate=pl.CostEstimate(flops=64 * work, bytes_accessed=work, transcendentals=0),
         name="backward",
-    )(k_hi, k_lo, f, by_freq)
+    )(f, by_freq)
     got = lax.ppermute(send, "row", [(i, i ^ 1) for i in range(n_row)])
     summed = (keep + got.astype(F32)).astype(BF16)
     groups = [[core + 2 * (i + quarter * h) for i in range(quarter)] for h in range(2) for core in range(2)]

time: 136 us -> 130 us (0.956)
  starting transfers between devices: 8.38 us -> 12 us
  Pallas kernels: 50.9 us -> 47.5 us
  local copies, waits for them, and re-layouts: 3.51 us -> 0.67 us
  blocking collectives: 54 us -> 52.5 us
  waiting for transfers between devices: 18.6 us -> 17.1 us
    unnamed x12 -> x6, local copies, waits for them, and re-layouts: 3.51 us -> 0.67 us
    all_to_all x1, starting transfers between devices: 3.71 us -> 6.34 us  [shards(): lax.all_to_all(t, ('row', 'col'), 0, 0, axis_index_groups=halves, tiled=T...]
    ppermute x2, waiting for transfers between devices: 14.5 us -> 12.5 us  [shards(): got = lax.ppermute(send, 'row', across)]
    pallas_call x3, Pallas kernels: 43.4 us -> 41.7 us  [the longest x1 18.2 us: shards(): pl.pallas_call(lambda *refs: separate_kernel(local, *refs), grid=(cols //...]
where the time goes in v5:
time: 130 us
  blocking collectives  52.5 us (40%)
  Pallas kernels  47.5 us (37%)
  waiting for transfers between devices  17.1 us (13%)
  starting transfers between devices  12 us (9%)
    all_to_all x1, blocking collectives, shards(): lax.all_to_all(f, ('row', 'col'), 0, 0, axis_index_groups=halves, tiled=T...  25.3 us
    pallas_call x1, Pallas kernels, shards(): pl.pallas_call(lambda *refs: separate_kernel(local, *refs), grid=(cols //...  18.2 us
    all_to_all x1, blocking collectives, shards(): lax.all_to_all(summed, 'row', 0, 0, axis_index_groups=groups, tiled=True)  14.6 us
    pallas_call x1, Pallas kernels, shards(): pl.pallas_call(lambda *refs: forward_kernel(local, n_freq, *refs), out_sh...  14.4 us
    all_to_all x1, blocking collectives, shards(): gram = lax.all_to_all(gram, ('row', 'col'), 0, 0, tiled=True)  12.7 us
    ppermute x2, waiting for transfers between devices, shards(): got = lax.ppermute(send, 'row', across)  12.5 us
    pallas_call x1, Pallas kernels, shards(): pl.pallas_call(lambda *refs: backward_kernel(local, n_row, n_blocks, amp,...  9.1 us
    all_to_all x1, starting transfers between devices, shards(): lax.all_to_all(t, ('row', 'col'), 0, 0, axis_index_groups=halves, tiled=T...  6.34 us
  transfers between devices with their start and end apart: 4, of which 4 were waited for; matrix products, arithmetic and copies ran while one was open for 0% of the time, Pallas kernels for 14%

profile of v5, /device:TPU:0, one launch (start us, length us, event | category | flops | bytes accessed | tf_op | source)
XLA Modules:
  0.0 130.1 jit_solution(4428692136490392220)
XLA Ops:
  0.0 0.0 copy-start.2
  0.0 0.7 copy-done.2
  0.7 14.4 %forward.1 = bf16[32,16,1536]{2,1,0:T(8,128)(2,1)} custom-call(s32[32]{0:T(128)S(1)} %copy-done.2, bf16[6144,1536]{1,0:T(8,128)(2,1)} %bitcast.11), custom_call_target="tpu_custom_call" | custom-call | flops 1207959552 | bytes 18874368 | tf_op jit(solution)/shard_map/forward/pallas_call | solution.py:366
  15.1 6.3 %all-to-all-start = ((bf16[16,32,1536]{2,1,0:T(8,128)(2,1)}), bf16[16,32,1536]{2,1,0:T(8,128)(2,1)S(1)}, u32[]{:S(2)}, u32[]{:S(2)}) async-start(bf16[16,32,1536]{2,1,0:T(8,128)(2,1)} %bitcast.1), calls=%async_computation | async-start | bytes 3145728 | tf_op jit(solution)/shard_map/all_to_all | solution.py:411
  21.4 0.0 copy-start.1
  21.4 18.2 %separate.1.refs_1_ = bf16[8,1536,768]{2,1,0:T(8,128)(2,1)} custom-call(bf16[6144,1536]{1,0:T(8,128)(2,1)} %bitcast.12), custom_call_target="tpu_custom_call" | custom-call | flops 18874368 | bytes 37748736 | tf_op jit(solution)/shard_map/separate/pallas_call | solution.py:391
  39.6 0.0 copy-start
  39.6 2.7 %all-to-all-done = bf16[16,32,1536]{2,1,0:T(8,128)(2,1)S(1)} async-done(((bf16[16,32,1536]{2,1,0:T(8,128)(2,1)}), bf16[16,32,1536]{2,1,0:T(8,128)(2,1)S(1)}, u32[]{:S(2)}, u32[]{:S(2)}) %all-to-all-start) | async-done | bytes 1572896 | tf_op jit(solution)/shard_map/all_to_all | solution.py:411
  42.3 0.0 copy-done.1
  42.3 0.4 gather.1
  42.7 2.6 %collective-permute-start = (bf16[2,32,1536]{2,1,0:T(8,128)(2,1)S(1)}, bf16[2,32,1536]{2,1,0:T(8,128)(2,1)S(1)}, u32[]{:S(2)}, u32[]{:S(2)}) collective-permute-start(bf16[2,32,1536]{2,1,0:T(8,128)(2,1)S(1)} %get-tuple-element.21), channel_id=1, source_target_pairs={{0,16},{2,18},{4,20},{6,22},{8,24},{10,26},{12,28},{14,30},{16,0},... | collective-permute-start | bytes 589832 | tf_op jit(solution)/shard_map/ppermute | solution.py:431
  45.3 8.4 %collective-permute-done.refs_2_ = bf16[2,32,1536]{2,1,0:T(8,128)(2,1)S(1)} collective-permute-done((bf16[2,32,1536]{2,1,0:T(8,128)(2,1)S(1)}, bf16[2,32,1536]{2,1,0:T(8,128)(2,1)S(1)}, u32[]{:S(2)}, u32[]{:S(2)}) %collective-permute-start) | collective-permute-done | bytes 196640 | tf_op jit(solution)/shard_map/ppermute | solution.py:431
  53.7 0.0 copy-done
  53.7 0.4 scatter.1
  54.1 25.3 %all_to_all.20 = bf16[16,32,1536]{2,1,0:T(8,128)(2,1)S(1)} all-to-all(bf16[16,32,1536]{2,1,0:T(8,128)(2,1)S(1)} %bitcast.9), channel_id=1, replica_groups={{0,1,2,3,4,5,6,7,8,9,10,11,12,13,14,15},{16,17,18,19,20,21,22,23,24,25,..., dimensions={0} | all-to-all | bytes 3145728 | tf_op jit(solution)/shard_map/all_to_all | solution.py:441
  79.4 9.1 %backward.1 = (f32[16,32,768]{2,1,0:T(8,128)S(1)}, bf16[16,32,768]{2,1,0:T(8,128)(2,1)S(1)}) custom-call(bf16[512,1536]{1,0:T(8,128)(2,1)S(1)} %bitcast.8, bf16[8,1536,768]{2,1,0:T(8,128)(2,1)} %separate.1.refs_1_), custom_call_target="tpu_custom_call" | custom-call | flops 1207959552 | bytes 18874368 | tf_op jit(solution)/shard_map/backward/pallas_call | solution.py:444
  88.5 0.5 collective-permute-start.1
  89.0 1.9 %collective-permute-done.1 = bf16[16,32,768]{2,1,0:T(8,128)(2,1)S(1)} collective-permute-done((bf16[16,32,768]{2,1,0:T(8,128)(2,1)S(1)}, bf16[16,32,768]{2,1,0:T(8,128)(2,1)S(1)}, u32[]{:S(2)}, u32[]{:S(2)}) %collective-permute-start.1) | collective-permute-done | bytes 786464 | tf_op jit(solution)/shard_map/ppermute | solution.py:462
  90.9 0.2 add_convert_fusion
  91.2 14.6 %all_to_all.21 = bf16[16,32,768]{2,1,0:T(8,128)(2,1)S(1)} all-to-all(bf16[16,32,768]{2,1,0:T(8,128)(2,1)S(1)} %add_convert_fusion), channel_id=1, replica_groups={{0,4,8,12},{2,6,10,14},{16,20,24,28},{18,22,26,30},{1,5,9,13},{3,7,11,1..., dimensions={0} | all-to-all | bytes 1572864 | tf_op jit(solution)/shard_map/all_to_all | solution.py:465
  105.7 0.1 join.1
  105.8 2.5 %collective-permute-start.2 = (bf16[2,32,768]{2,1,0:T(8,128)(2,1)S(1)}, bf16[2,32,768]{2,1,0:T(8,128)(2,1)S(1)}, u32[]{:S(2)}, u32[]{:S(2)}) collective-permute-start(bf16[2,32,768]{2,1,0:T(8,128)(2,1)S(1)} %get-tuple-element.26), channel_id=1, source_target_pairs={{0,16},{2,18},{4,20},{6,22},{8,24},{10,26},{12,28},{14,30},{16,0},... | collective-permute-start | bytes 294920 | tf_op jit(solution)/shard_map/ppermute | solution.py:478
  108.3 4.1 %collective-permute-done.2.got_ref = bf16[2,32,768]{2,1,0:T(8,128)(2,1)S(1)} collective-permute-done((bf16[2,32,768]{2,1,0:T(8,128)(2,1)S(1)}, bf16[2,32,768]{2,1,0:T(8,128)(2,1)S(1)}, u32[]{:S(2)}, u32[]{:S(2)}) %collective-permute-start.2) | collective-permute-done | bytes 98336 | tf_op jit(solution)/shard_map/ppermute | solution.py:478
  112.5 0.4 gram.1
  112.8 12.7 %all_to_all.22.refs_0_ = f32[32,8,128]{2,1,0:T(8,128)S(1)} all-to-all(f32[32,8,128]{2,1,0:T(8,128)S(1)} %get-tuple-element.27), channel_id=1, replica_groups=mesh['row'=16,'col'=2] {'row','col'}, dimensions={0} | all-to-all | bytes 262144 | tf_op jit(solution)/shard_map/all_to_all | solution.py:491
  125.5 4.6 %last.1 = f32[2,32,768]{2,1,0:T(8,128)} custom-call(f32[32,8,128]{2,1,0:T(8,128)S(1)} %all_to_all.22.refs_0_, f32[2,32,768]{2,1,0:T(8,128)S(1)} %get-tuple-element.28.refs_1_), custom_call_target="tpu_custom_call" | custom-call | tf_op jit(solution)/shard_map/last/pallas_call | solution.py:492
Async XLA Ops:
  0.0 0.7 copy-start.2
  15.1 27.2 %all-to-all-start = ((bf16[16,32,1536]{2,1,0:T(8,128)(2,1)}), bf16[16,32,1536]{2,1,0:T(8,128)(2,1)S(1)}, u32[]{:S(2)}, u32[]{:S(2)}) async-start(bf16[16,32,1536]{2,1,0:T(8,128)(2,1)} %bitcast.1), calls=%async_computation | async-start | bytes 3145728 | tf_op jit(solution)/shard_map/all_to_all | solution.py:411
  21.4 20.9 %copy-start.1 = (bf16[2,64,256]{2,1,0:T(8,128)(2,1)S(1)}, bf16[2,64,256]{2,1,0:T(8,128)(2,1)}, u32[]{:S(2)}) copy-start(bf16[2,64,256]{2,1,0:T(8,128)(2,1)} %constant.4.clone.refs_0_) | copy-start | bytes 196612
  39.6 14.1 %copy-start = (bf16[2,128,96]{2,1,0:T(8,128)(2,1)S(1)}, bf16[2,128,96]{2,1,0:T(8,128)(2,1)}, u32[]{:S(2)}) copy-start(bf16[2,128,96]{2,1,0:T(8,128)(2,1)} %constant.5.clone.refs_0_) | copy-start | bytes 147460
  42.7 11.0 %collective-permute-start = (bf16[2,32,1536]{2,1,0:T(8,128)(2,1)S(1)}, bf16[2,32,1536]{2,1,0:T(8,128)(2,1)S(1)}, u32[]{:S(2)}, u32[]{:S(2)}) collective-permute-start(bf16[2,32,1536]{2,1,0:T(8,128)(2,1)S(1)} %get-tuple-element.21), channel_id=1, source_target_pairs={{0,16},{2,18},{4,20},{6,22},{8,24},{10,26},{12,28},{14,30},{16,0},... | collective-permute-start | bytes 589832 | tf_op jit(solution)/shard_map/ppermute | solution.py:431
  88.5 2.4 %collective-permute-start.1 = (bf16[16,32,768]{2,1,0:T(8,128)(2,1)S(1)}, bf16[16,32,768]{2,1,0:T(8,128)(2,1)S(1)}, u32[]{:S(2)}, u32[]{:S(2)}) collective-permute-start(bf16[16,32,768]{2,1,0:T(8,128)(2,1)S(1)} %get-tuple-element.24), channel_id=1, source_target_pairs={{0,2},{2,0},{4,6},{6,4},{8,10},{10,8},{12,14},{14,12},{16,18},{18,... | collective-permute-start | bytes 2359304 | tf_op jit(solution)/shard_map/ppermute | solution.py:462
  105.8 6.6 %collective-permute-start.2 = (bf16[2,32,768]{2,1,0:T(8,128)(2,1)S(1)}, bf16[2,32,768]{2,1,0:T(8,128)(2,1)S(1)}, u32[]{:S(2)}, u32[]{:S(2)}) collective-permute-start(bf16[2,32,768]{2,1,0:T(8,128)(2,1)S(1)} %get-tuple-element.26), channel_id=1, source_target_pairs={{0,16},{2,18},{4,20},{6,22},{8,24},{10,26},{12,28},{14,30},{16,0},... | collective-permute-start | bytes 294920 | tf_op jit(solution)/shard_map/ppermute | solution.py:478

commit v6 on v5

--- a/solution.py
+++ b/solution.py
@@ -75,6 +75,10 @@
     return high, values - high
 
 
+def separate(x, local):
+    return jnp.swapaxes(x.reshape(x.shape[0] // local, local, x.shape[1]), 0, 1)
+
+
 def iotas(rows, cols):
     return (lax.broadcasted_iota(jnp.int32, (rows, cols), d) for d in range(2))
 
@@ -89,17 +93,15 @@
     return x - (x.astype(F32) * (1.0 / PRIME)).astype(jnp.int32) * PRIME
 
 
-def forward_kernel(local, n_freq, seeds_ref, d_ref, t_ref, held, wide, acc, probes, cos_shift, sin_shift, state, spread, q_all, own, sems, sem):
+def forward_kernel(local, n_freq, seeds_ref, d_ref, t_ref, held, by_freq, acc, probes, cos_shift, sin_shift, state, spread, q_all, own, sems, sem):
     n_chunks, rows, m = held.shape
     block_c = rows // local
     channels = 2 * local
     n_blocks, lanes = cos_shift.shape[1:]
     group = 8
     tiles = P_SIZE // 8
-    per_pass, lane_w = wide.shape[1], wide.shape[3]
-    passes = m // (per_pass * lane_w)
-
-    width = per_pass * lane_w
+    width, lane_w = by_freq.shape[3], acc.shape[3]
+    passes, per_pass = m // width, width // lane_w
 
     def copy(b, i):
         part = (slice(b * rows, (b + 1) * rows), slice(i * width, (i + 1) * width))
@@ -173,14 +175,11 @@
             if b + 1 < n_chunks:
                 for span in spans[len(spans) * i // passes : len(spans) * (i + 1) // passes]:
                     make_probes(b + 1, span)
-            for l in range(per_pass):
-                at = (i * per_pass + l) * lane_w
-                wide[i % 2, l] = held[b, :, at : at + lane_w].astype(F32)
+            at = slice(i * width, (i + 1) * width)
+            for c in range(0, block_c, 16):
+                by_freq[i % 2, :, c : c + 16, :] = separate(held[b, c * local : (c + 16) * local, at], local)
             for k in range(local):
-                s = jnp.concatenate(
-                    [wide[i % 2, l, pl.ds(k, block_c, stride=local), :] for l in range(per_pass)], axis=1
-                ).astype(BF16)
-                o = jnp.dot(q_all[b % 2, k], s, preferred_element_type=F32)
+                o = jnp.dot(q_all[b % 2, k], by_freq[i % 2, k], preferred_element_type=F32)
                 for l in range(per_pass):
                     for t in range(2 * tiles):
                         piece = o[t * 8 : t * 8 + 8, l * lane_w : (l + 1) * lane_w]
@@ -199,14 +198,15 @@
             make_channels(b + 1)
 
 
-def separate_kernel(local, d_ref, o_ref, wide):
+def separate_kernel(local, d_ref, o_ref):
     rows, m = d_ref.shape
-    lane_w = wide.shape[-1]
-    for l in range(m // lane_w):
-        at = slice(l * lane_w, (l + 1) * lane_w)
-        wide[l % 2] = d_ref[:, at].astype(F32)
+    width = 256 if m % 256 == 0 else m
+    for i in range(0, m, width):
+        parts = [
+            separate(d_ref[c : c + 16 * local, i : i + width], local) for c in range(0, rows, 16 * local)
+        ]
         for k in range(local):
-            o_ref[k, at, :] = wide[l % 2, pl.ds(k, rows // local, stride=local), :].T.astype(BF16)
+            o_ref[k, i : i + width, :] = jnp.concatenate([x[k] for x in parts], axis=0).T
 
 
 def half_of(n_row):
@@ -370,7 +370,7 @@
         out_specs=v_one,
         scratch_shapes=[
             pltpu.VMEM((cols // block_c, block_c * local, m), BF16),
-            pltpu.VMEM((2, per_pass, block_c * local, lane_w), F32),
+            pltpu.VMEM((2, local, block_c, per_pass * lane_w), BF16),
             pltpu.VMEM((m // lane_w, P_SIZE // 4, 8 * local, lane_w), F32),
             pltpu.VMEM((P_SIZE * n_blocks, block_c), BF16),
             pltpu.VMEM((P_SIZE, n_blocks, lanes_c), F32),
@@ -394,7 +394,6 @@
         out_shape=jax.ShapeDtypeStruct((local, m, cols), BF16),
         in_specs=[pl.BlockSpec((block_s * local, m), lambda i: (i, 0))],
         out_specs=pl.BlockSpec((local, m, block_s), lambda i: (0, 0, i)),
-        scratch_shapes=[pltpu.VMEM((2, block_s * local, lane_w), F32)],
         compiler_params=most,
         cost_estimate=pl.CostEstimate(flops=work, bytes_accessed=2 * work, transcendentals=0),
         name="separate",

time: 130 us -> 128 us (0.985)
  Pallas kernels: 47.5 us -> 44.2 us
    pallas_call x1, Pallas kernels: 14.4 us -> 12.3 us  [shards(): pl.pallas_call(lambda *refs: forward_kernel(local, n_freq, *refs), out_sh...]
  transfers between devices with their start and end apart: 4 -> 4, of which waited for: 4 -> 4; matrix products, arithmetic and copies ran while one was open for 0% -> 0% of each run, Pallas kernels for 14% -> 13%
where the time goes in v6:
time: 128 us
  blocking collectives  52.5 us (41%)
  Pallas kernels  44.2 us (35%)
  waiting for transfers between devices  18.3 us (14%)
  starting transfers between devices  12 us (9%)
    all_to_all x1, blocking collectives, shards(): lax.all_to_all(f, ('row', 'col'), 0, 0, axis_index_groups=halves, tiled=T...  25.3 us
    pallas_call x1, Pallas kernels, shards(): pl.pallas_call(lambda *refs: separate_kernel(local, *refs), grid=(cols //...  17 us
    all_to_all x1, blocking collectives, shards(): lax.all_to_all(summed, 'row', 0, 0, axis_index_groups=groups, tiled=True)  14.6 us
    all_to_all x1, blocking collectives, shards(): gram = lax.all_to_all(gram, ('row', 'col'), 0, 0, tiled=True)  12.7 us
    ppermute x2, waiting for transfers between devices, shards(): got = lax.ppermute(send, 'row', across)  12.5 us
    pallas_call x1, Pallas kernels, shards(): pl.pallas_call(lambda *refs: forward_kernel(local, n_freq, *refs), out_sh...  12.3 us
    pallas_call x1, Pallas kernels, shards(): pl.pallas_call(lambda *refs: backward_kernel(local, n_row, n_blocks, amp,...  9.11 us
    all_to_all x1, starting transfers between devices, shards(): lax.all_to_all(t, ('row', 'col'), 0, 0, axis_index_groups=halves, tiled=T...  6.32 us
  transfers between devices with their start and end apart: 4, of which 4 were waited for; matrix products, arithmetic and copies ran while one was open for 0% of the time, Pallas kernels for 13%

profile of v6, /device:TPU:0, one launch (start us, length us, event | category | flops | bytes accessed | tf_op | source)
XLA Modules:
  0.0 128.0 jit_solution(7118661585435246281)
XLA Ops:
  0.0 0.0 copy-start.2
  0.0 0.7 copy-done.2
  0.7 12.3 %forward.1 = bf16[32,16,1536]{2,1,0:T(8,128)(2,1)} custom-call(s32[32]{0:T(128)S(1)} %copy-done.2, bf16[6144,1536]{1,0:T(8,128)(2,1)} %bitcast.11), custom_call_target="tpu_custom_call" | custom-call | flops 1207959552 | bytes 18874368 | tf_op jit(solution)/shard_map/forward/pallas_call | solution.py:366
  13.0 6.3 %all-to-all-start = ((bf16[16,32,1536]{2,1,0:T(8,128)(2,1)}), bf16[16,32,1536]{2,1,0:T(8,128)(2,1)S(1)}, u32[]{:S(2)}, u32[]{:S(2)}) async-start(bf16[16,32,1536]{2,1,0:T(8,128)(2,1)} %bitcast.1), calls=%async_computation | async-start | bytes 3145728 | tf_op jit(solution)/shard_map/all_to_all | solution.py:410
  19.3 0.0 copy-start.1
  19.3 17.0 %separate.1.refs_1_ = bf16[8,1536,768]{2,1,0:T(8,128)(2,1)} custom-call(bf16[6144,1536]{1,0:T(8,128)(2,1)} %bitcast.12), custom_call_target="tpu_custom_call" | custom-call | flops 18874368 | bytes 37748736 | tf_op jit(solution)/shard_map/separate/pallas_call | solution.py:391
  36.3 0.0 copy-start
  36.3 3.9 %all-to-all-done = bf16[16,32,1536]{2,1,0:T(8,128)(2,1)S(1)} async-done(((bf16[16,32,1536]{2,1,0:T(8,128)(2,1)}), bf16[16,32,1536]{2,1,0:T(8,128)(2,1)S(1)}, u32[]{:S(2)}, u32[]{:S(2)}) %all-to-all-start) | async-done | bytes 1572896 | tf_op jit(solution)/shard_map/all_to_all | solution.py:410
  40.2 0.0 copy-done.1
  40.2 0.4 gather.1
  40.6 2.6 %collective-permute-start = (bf16[2,32,1536]{2,1,0:T(8,128)(2,1)S(1)}, bf16[2,32,1536]{2,1,0:T(8,128)(2,1)S(1)}, u32[]{:S(2)}, u32[]{:S(2)}) collective-permute-start(bf16[2,32,1536]{2,1,0:T(8,128)(2,1)S(1)} %get-tuple-element.21), channel_id=1, source_target_pairs={{0,16},{2,18},{4,20},{6,22},{8,24},{10,26},{12,28},{14,30},{16,0},... | collective-permute-start | bytes 589832 | tf_op jit(solution)/shard_map/ppermute | solution.py:430
  43.2 8.4 %collective-permute-done.refs_2_ = bf16[2,32,1536]{2,1,0:T(8,128)(2,1)S(1)} collective-permute-done((bf16[2,32,1536]{2,1,0:T(8,128)(2,1)S(1)}, bf16[2,32,1536]{2,1,0:T(8,128)(2,1)S(1)}, u32[]{:S(2)}, u32[]{:S(2)}) %collective-permute-start) | collective-permute-done | bytes 196640 | tf_op jit(solution)/shard_map/ppermute | solution.py:430
  51.6 0.0 copy-done
  51.6 0.4 scatter.1
  52.0 25.3 %all_to_all.20 = bf16[16,32,1536]{2,1,0:T(8,128)(2,1)S(1)} all-to-all(bf16[16,32,1536]{2,1,0:T(8,128)(2,1)S(1)} %bitcast.9), channel_id=1, replica_groups={{0,1,2,3,4,5,6,7,8,9,10,11,12,13,14,15},{16,17,18,19,20,21,22,23,24,25,..., dimensions={0} | all-to-all | bytes 3145728 | tf_op jit(solution)/shard_map/all_to_all | solution.py:440
  77.3 9.1 %backward.1 = (f32[16,32,768]{2,1,0:T(8,128)S(1)}, bf16[16,32,768]{2,1,0:T(8,128)(2,1)S(1)}) custom-call(bf16[512,1536]{1,0:T(8,128)(2,1)S(1)} %bitcast.8, bf16[8,1536,768]{2,1,0:T(8,128)(2,1)} %separate.1.refs_1_), custom_call_target="tpu_custom_call" | custom-call | flops 1207959552 | bytes 18874368 | tf_op jit(solution)/shard_map/backward/pallas_call | solution.py:443
  86.4 0.5 collective-permute-start.1
  86.9 1.9 %collective-permute-done.1 = bf16[16,32,768]{2,1,0:T(8,128)(2,1)S(1)} collective-permute-done((bf16[16,32,768]{2,1,0:T(8,128)(2,1)S(1)}, bf16[16,32,768]{2,1,0:T(8,128)(2,1)S(1)}, u32[]{:S(2)}, u32[]{:S(2)}) %collective-permute-start.1) | collective-permute-done | bytes 786464 | tf_op jit(solution)/shard_map/ppermute | solution.py:461
  88.8 0.2 add_convert_fusion
  89.1 14.6 %all_to_all.21 = bf16[16,32,768]{2,1,0:T(8,128)(2,1)S(1)} all-to-all(bf16[16,32,768]{2,1,0:T(8,128)(2,1)S(1)} %add_convert_fusion), channel_id=1, replica_groups={{0,4,8,12},{2,6,10,14},{16,20,24,28},{18,22,26,30},{1,5,9,13},{3,7,11,1..., dimensions={0} | all-to-all | bytes 1572864 | tf_op jit(solution)/shard_map/all_to_all | solution.py:464
  103.6 0.1 join.1
  103.7 2.5 %collective-permute-start.2 = (bf16[2,32,768]{2,1,0:T(8,128)(2,1)S(1)}, bf16[2,32,768]{2,1,0:T(8,128)(2,1)S(1)}, u32[]{:S(2)}, u32[]{:S(2)}) collective-permute-start(bf16[2,32,768]{2,1,0:T(8,128)(2,1)S(1)} %get-tuple-element.26), channel_id=1, source_target_pairs={{0,16},{2,18},{4,20},{6,22},{8,24},{10,26},{12,28},{14,30},{16,0},... | collective-permute-start | bytes 294920 | tf_op jit(solution)/shard_map/ppermute | solution.py:477
  106.2 4.1 %collective-permute-done.2.got_ref = bf16[2,32,768]{2,1,0:T(8,128)(2,1)S(1)} collective-permute-done((bf16[2,32,768]{2,1,0:T(8,128)(2,1)S(1)}, bf16[2,32,768]{2,1,0:T(8,128)(2,1)S(1)}, u32[]{:S(2)}, u32[]{:S(2)}) %collective-permute-start.2) | collective-permute-done | bytes 98336 | tf_op jit(solution)/shard_map/ppermute | solution.py:477
  110.4 0.4 gram.1
  110.8 12.7 %all_to_all.22.refs_0_ = f32[32,8,128]{2,1,0:T(8,128)S(1)} all-to-all(f32[32,8,128]{2,1,0:T(8,128)S(1)} %get-tuple-element.27), channel_id=1, replica_groups=mesh['row'=16,'col'=2] {'row','col'}, dimensions={0} | all-to-all | bytes 262144 | tf_op jit(solution)/shard_map/all_to_all | solution.py:490
  123.4 4.6 %last.1 = f32[2,32,768]{2,1,0:T(8,128)} custom-call(f32[32,8,128]{2,1,0:T(8,128)S(1)} %all_to_all.22.refs_0_, f32[2,32,768]{2,1,0:T(8,128)S(1)} %get-tuple-element.28.refs_1_), custom_call_target="tpu_custom_call" | custom-call | tf_op jit(solution)/shard_map/last/pallas_call | solution.py:491
Async XLA Ops:
  0.0 0.7 copy-start.2
  13.0 27.2 %all-to-all-start = ((bf16[16,32,1536]{2,1,0:T(8,128)(2,1)}), bf16[16,32,1536]{2,1,0:T(8,128)(2,1)S(1)}, u32[]{:S(2)}, u32[]{:S(2)}) async-start(bf16[16,32,1536]{2,1,0:T(8,128)(2,1)} %bitcast.1), calls=%async_computation | async-start | bytes 3145728 | tf_op jit(solution)/shard_map/all_to_all | solution.py:410
  19.3 20.9 %copy-start.1 = (bf16[2,64,256]{2,1,0:T(8,128)(2,1)S(1)}, bf16[2,64,256]{2,1,0:T(8,128)(2,1)}, u32[]{:S(2)}) copy-start(bf16[2,64,256]{2,1,0:T(8,128)(2,1)} %constant.4.clone.refs_0_) | copy-start | bytes 196612
  36.3 15.3 %copy-start = (bf16[2,128,96]{2,1,0:T(8,128)(2,1)S(1)}, bf16[2,128,96]{2,1,0:T(8,128)(2,1)}, u32[]{:S(2)}) copy-start(bf16[2,128,96]{2,1,0:T(8,128)(2,1)} %constant.5.clone.refs_0_) | copy-start | bytes 147460
  40.6 11.0 %collective-permute-start = (bf16[2,32,1536]{2,1,0:T(8,128)(2,1)S(1)}, bf16[2,32,1536]{2,1,0:T(8,128)(2,1)S(1)}, u32[]{:S(2)}, u32[]{:S(2)}) collective-permute-start(bf16[2,32,1536]{2,1,0:T(8,128)(2,1)S(1)} %get-tuple-element.21), channel_id=1, source_target_pairs={{0,16},{2,18},{4,20},{6,22},{8,24},{10,26},{12,28},{14,30},{16,0},... | collective-permute-start | bytes 589832 | tf_op jit(solution)/shard_map/ppermute | solution.py:430
  86.4 2.4 %collective-permute-start.1 = (bf16[16,32,768]{2,1,0:T(8,128)(2,1)S(1)}, bf16[16,32,768]{2,1,0:T(8,128)(2,1)S(1)}, u32[]{:S(2)}, u32[]{:S(2)}) collective-permute-start(bf16[16,32,768]{2,1,0:T(8,128)(2,1)S(1)} %get-tuple-element.24), channel_id=1, source_target_pairs={{0,2},{2,0},{4,6},{6,4},{8,10},{10,8},{12,14},{14,12},{16,18},{18,... | collective-permute-start | bytes 2359304 | tf_op jit(solution)/shard_map/ppermute | solution.py:461
  103.7 6.6 %collective-permute-start.2 = (bf16[2,32,768]{2,1,0:T(8,128)(2,1)S(1)}, bf16[2,32,768]{2,1,0:T(8,128)(2,1)S(1)}, u32[]{:S(2)}, u32[]{:S(2)}) collective-permute-start(bf16[2,32,768]{2,1,0:T(8,128)(2,1)S(1)} %get-tuple-element.26), channel_id=1, source_target_pairs={{0,16},{2,18},{4,20},{6,22},{8,24},{10,26},{12,28},{14,30},{16,0},... | collective-permute-start | bytes 294920 | tf_op jit(solution)/shard_map/ppermute | solution.py:477

commit v7 on v6

--- a/solution.py
+++ b/solution.py
@@ -103,14 +103,16 @@
     width, lane_w = by_freq.shape[3], acc.shape[3]
     passes, per_pass = m // width, width // lane_w
 
+    n_parts = sems.shape[1]
+
     def copy(b, i):
-        part = (slice(b * rows, (b + 1) * rows), slice(i * width, (i + 1) * width))
+        part = (slice(b * rows, (b + 1) * rows), slice(i * m // n_parts, (i + 1) * m // n_parts))
         return pltpu.make_async_copy(d_ref.at[part], held.at[b, :, part[1]], sems.at[b, i])
 
     fetch = pltpu.make_async_copy(seeds_ref, own, sem)
     fetch.start()
     for b in range(n_chunks):
-        for i in range(passes):
+        for i in range(n_parts):
             copy(b, i).start()
 
     row, col = iotas(channels, n_blocks)
@@ -171,7 +173,8 @@
     make_channels(0)
     for b in range(n_chunks):
         for i in range(passes):
-            copy(b, i).wait()
+            if i * n_parts % passes == 0:
+                copy(b, i * n_parts // passes).wait()
             if b + 1 < n_chunks:
                 for span in spans[len(spans) * i // passes : len(spans) * (i + 1) // passes]:
                     make_probes(b + 1, span)
@@ -198,17 +201,6 @@
             make_channels(b + 1)
 
 
-def separate_kernel(local, d_ref, o_ref):
-    rows, m = d_ref.shape
-    width = 256 if m % 256 == 0 else m
-    for i in range(0, m, width):
-        parts = [
-            separate(d_ref[c : c + 16 * local, i : i + width], local) for c in range(0, rows, 16 * local)
-        ]
-        for k in range(local):
-            o_ref[k, i : i + width, :] = jnp.concatenate([x[k] for x in parts], axis=0).T
-
-
 def half_of(n_row):
     return lax.axis_index("row") // (n_row // 2)
 
@@ -245,17 +237,22 @@
     send_ref[...] = total[1].astype(BF16)
 
 
-def backward_kernel(local, n_row, n_blocks, amp, f_ref, d_ref, keep_ref, send_ref, held, f_by, k_parts, sems):
-    n_chunks, _, m, block_c = held.shape
+def backward_kernel(local, n_row, n_blocks, amp, f_ref, d_ref, keep_ref, send_ref, held, by_freq, sums, f_by, k_parts, sems):
+    n_chunks, tall, m = held.shape
+    block_c = tall // local
+    width = 256 if m % 256 == 0 else m
     rows = f_ref.shape[0] // 4
     channels = 2 * local
 
-    def copy(b):
-        at = pl.ds(pl.multiple_of(b * block_c, block_c), block_c) if n_chunks > 1 else slice(None)
-        return pltpu.make_async_copy(d_ref.at[:, :, at], held.at[b], sems.at[b])
+    n_parts = sems.shape[1]
+
+    def copy(b, i):
+        at = pl.ds(i * m // n_parts, m // n_parts)
+        return pltpu.make_async_copy(d_ref.at[pl.ds(b * tall, tall), at], held.at[b, :, at], sems.at[b, i])
 
     for b in range(n_chunks):
-        copy(b).start()
+        for i in range(n_parts):
+            copy(b, i).start()
 
     row_at = lax.axis_index("row")
     half, per_owner, quarter = n_blocks // 2, n_blocks // n_row, n_row // 4
@@ -281,9 +278,19 @@
 
     @pl.loop(0, n_chunks)
     def _(b):
-        copy(b).wait()
         at = pl.ds(pl.multiple_of(b * block_c, block_c), block_c) if n_chunks > 1 else slice(None)
-        u = [jnp.dot(f_by[k], held[b, k], preferred_element_type=F32).astype(BF16) for k in range(local)]
+        for i in range(0, m, width):
+            if i * n_parts % m == 0:
+                copy(b, i * n_parts // m).wait()
+            for c in range(0, block_c, 16):
+                piece = held[b, c * local : (c + 16) * local, i : i + width]
+                by_freq[:, c : c + 16, i : i + width] = separate(piece, local)
+            for k in range(local):
+                part = lax.dot_general(
+                    f_by[k, :, i : i + width], by_freq[k, :, i : i + width], NT, preferred_element_type=F32
+                )
+                sums[k] = part if i == 0 else sums[k] + part
+        u = [sums[k].astype(BF16) for k in range(local)]
         for g in range(2):
             block = jnp.concatenate([x[g * 32 : g * 32 + 32] for x in u], axis=0)
             out = jnp.dot(k_parts[0], block, preferred_element_type=F32) + jnp.dot(
@@ -346,12 +353,13 @@
     channels = 2 * local
     n_dev = n_row * n_col
     amp = math.sqrt(2.0 / n_freq) / math.sqrt(n_blocks * m)
-    most, large, params = (pltpu.CompilerParams(vmem_limit_bytes=x << 20) for x in (54, 40, 20))
+    large, params = (pltpu.CompilerParams(vmem_limit_bytes=x << 20) for x in (40, 20))
 
     block_c = 256 if cols % 256 == 0 else cols
     lanes_c = 128 if block_c % 128 == 0 else block_c
     lane_w = 128 if m % 128 == 0 else m
     per_pass = 2 if m % (2 * lane_w) == 0 else 1
+    halves_m = 2 if m % (4 * lane_w) == 0 else 1
     flat = damping.reshape(cols * local, m)
 
     w_row = channel_table(n_freq, np.arange(n_freq), np.arange(n_blocks), n_blocks)
@@ -379,25 +387,14 @@
             pltpu.VMEM((2, channels * 8, 8 * n_blocks), BF16),
             pltpu.VMEM((2, local, 2 * P_SIZE, block_c), BF16),
             pltpu.SMEM((n_blocks,), jnp.int32),
-            pltpu.SemaphoreType.DMA((cols // block_c, m // (per_pass * lane_w))),
+            pltpu.SemaphoreType.DMA((cols // block_c, halves_m)),
             pltpu.SemaphoreType.DMA,
         ],
         compiler_params=large,
         cost_estimate=pl.CostEstimate(flops=64 * work, bytes_accessed=work, transcendentals=0),
         name="forward",
     )(block_seeds, flat)
-    t, flat = lax.optimization_barrier((t, flat))
-    block_s = 128 if cols % 128 == 0 else cols
-    by_freq = pl.pallas_call(
-        lambda *refs: separate_kernel(local, *refs),
-        grid=(cols // block_s,),
-        out_shape=jax.ShapeDtypeStruct((local, m, cols), BF16),
-        in_specs=[pl.BlockSpec((block_s * local, m), lambda i: (i, 0))],
-        out_specs=pl.BlockSpec((local, m, block_s), lambda i: (0, 0, i)),
-        compiler_params=most,
-        cost_estimate=pl.CostEstimate(flops=work, bytes_accessed=2 * work, transcendentals=0),
-        name="separate",
-    )(flat)
+    block_s = 256 if cols % 256 == 0 else cols
 
     n_grp = n_dev // 2
     n_p = math.gcd(P_SIZE, n_grp)
@@ -408,7 +405,6 @@
     t = t.reshape(n_p, p_own * channels, n_r, lanes).transpose(0, 2, 1, 3)
     t = t.reshape(n_grp, p_own * channels, lanes)
     t = lax.all_to_all(t, ("row", "col"), 0, 0, axis_index_groups=halves, tiled=True)
-    t, by_freq = lax.optimization_barrier((t, by_freq))
     t = t.reshape(n_grp, p_own, channels, lanes)
 
     merge = (w_row * sign).reshape(2, n_row // 2, 1, channels, n_blocks).repeat(n_col, axis=2)
@@ -449,15 +445,17 @@
         in_specs=vmem(1) + [pl.BlockSpec(memory_space=pl.ANY)],
         out_specs=tuple(vmem(2)),
         scratch_shapes=[
-            pltpu.VMEM((cols // block_s, local, m, block_s), BF16),
+            pltpu.VMEM((cols // block_s, block_s * local, m), BF16),
+            pltpu.VMEM((local, block_s, m), BF16),
+            pltpu.VMEM((local, 2 * P_SIZE, block_s), F32),
             pltpu.VMEM((local, 2 * P_SIZE, m), BF16),
             pltpu.VMEM((2, n_blocks * 16, channels * 16), BF16),
-            pltpu.SemaphoreType.DMA((cols // block_s,)),
+            pltpu.SemaphoreType.DMA((cols // block_s, halves_m)),
         ],
         compiler_params=large,
         cost_estimate=pl.CostEstimate(flops=64 * work, bytes_accessed=work, transcendentals=0),
         name="backward",
-    )(f, by_freq)
+    )(f, flat)
     got = lax.ppermute(send, "row", [(i, i ^ 1) for i in range(n_row)])
     summed = (keep + got.astype(F32)).astype(BF16)
     groups = [[core + 2 * (i + quarter * h) for i in range(quarter)] for h in range(2) for core in range(2)]

time: 128 us -> 127 us (level)
  blocking collectives: 52.5 us -> 77 us
  Pallas kernels: 44.2 us -> 27.3 us
  starting transfers between devices: 12 us -> 5.86 us
  waiting for transfers between devices: 18.3 us -> 15.7 us
    all_to_all x0 -> x1, blocking collectives: none -> 26.6 us  [shards(): lax.all_to_all(t, ('row', 'col'), 0, 0, axis_index_groups=halves, tiled=T...]
    pallas_call x1 -> x0, Pallas kernels: 17 us -> none  [shards(): pl.pallas_call(lambda *refs: separate_kernel(local, *refs), grid=(cols //...]
    all_to_all x1 -> x0, starting transfers between devices: 6.32 us -> none  [shards(): lax.all_to_all(t, ('row', 'col'), 0, 0, axis_index_groups=halves, tiled=T...]
    all_to_all x1 -> x0, waiting for transfers between devices: 3.87 us -> none  [shards(): lax.all_to_all(t, ('row', 'col'), 0, 0, axis_index_groups=halves, tiled=T...]
    all_to_all x1, blocking collectives: 25.3 us -> 23 us  [shards(): lax.all_to_all(f, ('row', 'col'), 0, 0, axis_index_groups=halves, tiled=T...]
    pallas_call x1, Pallas kernels: 9.11 us -> 10.9 us  [shards(): pl.pallas_call(lambda *refs: backward_kernel(local, n_row, n_blocks, amp,...]
    pallas_call x1, Pallas kernels: 12.3 us -> 10.6 us  [shards(): pl.pallas_call(lambda *refs: forward_kernel(local, n_freq, *refs), out_sh...]
  transfers between devices with their start and end apart: 4 -> 3, of which waited for: 4 -> 3; matrix products, arithmetic and copies ran while one was open for 0% -> 0% of each run, Pallas kernels for 13% -> 0%
where the time goes in v7:
time: 127 us
  blocking collectives  77 us (61%)
  Pallas kernels  27.3 us (21%)
  waiting for transfers between devices  15.7 us (12%)
  starting transfers between devices  5.86 us (5%)
    all_to_all x1, blocking collectives, shards(): lax.all_to_all(t, ('row', 'col'), 0, 0, axis_index_groups=halves, tiled=T...  26.6 us
    all_to_all x1, blocking collectives, shards(): lax.all_to_all(f, ('row', 'col'), 0, 0, axis_index_groups=halves, tiled=T...  23 us
    all_to_all x1, blocking collectives, shards(): lax.all_to_all(summed, 'row', 0, 0, axis_index_groups=groups, tiled=True)  14.6 us
    ppermute x2, waiting for transfers between devices, shards(): got = lax.ppermute(send, 'row', across)  13.7 us
    all_to_all x1, blocking collectives, shards(): gram = lax.all_to_all(gram, ('row', 'col'), 0, 0, tiled=True)  12.9 us
    pallas_call x1, Pallas kernels, shards(): pl.pallas_call(lambda *refs: backward_kernel(local, n_row, n_blocks, amp,...  10.9 us
    pallas_call x1, Pallas kernels, shards(): pl.pallas_call(lambda *refs: forward_kernel(local, n_freq, *refs), out_sh...  10.6 us
    ppermute x2, starting transfers between devices, shards(): got = lax.ppermute(send, 'row', across)  5.35 us
  transfers between devices with their start and end apart: 3, of which 3 were waited for; matrix products, arithmetic and copies ran while one was open for 0% of the time, Pallas kernels for 0%

profile of v7, /device:TPU:0, one launch (start us, length us, event | category | flops | bytes accessed | tf_op | source)
XLA Modules:
  0.0 126.8 jit_solution(10857199006547778344)
XLA Ops:
  0.0 0.0 copy-start.2
  0.0 0.7 copy-done.2
  0.7 10.6 %forward.1 = bf16[32,16,1536]{2,1,0:T(8,128)(2,1)S(1)} custom-call(s32[32]{0:T(128)S(1)} %copy-done.2, bf16[6144,1536]{1,0:T(8,128)(2,1)} %bitcast.12), custom_call_target="tpu_custom_call" | custom-call | flops 1207959552 | bytes 18874368 | tf_op jit(solution)/shard_map/forward/pallas_call | solution.py:374
  11.2 0.0 copy-start.1
  11.3 26.6 %all_to_all.20 = bf16[16,32,1536]{2,1,0:T(8,128)(2,1)S(1)} all-to-all(bf16[16,32,1536]{2,1,0:T(8,128)(2,1)S(1)} %bitcast.10), channel_id=1, replica_groups={{0,1,2,3,4,5,6,7,8,9,10,11,12,13,14,15},{16,17,18,19,20,21,22,23,24,25,..., dimensions={0} | all-to-all | bytes 3145728 | tf_op jit(solution)/shard_map/all_to_all | solution.py:407
  37.9 0.0 copy-start
  37.9 0.0 copy-done.1
  37.9 0.4 gather.1
  38.3 2.6 %collective-permute-start = (bf16[2,32,1536]{2,1,0:T(8,128)(2,1)S(1)}, bf16[2,32,1536]{2,1,0:T(8,128)(2,1)S(1)}, u32[]{:S(2)}, u32[]{:S(2)}) collective-permute-start(bf16[2,32,1536]{2,1,0:T(8,128)(2,1)S(1)} %get-tuple-element.14), channel_id=1, source_target_pairs={{0,16},{2,18},{4,20},{6,22},{8,24},{10,26},{12,28},{14,30},{16,0},... | collective-permute-start | bytes 589832 | tf_op jit(solution)/shard_map/ppermute | solution.py:426
  40.9 9.8 %collective-permute-done.refs_2_ = bf16[2,32,1536]{2,1,0:T(8,128)(2,1)S(1)} collective-permute-done((bf16[2,32,1536]{2,1,0:T(8,128)(2,1)S(1)}, bf16[2,32,1536]{2,1,0:T(8,128)(2,1)S(1)}, u32[]{:S(2)}, u32[]{:S(2)}) %collective-permute-start) | collective-permute-done | bytes 196640 | tf_op jit(solution)/shard_map/ppermute | solution.py:426
  50.7 0.0 copy-done
  50.7 0.4 scatter.1
  51.0 23.0 %all_to_all.21 = bf16[16,32,1536]{2,1,0:T(8,128)(2,1)S(1)} all-to-all(bf16[16,32,1536]{2,1,0:T(8,128)(2,1)S(1)} %bitcast.8), channel_id=1, replica_groups={{0,1,2,3,4,5,6,7,8,9,10,11,12,13,14,15},{16,17,18,19,20,21,22,23,24,25,..., dimensions={0} | all-to-all | bytes 3145728 | tf_op jit(solution)/shard_map/all_to_all | solution.py:436
  74.0 10.9 %backward.1 = (f32[16,32,768]{2,1,0:T(8,128)S(1)}, bf16[16,32,768]{2,1,0:T(8,128)(2,1)S(1)}) custom-call(bf16[512,1536]{1,0:T(8,128)(2,1)S(1)} %bitcast.9, bf16[6144,1536]{1,0:T(8,128)(2,1)} %bitcast.13), custom_call_target="tpu_custom_call" | custom-call | flops 1207959552 | bytes 18874368 | tf_op jit(solution)/shard_map/backward/pallas_call | solution.py:439
  85.0 0.5 collective-permute-start.1
  85.5 1.9 %collective-permute-done.1 = bf16[16,32,768]{2,1,0:T(8,128)(2,1)S(1)} collective-permute-done((bf16[16,32,768]{2,1,0:T(8,128)(2,1)S(1)}, bf16[16,32,768]{2,1,0:T(8,128)(2,1)S(1)}, u32[]{:S(2)}, u32[]{:S(2)}) %collective-permute-start.1) | collective-permute-done | bytes 786464 | tf_op jit(solution)/shard_map/ppermute | solution.py:459
  87.4 0.2 add_convert_fusion
  87.6 14.6 %all_to_all.22 = bf16[16,32,768]{2,1,0:T(8,128)(2,1)S(1)} all-to-all(bf16[16,32,768]{2,1,0:T(8,128)(2,1)S(1)} %add_convert_fusion), channel_id=1, replica_groups={{0,4,8,12},{2,6,10,14},{16,20,24,28},{18,22,26,30},{1,5,9,13},{3,7,11,1..., dimensions={0} | all-to-all | bytes 1572864 | tf_op jit(solution)/shard_map/all_to_all | solution.py:462
  102.2 0.1 join.1
  102.3 2.7 %collective-permute-start.2 = (bf16[2,32,768]{2,1,0:T(8,128)(2,1)S(1)}, bf16[2,32,768]{2,1,0:T(8,128)(2,1)S(1)}, u32[]{:S(2)}, u32[]{:S(2)}) collective-permute-start(bf16[2,32,768]{2,1,0:T(8,128)(2,1)S(1)} %get-tuple-element.18), channel_id=1, source_target_pairs={{0,16},{2,18},{4,20},{6,22},{8,24},{10,26},{12,28},{14,30},{16,0},... | collective-permute-start | bytes 294920 | tf_op jit(solution)/shard_map/ppermute | solution.py:475
  105.0 3.9 %collective-permute-done.2.got_ref = bf16[2,32,768]{2,1,0:T(8,128)(2,1)S(1)} collective-permute-done((bf16[2,32,768]{2,1,0:T(8,128)(2,1)S(1)}, bf16[2,32,768]{2,1,0:T(8,128)(2,1)S(1)}, u32[]{:S(2)}, u32[]{:S(2)}) %collective-permute-start.2) | collective-permute-done | bytes 98336 | tf_op jit(solution)/shard_map/ppermute | solution.py:475
  109.0 0.4 gram.1
  109.4 12.9 %all_to_all.23.refs_0_ = f32[32,8,128]{2,1,0:T(8,128)S(1)} all-to-all(f32[32,8,128]{2,1,0:T(8,128)S(1)} %get-tuple-element.19), channel_id=1, replica_groups=mesh['row'=16,'col'=2] {'row','col'}, dimensions={0} | all-to-all | bytes 262144 | tf_op jit(solution)/shard_map/all_to_all | solution.py:488
  122.2 4.6 %last.1 = f32[2,32,768]{2,1,0:T(8,128)} custom-call(f32[32,8,128]{2,1,0:T(8,128)S(1)} %all_to_all.23.refs_0_, f32[2,32,768]{2,1,0:T(8,128)S(1)} %get-tuple-element.20.refs_1_), custom_call_target="tpu_custom_call" | custom-call | tf_op jit(solution)/shard_map/last/pallas_call | solution.py:489
Async XLA Ops:
  0.0 0.7 copy-start.2
  11.2 26.6 %copy-start.1 = (bf16[2,64,256]{2,1,0:T(8,128)(2,1)S(1)}, bf16[2,64,256]{2,1,0:T(8,128)(2,1)}, u32[]{:S(2)}) copy-start(bf16[2,64,256]{2,1,0:T(8,128)(2,1)} %constant.4.clone.refs_0_) | copy-start | bytes 196612
  37.9 12.8 %copy-start = (bf16[2,128,96]{2,1,0:T(8,128)(2,1)S(1)}, bf16[2,128,96]{2,1,0:T(8,128)(2,1)}, u32[]{:S(2)}) copy-start(bf16[2,128,96]{2,1,0:T(8,128)(2,1)} %constant.5.clone.refs_0_) | copy-start | bytes 147460
  38.3 12.4 %collective-permute-start = (bf16[2,32,1536]{2,1,0:T(8,128)(2,1)S(1)}, bf16[2,32,1536]{2,1,0:T(8,128)(2,1)S(1)}, u32[]{:S(2)}, u32[]{:S(2)}) collective-permute-start(bf16[2,32,1536]{2,1,0:T(8,128)(2,1)S(1)} %get-tuple-element.14), channel_id=1, source_target_pairs={{0,16},{2,18},{4,20},{6,22},{8,24},{10,26},{12,28},{14,30},{16,0},... | collective-permute-start | bytes 589832 | tf_op jit(solution)/shard_map/ppermute | solution.py:426
  85.0 2.4 %collective-permute-start.1 = (bf16[16,32,768]{2,1,0:T(8,128)(2,1)S(1)}, bf16[16,32,768]{2,1,0:T(8,128)(2,1)S(1)}, u32[]{:S(2)}, u32[]{:S(2)}) collective-permute-start(bf16[16,32,768]{2,1,0:T(8,128)(2,1)S(1)} %get-tuple-element.16), channel_id=1, source_target_pairs={{0,2},{2,0},{4,6},{6,4},{8,10},{10,8},{12,14},{14,12},{16,18},{18,... | collective-permute-start | bytes 2359304 | tf_op jit(solution)/shard_map/ppermute | solution.py:459
  102.3 6.7 %collective-permute-start.2 = (bf16[2,32,768]{2,1,0:T(8,128)(2,1)S(1)}, bf16[2,32,768]{2,1,0:T(8,128)(2,1)S(1)}, u32[]{:S(2)}, u32[]{:S(2)}) collective-permute-start(bf16[2,32,768]{2,1,0:T(8,128)(2,1)S(1)} %get-tuple-element.18), channel_id=1, source_target_pairs={{0,16},{2,18},{4,20},{6,22},{8,24},{10,26},{12,28},{14,30},{16,0},... | collective-permute-start | bytes 294920 | tf_op jit(solution)/shard_map/ppermute | solution.py:475

commit v8 on v7

--- a/solution.py
+++ b/solution.py
@@ -237,23 +237,8 @@
     send_ref[...] = total[1].astype(BF16)
 
 
-def backward_kernel(local, n_row, n_blocks, amp, f_ref, d_ref, keep_ref, send_ref, held, by_freq, sums, f_by, k_parts, sems):
-    n_chunks, tall, m = held.shape
-    block_c = tall // local
-    width = 256 if m % 256 == 0 else m
-    rows = f_ref.shape[0] // 4
+def blocks_kernel(local, n_row, n_blocks, amp, k_ref):
     channels = 2 * local
-
-    n_parts = sems.shape[1]
-
-    def copy(b, i):
-        at = pl.ds(i * m // n_parts, m // n_parts)
-        return pltpu.make_async_copy(d_ref.at[pl.ds(b * tall, tall), at], held.at[b, :, at], sems.at[b, i])
-
-    for b in range(n_chunks):
-        for i in range(n_parts):
-            copy(b, i).start()
-
     row_at = lax.axis_index("row")
     half, per_owner, quarter = n_blocks // 2, n_blocks // n_row, n_row // 4
     r, c = iotas(n_blocks, channels)
@@ -268,7 +253,39 @@
     same = place(n_blocks * 16, channels * 16, lambda r, c: r % 16 == c // 16 % 2 * 8 + c % 8)
     for part, k in enumerate(split(table)):
         k = jnp.dot(left, jnp.dot(k, right, preferred_element_type=F32), preferred_element_type=F32)
-        k_parts[part] = (k * same).astype(BF16)
+        k_ref[part] = (k * same).astype(BF16)
+
+
+def separate_kernel(local, d_ref, o_ref):
+    rows, m = d_ref.shape
+    for i in range(0, m, 256):
+        for c in range(0, rows // local, 16):
+            piece = d_ref[c * local : (c + 16) * local, i : i + 256]
+            o_ref[:, c : c + 16, i : i + 256] = separate(piece, local)
+
+
+def backward_kernel(local, n_blocks, n_ready, f_ref, k_ref, d_ref, *refs):
+    ready_ref = refs[0] if n_ready else None
+    keep_ref, send_ref, raw, held, sums, f_by, k_parts, sems, sem = refs[bool(n_ready) :]
+    n_chunks, _, block_c, m = held.shape
+    n_parts = sems.shape[1]
+    width = m // n_parts
+    tall = block_c * local
+    rows = f_ref.shape[0] // 4
+    half = n_blocks // 2
+
+    def copy(b, i):
+        at = slice(i * width, (i + 1) * width)
+        if b == 0:
+            return pltpu.make_async_copy(d_ref.at[pl.ds(0, tall), at], raw.at[:, at], sems.at[b, i])
+        source = ready_ref.at[:, pl.ds((b - 1) * block_c, block_c), at]
+        return pltpu.make_async_copy(source, held.at[b, :, :, at], sems.at[b, i])
+
+    tables = pltpu.make_async_copy(k_ref, k_parts, sem)
+    for i in range(n_parts):
+        for b in range(n_chunks):
+            copy(b, i).start()
+    tables.start()
 
     swap = place(rows, rows, lambda r, c: (r % 8 * 2 + r // 8 % 2) * local + r // 16 == c).astype(BF16)
     for g in range(4):
@@ -276,21 +293,21 @@
         for k in range(local):
             f_by[k, g * 16 : g * 16 + 16, :] = out[k * 16 : k * 16 + 16]
 
-    @pl.loop(0, n_chunks)
-    def _(b):
-        at = pl.ds(pl.multiple_of(b * block_c, block_c), block_c) if n_chunks > 1 else slice(None)
-        for i in range(0, m, width):
-            if i * n_parts % m == 0:
-                copy(b, i * n_parts // m).wait()
-            for c in range(0, block_c, 16):
-                piece = held[b, c * local : (c + 16) * local, i : i + width]
-                by_freq[:, c : c + 16, i : i + width] = separate(piece, local)
+    for i in range(n_parts):
+        at = slice(i * width, (i + 1) * width)
+        for b in range(n_chunks):
+            copy(b, i).wait()
+        for c in range(0, block_c, 16):
+            held[0, :, c : c + 16, at] = separate(raw[c * local : (c + 16) * local, at], local)
+        for b in (*range(1, n_chunks), 0):
             for k in range(local):
-                part = lax.dot_general(
-                    f_by[k, :, i : i + width], by_freq[k, :, i : i + width], NT, preferred_element_type=F32
-                )
-                sums[k] = part if i == 0 else sums[k] + part
-        u = [sums[k].astype(BF16) for k in range(local)]
+                part = lax.dot_general(f_by[k, :, at], held[b, k, :, at], NT, preferred_element_type=F32)
+                sums[b, k] = part if i == 0 else sums[b, k] + part
+
+    tables.wait()
+    for b in range(n_chunks):
+        at = slice(b * block_c, (b + 1) * block_c)
+        u = [sums[b, k].astype(BF16) for k in range(local)]
         for g in range(2):
             block = jnp.concatenate([x[g * 32 : g * 32 + 32] for x in u], axis=0)
             out = jnp.dot(k_parts[0], block, preferred_element_type=F32) + jnp.dot(
@@ -353,7 +370,7 @@
     channels = 2 * local
     n_dev = n_row * n_col
     amp = math.sqrt(2.0 / n_freq) / math.sqrt(n_blocks * m)
-    large, params = (pltpu.CompilerParams(vmem_limit_bytes=x << 20) for x in (40, 20))
+    most, large, params = (pltpu.CompilerParams(vmem_limit_bytes=x << 20) for x in (54, 44, 20))
 
     block_c = 256 if cols % 256 == 0 else cols
     lanes_c = 128 if block_c % 128 == 0 else block_c
@@ -394,8 +411,6 @@
         cost_estimate=pl.CostEstimate(flops=64 * work, bytes_accessed=work, transcendentals=0),
         name="forward",
     )(block_seeds, flat)
-    block_s = 256 if cols % 256 == 0 else cols
-
     n_grp = n_dev // 2
     n_p = math.gcd(P_SIZE, n_grp)
     n_r = n_grp // n_p
@@ -423,7 +438,33 @@
         compiler_params=params,
         name="gather",
     )(jnp.asarray(merge), t)
+    send, flat = lax.optimization_barrier((send, flat))
     got = lax.ppermute(send, "row", across)
+    n_ready = cols // block_c - 1 if m % 256 == 0 else 0
+    k_tables = pl.pallas_call(
+        lambda *refs: blocks_kernel(local, n_row, n_blocks, amp, *refs),
+        out_shape=jax.ShapeDtypeStruct((2, n_blocks * 16, channels * 16), BF16),
+        in_specs=[],
+        out_specs=v_one,
+        compiler_params=params,
+        cost_estimate=pl.CostEstimate(flops=10**9, bytes_accessed=10**6, transcendentals=0),
+        name="blocks",
+    )()
+    ready = []
+    if n_ready:
+        ready.append(
+            pl.pallas_call(
+                lambda *refs: separate_kernel(local, *refs),
+                grid=(2 * n_ready,),
+                out_shape=jax.ShapeDtypeStruct((local, n_ready * block_c, m), BF16),
+                in_specs=[pl.BlockSpec((block_c // 2 * local, m), lambda i: (i + 2, 0))],
+                out_specs=pl.BlockSpec((local, block_c // 2, m), lambda i: (0, i, 0)),
+                compiler_params=most,
+                cost_estimate=pl.CostEstimate(flops=work, bytes_accessed=2 * work, transcendentals=0),
+                name="separate",
+            )(flat)
+        )
+    got, k_tables, *ready = lax.optimization_barrier((got, k_tables, *ready))
     f = pl.pallas_call(
         lambda *refs: scatter_kernel(n_row, *refs),
         out_shape=jax.ShapeDtypeStruct((n_row // 2, n_col, p_own, channels, lanes), BF16),
@@ -436,26 +477,30 @@
     f = lax.all_to_all(f, ("row", "col"), 0, 0, axis_index_groups=halves, tiled=True)
     f = f.reshape(n_p, n_r, p_own * channels, lanes).transpose(0, 2, 1, 3).reshape(n_rows, m)
 
+    n_parts = m // 256 if m % 256 == 0 else 1
+    n_chunks = n_ready + 1
+    deep = cols // n_chunks
     keep, send = pl.pallas_call(
-        lambda *refs: backward_kernel(local, n_row, n_blocks, amp, *refs),
+        lambda *refs: backward_kernel(local, n_blocks, n_ready, *refs),
         out_shape=(
             jax.ShapeDtypeStruct((half, P_SIZE, cols), F32),
             jax.ShapeDtypeStruct((half, P_SIZE, cols), BF16),
         ),
-        in_specs=vmem(1) + [pl.BlockSpec(memory_space=pl.ANY)],
+        in_specs=vmem(1) + [pl.BlockSpec(memory_space=pl.ANY)] * (2 + len(ready)),
         out_specs=tuple(vmem(2)),
         scratch_shapes=[
-            pltpu.VMEM((cols // block_s, block_s * local, m), BF16),
-            pltpu.VMEM((local, block_s, m), BF16),
-            pltpu.VMEM((local, 2 * P_SIZE, block_s), F32),
+            pltpu.VMEM((deep * local, m), BF16),
+            pltpu.VMEM((n_chunks, local, deep, m), BF16),
+            pltpu.VMEM((n_chunks, local, 2 * P_SIZE, deep), F32),
             pltpu.VMEM((local, 2 * P_SIZE, m), BF16),
             pltpu.VMEM((2, n_blocks * 16, channels * 16), BF16),
-            pltpu.SemaphoreType.DMA((cols // block_s, halves_m)),
+            pltpu.SemaphoreType.DMA((n_chunks, n_parts)),
+            pltpu.SemaphoreType.DMA,
         ],
         compiler_params=large,
         cost_estimate=pl.CostEstimate(flops=64 * work, bytes_accessed=work, transcendentals=0),
         name="backward",
-    )(f, flat)
+    )(f, k_tables, flat, *ready)
     got = lax.ppermute(send, "row", [(i, i ^ 1) for i in range(n_row)])
     summed = (keep + got.astype(F32)).astype(BF16)
     groups = [[core + 2 * (i + quarter * h) for i in range(quarter)] for h in range(2) for core in range(2)]

time: 127 us -> 125 us (0.984)
  Pallas kernels: 27.3 us -> 36.2 us
  waiting for transfers between devices: 15.7 us -> 7 us
    pallas_call x1 -> x3, Pallas kernels: 10.9 us -> 19.8 us  [the longest x1 10.2 us: shards(): pl.pallas_call(lambda *refs: separate_kernel(local, *refs), grid=(2 * n_r...]
    ppermute x2, waiting for transfers between devices: 13.7 us -> 5.09 us  [shards(): got = lax.ppermute(send, 'row', across)]
  transfers between devices with their start and end apart: 3 -> 3, of which waited for: 3 -> 2; matrix products, arithmetic and copies ran while one was open for 0% -> 0% of each run, Pallas kernels for 0% -> 9%
where the time goes in v8:
time: 125 us
  blocking collectives  76.2 us (61%)
  Pallas kernels  36.2 us (29%)
  waiting for transfers between devices  7 us (6%)
  starting transfers between devices  4.71 us (4%)
    all_to_all x1, blocking collectives, shards(): lax.all_to_all(t, ('row', 'col'), 0, 0, axis_index_groups=halves, tiled=T...  26.6 us
    all_to_all x1, blocking collectives, shards(): lax.all_to_all(f, ('row', 'col'), 0, 0, axis_index_groups=halves, tiled=T...  23.3 us
    all_to_all x1, blocking collectives, shards(): lax.all_to_all(summed, 'row', 0, 0, axis_index_groups=groups, tiled=True)  14.6 us
    all_to_all x1, blocking collectives, shards(): gram = lax.all_to_all(gram, ('row', 'col'), 0, 0, tiled=True)  11.7 us
    pallas_call x1, Pallas kernels, shards(): pl.pallas_call(lambda *refs: forward_kernel(local, n_freq, *refs), out_sh...  10.6 us
    pallas_call x1, Pallas kernels, shards(): pl.pallas_call(lambda *refs: separate_kernel(local, *refs), grid=(2 * n_r...  10.2 us
    pallas_call x1, Pallas kernels, shards(): pl.pallas_call(lambda *refs: backward_kernel(local, n_blocks, n_ready, *r...  9.14 us
    ppermute x2, waiting for transfers between devices, shards(): got = lax.ppermute(send, 'row', across)  5.09 us
  transfers between devices with their start and end apart: 3, of which 2 were waited for; matrix products, arithmetic and copies ran while one was open for 0% of the time, Pallas kernels for 9%

profile of v8, /device:TPU:0, one launch (start us, length us, event | category | flops | bytes accessed | tf_op | source)
XLA Modules:
  0.0 125.0 jit_solution(4819412856592512422)
XLA Ops:
  0.0 0.0 copy-start.2
  0.0 0.7 copy-done.2
  0.7 10.6 %forward.1 = bf16[32,16,1536]{2,1,0:T(8,128)(2,1)S(1)} custom-call(s32[32]{0:T(128)S(1)} %copy-done.2, bf16[6144,1536]{1,0:T(8,128)(2,1)} %bitcast.12), custom_call_target="tpu_custom_call" | custom-call | flops 1207959552 | bytes 18874368 | tf_op jit(solution)/shard_map/forward/pallas_call | solution.py:391
  11.2 0.0 copy-start.1
  11.3 26.6 %all_to_all.20 = bf16[16,32,1536]{2,1,0:T(8,128)(2,1)S(1)} all-to-all(bf16[16,32,1536]{2,1,0:T(8,128)(2,1)S(1)} %bitcast.10), channel_id=1, replica_groups={{0,1,2,3,4,5,6,7,8,9,10,11,12,13,14,15},{16,17,18,19,20,21,22,23,24,25,..., dimensions={0} | all-to-all | bytes 3145728 | tf_op jit(solution)/shard_map/all_to_all | solution.py:422
  37.9 0.0 copy-done.1
  37.9 0.4 gather.1
  38.3 2.6 %collective-permute-start = (bf16[2,32,1536]{2,1,0:T(8,128)(2,1)S(1)}, bf16[2,32,1536]{2,1,0:T(8,128)(2,1)S(1)}, u32[]{:S(2)}, u32[]{:S(2)}) collective-permute-start(bf16[2,32,1536]{2,1,0:T(8,128)(2,1)S(1)} %get-tuple-element.20), channel_id=1, source_target_pairs={{0,16},{2,18},{4,20},{6,22},{8,24},{10,26},{12,28},{14,30},{16,0},... | collective-permute-start | bytes 589832 | tf_op jit(solution)/shard_map/ppermute | solution.py:442
  40.9 0.5 blocks.1.refs_1_
  41.3 0.0 copy-start
  41.4 10.2 %separate.1.refs_3_ = bf16[8,512,1536]{2,1,0:T(8,128)(2,1)} custom-call(bf16[6144,1536]{1,0:T(8,128)(2,1)} %bitcast.13), custom_call_target="tpu_custom_call" | custom-call | flops 18874368 | bytes 37748736 | tf_op jit(solution)/shard_map/separate/pallas_call | solution.py:456
  51.6 0.0 collective-permute-done.refs_2_
  51.6 0.0 copy-done
  51.6 0.4 scatter.1
  51.9 23.3 %all_to_all.21 = bf16[16,32,1536]{2,1,0:T(8,128)(2,1)S(1)} all-to-all(bf16[16,32,1536]{2,1,0:T(8,128)(2,1)S(1)} %bitcast.9), channel_id=1, replica_groups={{0,1,2,3,4,5,6,7,8,9,10,11,12,13,14,15},{16,17,18,19,20,21,22,23,24,25,..., dimensions={0} | all-to-all | bytes 3145728 | tf_op jit(solution)/shard_map/all_to_all | solution.py:477
  75.2 9.1 %backward.1 = (f32[16,32,768]{2,1,0:T(8,128)S(1)}, bf16[16,32,768]{2,1,0:T(8,128)(2,1)S(1)}) custom-call(bf16[512,1536]{1,0:T(8,128)(2,1)S(1)} %bitcast.7, bf16[2,512,256]{2,1,0:T(8,128)(2,1)S(1)} %blocks.1.refs_1_, bf16[6144,1536]{1,0:T(8,128)(2,1)} %bitcast.14, bf16[8,512,1536]{2,1,0:T(8,128)(2,1)} %separate.1.refs_3_), custom_call_target="tpu_custom_call" | custom-call | flops 1207959552 | bytes 18874368 | tf_op jit(solution)/shard_map/backward/pallas_call | solution.py:483
  84.3 0.5 collective-permute-start.1
  84.9 1.9 %collective-permute-done.1 = bf16[16,32,768]{2,1,0:T(8,128)(2,1)S(1)} collective-permute-done((bf16[16,32,768]{2,1,0:T(8,128)(2,1)S(1)}, bf16[16,32,768]{2,1,0:T(8,128)(2,1)S(1)}, u32[]{:S(2)}, u32[]{:S(2)}) %collective-permute-start.1) | collective-permute-done | bytes 786464 | tf_op jit(solution)/shard_map/ppermute | solution.py:504
  86.8 0.2 add_convert_fusion
  87.0 14.6 %all_to_all.22 = bf16[16,32,768]{2,1,0:T(8,128)(2,1)S(1)} all-to-all(bf16[16,32,768]{2,1,0:T(8,128)(2,1)S(1)} %add_convert_fusion), channel_id=1, replica_groups={{0,4,8,12},{2,6,10,14},{16,20,24,28},{18,22,26,30},{1,5,9,13},{3,7,11,1..., dimensions={0} | all-to-all | bytes 1572864 | tf_op jit(solution)/shard_map/all_to_all | solution.py:507
  101.6 0.1 join.1
  101.7 1.6 %collective-permute-start.2 = (bf16[2,32,768]{2,1,0:T(8,128)(2,1)S(1)}, bf16[2,32,768]{2,1,0:T(8,128)(2,1)S(1)}, u32[]{:S(2)}, u32[]{:S(2)}) collective-permute-start(bf16[2,32,768]{2,1,0:T(8,128)(2,1)S(1)} %get-tuple-element.28), channel_id=1, source_target_pairs={{0,16},{2,18},{4,20},{6,22},{8,24},{10,26},{12,28},{14,30},{16,0},... | collective-permute-start | bytes 294920 | tf_op jit(solution)/shard_map/ppermute | solution.py:520
  103.2 5.1 %collective-permute-done.2.got_ref = bf16[2,32,768]{2,1,0:T(8,128)(2,1)S(1)} collective-permute-done((bf16[2,32,768]{2,1,0:T(8,128)(2,1)S(1)}, bf16[2,32,768]{2,1,0:T(8,128)(2,1)S(1)}, u32[]{:S(2)}, u32[]{:S(2)}) %collective-permute-start.2) | collective-permute-done | bytes 98336 | tf_op jit(solution)/shard_map/ppermute | solution.py:520
  108.3 0.4 gram.1
  108.7 11.7 %all_to_all.23.refs_0_ = f32[32,8,128]{2,1,0:T(8,128)S(1)} all-to-all(f32[32,8,128]{2,1,0:T(8,128)S(1)} %get-tuple-element.29), channel_id=1, replica_groups=mesh['row'=16,'col'=2] {'row','col'}, dimensions={0} | all-to-all | bytes 262144 | tf_op jit(solution)/shard_map/all_to_all | solution.py:533
  120.4 4.6 %last.1 = f32[2,32,768]{2,1,0:T(8,128)} custom-call(f32[32,8,128]{2,1,0:T(8,128)S(1)} %all_to_all.23.refs_0_, f32[2,32,768]{2,1,0:T(8,128)S(1)} %get-tuple-element.30.refs_1_), custom_call_target="tpu_custom_call" | custom-call | tf_op jit(solution)/shard_map/last/pallas_call | solution.py:534
Async XLA Ops:
  0.0 0.7 copy-start.2
  11.2 26.6 %copy-start.1 = (bf16[2,64,256]{2,1,0:T(8,128)(2,1)S(1)}, bf16[2,64,256]{2,1,0:T(8,128)(2,1)}, u32[]{:S(2)}) copy-start(bf16[2,64,256]{2,1,0:T(8,128)(2,1)} %constant.4.clone.refs_0_) | copy-start | bytes 196612
  38.3 13.3 %collective-permute-start = (bf16[2,32,1536]{2,1,0:T(8,128)(2,1)S(1)}, bf16[2,32,1536]{2,1,0:T(8,128)(2,1)S(1)}, u32[]{:S(2)}, u32[]{:S(2)}) collective-permute-start(bf16[2,32,1536]{2,1,0:T(8,128)(2,1)S(1)} %get-tuple-element.20), channel_id=1, source_target_pairs={{0,16},{2,18},{4,20},{6,22},{8,24},{10,26},{12,28},{14,30},{16,0},... | collective-permute-start | bytes 589832 | tf_op jit(solution)/shard_map/ppermute | solution.py:442
  41.3 10.2 %copy-start = (bf16[2,128,96]{2,1,0:T(8,128)(2,1)S(1)}, bf16[2,128,96]{2,1,0:T(8,128)(2,1)}, u32[]{:S(2)}) copy-start(bf16[2,128,96]{2,1,0:T(8,128)(2,1)} %constant.5.clone.refs_0_) | copy-start | bytes 147460
  84.3 2.4 %collective-permute-start.1 = (bf16[16,32,768]{2,1,0:T(8,128)(2,1)S(1)}, bf16[16,32,768]{2,1,0:T(8,128)(2,1)S(1)}, u32[]{:S(2)}, u32[]{:S(2)}) collective-permute-start(bf16[16,32,768]{2,1,0:T(8,128)(2,1)S(1)} %get-tuple-element.26), channel_id=1, source_target_pairs={{0,2},{2,0},{4,6},{6,4},{8,10},{10,8},{12,14},{14,12},{16,18},{18,... | collective-permute-start | bytes 2359304 | tf_op jit(solution)/shard_map/ppermute | solution.py:504
  101.7 6.6 %collective-permute-start.2 = (bf16[2,32,768]{2,1,0:T(8,128)(2,1)S(1)}, bf16[2,32,768]{2,1,0:T(8,128)(2,1)S(1)}, u32[]{:S(2)}, u32[]{:S(2)}) collective-permute-start(bf16[2,32,768]{2,1,0:T(8,128)(2,1)S(1)} %get-tuple-element.28), channel_id=1, source_target_pairs={{0,16},{2,18},{4,20},{6,22},{8,24},{10,26},{12,28},{14,30},{16,0},... | collective-permute-start | bytes 294920 | tf_op jit(solution)/shard_map/ppermute | solution.py:520

commit v9 on v8

--- a/solution.py
+++ b/solution.py
@@ -268,22 +268,24 @@
     ready_ref = refs[0] if n_ready else None
     keep_ref, send_ref, raw, held, sums, f_by, k_parts, sems, sem = refs[bool(n_ready) :]
     n_chunks, _, block_c, m = held.shape
-    n_parts = sems.shape[1]
+    n_raw, n_parts = n_chunks - n_ready, sems.shape[1]
     width = m // n_parts
+    step = 256 if width % 256 == 0 else width
     tall = block_c * local
     rows = f_ref.shape[0] // 4
     half = n_blocks // 2
 
     def copy(b, i):
         at = slice(i * width, (i + 1) * width)
-        if b == 0:
-            return pltpu.make_async_copy(d_ref.at[pl.ds(0, tall), at], raw.at[:, at], sems.at[b, i])
-        source = ready_ref.at[:, pl.ds((b - 1) * block_c, block_c), at]
+        if b < n_raw:
+            return pltpu.make_async_copy(d_ref.at[pl.ds(b * tall, tall), at], raw.at[b, :, at], sems.at[b, i])
+        source = ready_ref.at[:, pl.ds((b - n_raw) * block_c, block_c), at]
         return pltpu.make_async_copy(source, held.at[b, :, :, at], sems.at[b, i])
 
     tables = pltpu.make_async_copy(k_ref, k_parts, sem)
+    order = (*range(n_raw, n_chunks), *range(n_raw))
     for i in range(n_parts):
-        for b in range(n_chunks):
+        for b in order:
             copy(b, i).start()
     tables.start()
 
@@ -295,11 +297,12 @@
 
     for i in range(n_parts):
         at = slice(i * width, (i + 1) * width)
-        for b in range(n_chunks):
+        for b in order:
             copy(b, i).wait()
-        for c in range(0, block_c, 16):
-            held[0, :, c : c + 16, at] = separate(raw[c * local : (c + 16) * local, at], local)
-        for b in (*range(1, n_chunks), 0):
+            for p in range(i * width, (i + 1) * width, step) if b < n_raw else ():
+                for c in range(0, block_c, 16):
+                    piece = raw[b, c * local : (c + 16) * local, p : p + step]
+                    held[b, :, c : c + 16, p : p + step] = separate(piece, local)
             for k in range(local):
                 part = lax.dot_general(f_by[k, :, at], held[b, k, :, at], NT, preferred_element_type=F32)
                 sums[b, k] = part if i == 0 else sums[b, k] + part
@@ -370,7 +373,7 @@
     channels = 2 * local
     n_dev = n_row * n_col
     amp = math.sqrt(2.0 / n_freq) / math.sqrt(n_blocks * m)
-    most, large, params = (pltpu.CompilerParams(vmem_limit_bytes=x << 20) for x in (54, 44, 20))
+    most, large, params = (pltpu.CompilerParams(vmem_limit_bytes=x << 20) for x in (54, 46, 20))
 
     block_c = 256 if cols % 256 == 0 else cols
     lanes_c = 128 if block_c % 128 == 0 else block_c
@@ -440,7 +443,8 @@
     )(jnp.asarray(merge), t)
     send, flat = lax.optimization_barrier((send, flat))
     got = lax.ppermute(send, "row", across)
-    n_ready = cols // block_c - 1 if m % 256 == 0 else 0
+    n_ready = (cols // block_c) // 2 if m % 256 == 0 else 0
+    n_raw = cols // block_c - n_ready
     k_tables = pl.pallas_call(
         lambda *refs: blocks_kernel(local, n_row, n_blocks, amp, *refs),
         out_shape=jax.ShapeDtypeStruct((2, n_blocks * 16, channels * 16), BF16),
@@ -457,7 +461,7 @@
                 lambda *refs: separate_kernel(local, *refs),
                 grid=(2 * n_ready,),
                 out_shape=jax.ShapeDtypeStruct((local, n_ready * block_c, m), BF16),
-                in_specs=[pl.BlockSpec((block_c // 2 * local, m), lambda i: (i + 2, 0))],
+                in_specs=[pl.BlockSpec((block_c // 2 * local, m), lambda i: (i + 2 * n_raw, 0))],
                 out_specs=pl.BlockSpec((local, block_c // 2, m), lambda i: (0, i, 0)),
                 compiler_params=most,
                 cost_estimate=pl.CostEstimate(flops=work, bytes_accessed=2 * work, transcendentals=0),
@@ -477,8 +481,8 @@
     f = lax.all_to_all(f, ("row", "col"), 0, 0, axis_index_groups=halves, tiled=True)
     f = f.reshape(n_p, n_r, p_own * channels, lanes).transpose(0, 2, 1, 3).reshape(n_rows, m)
 
-    n_parts = m // 256 if m % 256 == 0 else 1
-    n_chunks = n_ready + 1
+    n_parts = 3 if m % 768 == 0 else 1
+    n_chunks = n_raw + n_ready
     deep = cols // n_chunks
     keep, send = pl.pallas_call(
         lambda *refs: backward_kernel(local, n_blocks, n_ready, *refs),
@@ -489,7 +493,7 @@
         in_specs=vmem(1) + [pl.BlockSpec(memory_space=pl.ANY)] * (2 + len(ready)),
         out_specs=tuple(vmem(2)),
         scratch_shapes=[
-            pltpu.VMEM((deep * local, m), BF16),
+            pltpu.VMEM((n_raw, deep * local, m), BF16),
             pltpu.VMEM((n_chunks, local, deep, m), BF16),
             pltpu.VMEM((n_chunks, local, 2 * P_SIZE, deep), F32),
             pltpu.VMEM((local, 2 * P_SIZE, m), BF16),

time: 125 us -> 126 us (level)
  Pallas kernels: 36.2 us -> 32.1 us
  waiting for transfers between devices: 7 us -> 9.93 us
    pallas_call x1, Pallas kernels: 10.2 us -> 5.24 us  [shards(): pl.pallas_call(lambda *refs: separate_kernel(local, *refs), grid=(2 * n_r...]
    ppermute x2, waiting for transfers between devices: 5.09 us -> 8.02 us  [shards(): got = lax.ppermute(send, 'row', across)]
  transfers between devices with their start and end apart: 3 -> 3, of which waited for: 2 -> 3; matrix products, arithmetic and copies ran while one was open for 0% -> 0% of each run, Pallas kernels for 9% -> 5%
where the time goes in v9:
time: 126 us
  blocking collectives  77 us (61%)
  Pallas kernels  32.1 us (25%)
  waiting for transfers between devices  9.93 us (8%)
  starting transfers between devices  5.86 us (5%)
    all_to_all x1, blocking collectives, shards(): lax.all_to_all(t, ('row', 'col'), 0, 0, axis_index_groups=halves, tiled=T...  26.6 us
    all_to_all x1, blocking collectives, shards(): lax.all_to_all(f, ('row', 'col'), 0, 0, axis_index_groups=halves, tiled=T...  23 us
    all_to_all x1, blocking collectives, shards(): lax.all_to_all(summed, 'row', 0, 0, axis_index_groups=groups, tiled=True)  14.6 us
    all_to_all x1, blocking collectives, shards(): gram = lax.all_to_all(gram, ('row', 'col'), 0, 0, tiled=True)  12.9 us
    pallas_call x1, Pallas kernels, shards(): pl.pallas_call(lambda *refs: forward_kernel(local, n_freq, *refs), out_sh...  10.6 us
    pallas_call x1, Pallas kernels, shards(): pl.pallas_call(lambda *refs: backward_kernel(local, n_blocks, n_ready, *r...  10 us
    ppermute x2, waiting for transfers between devices, shards(): got = lax.ppermute(send, 'row', across)  8.02 us
    ppermute x2, starting transfers between devices, shards(): got = lax.ppermute(send, 'row', across)  5.35 us
  transfers between devices with their start and end apart: 3, of which 3 were waited for; matrix products, arithmetic and copies ran while one was open for 0% of the time, Pallas kernels for 5%

profile of v9, /device:TPU:0, one launch (start us, length us, event | category | flops | bytes accessed | tf_op | source)
XLA Modules:
  0.0 125.9 jit_solution(14969295183445869207)
XLA Ops:
  0.0 0.0 copy-start.2
  0.0 0.7 copy-done.2
  0.7 10.6 %forward.1 = bf16[32,16,1536]{2,1,0:T(8,128)(2,1)S(1)} custom-call(s32[32]{0:T(128)S(1)} %copy-done.2, bf16[6144,1536]{1,0:T(8,128)(2,1)} %bitcast.12), custom_call_target="tpu_custom_call" | custom-call | flops 1207959552 | bytes 18874368 | tf_op jit(solution)/shard_map/forward/pallas_call | solution.py:394
  11.2 0.0 copy-start.1
  11.3 26.6 %all_to_all.20 = bf16[16,32,1536]{2,1,0:T(8,128)(2,1)S(1)} all-to-all(bf16[16,32,1536]{2,1,0:T(8,128)(2,1)S(1)} %bitcast.9), channel_id=1, replica_groups={{0,1,2,3,4,5,6,7,8,9,10,11,12,13,14,15},{16,17,18,19,20,21,22,23,24,25,..., dimensions={0} | all-to-all | bytes 3145728 | tf_op jit(solution)/shard_map/all_to_all | solution.py:425
  37.9 0.0 copy-done.1
  37.9 0.4 gather.1
  38.3 2.6 %collective-permute-start = (bf16[2,32,1536]{2,1,0:T(8,128)(2,1)S(1)}, bf16[2,32,1536]{2,1,0:T(8,128)(2,1)S(1)}, u32[]{:S(2)}, u32[]{:S(2)}) collective-permute-start(bf16[2,32,1536]{2,1,0:T(8,128)(2,1)S(1)} %get-tuple-element.20), channel_id=1, source_target_pairs={{0,16},{2,18},{4,20},{6,22},{8,24},{10,26},{12,28},{14,30},{16,0},... | collective-permute-start | bytes 589832 | tf_op jit(solution)/shard_map/ppermute | solution.py:445
  40.9 0.5 blocks.1.refs_1_
  41.3 0.0 copy-start
  41.4 5.2 %separate.1.refs_3_ = bf16[8,256,1536]{2,1,0:T(8,128)(2,1)} custom-call(bf16[6144,1536]{1,0:T(8,128)(2,1)} %bitcast.13), custom_call_target="tpu_custom_call" | custom-call | flops 18874368 | bytes 37748736 | tf_op jit(solution)/shard_map/separate/pallas_call | solution.py:460
  46.6 4.1 %collective-permute-done.refs_2_ = bf16[2,32,1536]{2,1,0:T(8,128)(2,1)S(1)} collective-permute-done((bf16[2,32,1536]{2,1,0:T(8,128)(2,1)S(1)}, bf16[2,32,1536]{2,1,0:T(8,128)(2,1)S(1)}, u32[]{:S(2)}, u32[]{:S(2)}) %collective-permute-start) | collective-permute-done | bytes 196640 | tf_op jit(solution)/shard_map/ppermute | solution.py:445
  50.7 0.0 copy-done
  50.7 0.4 scatter.1
  51.0 23.0 %all_to_all.21 = bf16[16,32,1536]{2,1,0:T(8,128)(2,1)S(1)} all-to-all(bf16[16,32,1536]{2,1,0:T(8,128)(2,1)S(1)} %bitcast.8), channel_id=1, replica_groups={{0,1,2,3,4,5,6,7,8,9,10,11,12,13,14,15},{16,17,18,19,20,21,22,23,24,25,..., dimensions={0} | all-to-all | bytes 3145728 | tf_op jit(solution)/shard_map/all_to_all | solution.py:481
  74.0 10.0 %backward.1 = (f32[16,32,768]{2,1,0:T(8,128)S(1)}, bf16[16,32,768]{2,1,0:T(8,128)(2,1)S(1)}) custom-call(bf16[512,1536]{1,0:T(8,128)(2,1)S(1)} %bitcast.10, bf16[2,512,256]{2,1,0:T(8,128)(2,1)S(1)} %blocks.1.refs_1_, bf16[6144,1536]{1,0:T(8,128)(2,1)} %bitcast.14, bf16[8,256,1536]{2,1,0:T(8,128)(2,1)} %separate.1.refs_3_), custom_call_target="tpu_custom_call" | custom-call | flops 1207959552 | bytes 18874368 | tf_op jit(solution)/shard_map/backward/pallas_call | solution.py:487
  84.0 0.5 collective-permute-start.1
  84.6 1.9 %collective-permute-done.1 = bf16[16,32,768]{2,1,0:T(8,128)(2,1)S(1)} collective-permute-done((bf16[16,32,768]{2,1,0:T(8,128)(2,1)S(1)}, bf16[16,32,768]{2,1,0:T(8,128)(2,1)S(1)}, u32[]{:S(2)}, u32[]{:S(2)}) %collective-permute-start.1) | collective-permute-done | bytes 786464 | tf_op jit(solution)/shard_map/ppermute | solution.py:508
  86.5 0.2 add_convert_fusion
  86.7 14.6 %all_to_all.22 = bf16[16,32,768]{2,1,0:T(8,128)(2,1)S(1)} all-to-all(bf16[16,32,768]{2,1,0:T(8,128)(2,1)S(1)} %add_convert_fusion), channel_id=1, replica_groups={{0,4,8,12},{2,6,10,14},{16,20,24,28},{18,22,26,30},{1,5,9,13},{3,7,11,1..., dimensions={0} | all-to-all | bytes 1572864 | tf_op jit(solution)/shard_map/all_to_all | solution.py:511
  101.3 0.1 join.1
  101.4 2.7 %collective-permute-start.2 = (bf16[2,32,768]{2,1,0:T(8,128)(2,1)S(1)}, bf16[2,32,768]{2,1,0:T(8,128)(2,1)S(1)}, u32[]{:S(2)}, u32[]{:S(2)}) collective-permute-start(bf16[2,32,768]{2,1,0:T(8,128)(2,1)S(1)} %get-tuple-element.28), channel_id=1, source_target_pairs={{0,16},{2,18},{4,20},{6,22},{8,24},{10,26},{12,28},{14,30},{16,0},... | collective-permute-start | bytes 294920 | tf_op jit(solution)/shard_map/ppermute | solution.py:524
  104.1 3.9 %collective-permute-done.2.got_ref = bf16[2,32,768]{2,1,0:T(8,128)(2,1)S(1)} collective-permute-done((bf16[2,32,768]{2,1,0:T(8,128)(2,1)S(1)}, bf16[2,32,768]{2,1,0:T(8,128)(2,1)S(1)}, u32[]{:S(2)}, u32[]{:S(2)}) %collective-permute-start.2) | collective-permute-done | bytes 98336 | tf_op jit(solution)/shard_map/ppermute | solution.py:524
  108.0 0.4 gram.1
  108.4 12.9 %all_to_all.23.refs_0_ = f32[32,8,128]{2,1,0:T(8,128)S(1)} all-to-all(f32[32,8,128]{2,1,0:T(8,128)S(1)} %get-tuple-element.29), channel_id=1, replica_groups=mesh['row'=16,'col'=2] {'row','col'}, dimensions={0} | all-to-all | bytes 262144 | tf_op jit(solution)/shard_map/all_to_all | solution.py:537
  121.3 4.6 %last.1 = f32[2,32,768]{2,1,0:T(8,128)} custom-call(f32[32,8,128]{2,1,0:T(8,128)S(1)} %all_to_all.23.refs_0_, f32[2,32,768]{2,1,0:T(8,128)S(1)} %get-tuple-element.30.refs_1_), custom_call_target="tpu_custom_call" | custom-call | tf_op jit(solution)/shard_map/last/pallas_call | solution.py:538
Async XLA Ops:
  0.0 0.7 copy-start.2
  11.2 26.6 %copy-start.1 = (bf16[2,64,256]{2,1,0:T(8,128)(2,1)S(1)}, bf16[2,64,256]{2,1,0:T(8,128)(2,1)}, u32[]{:S(2)}) copy-start(bf16[2,64,256]{2,1,0:T(8,128)(2,1)} %constant.4.clone.refs_0_) | copy-start | bytes 196612
  38.3 12.4 %collective-permute-start = (bf16[2,32,1536]{2,1,0:T(8,128)(2,1)S(1)}, bf16[2,32,1536]{2,1,0:T(8,128)(2,1)S(1)}, u32[]{:S(2)}, u32[]{:S(2)}) collective-permute-start(bf16[2,32,1536]{2,1,0:T(8,128)(2,1)S(1)} %get-tuple-element.20), channel_id=1, source_target_pairs={{0,16},{2,18},{4,20},{6,22},{8,24},{10,26},{12,28},{14,30},{16,0},... | collective-permute-start | bytes 589832 | tf_op jit(solution)/shard_map/ppermute | solution.py:445
  41.3 9.3 %copy-start = (bf16[2,128,96]{2,1,0:T(8,128)(2,1)S(1)}, bf16[2,128,96]{2,1,0:T(8,128)(2,1)}, u32[]{:S(2)}) copy-start(bf16[2,128,96]{2,1,0:T(8,128)(2,1)} %constant.5.clone.refs_0_) | copy-start | bytes 147460
  84.0 2.4 %collective-permute-start.1 = (bf16[16,32,768]{2,1,0:T(8,128)(2,1)S(1)}, bf16[16,32,768]{2,1,0:T(8,128)(2,1)S(1)}, u32[]{:S(2)}, u32[]{:S(2)}) collective-permute-start(bf16[16,32,768]{2,1,0:T(8,128)(2,1)S(1)} %get-tuple-element.26), channel_id=1, source_target_pairs={{0,2},{2,0},{4,6},{6,4},{8,10},{10,8},{12,14},{14,12},{16,18},{18,... | collective-permute-start | bytes 2359304 | tf_op jit(solution)/shard_map/ppermute | solution.py:508
  101.4 6.7 %collective-permute-start.2 = (bf16[2,32,768]{2,1,0:T(8,128)(2,1)S(1)}, bf16[2,32,768]{2,1,0:T(8,128)(2,1)S(1)}, u32[]{:S(2)}, u32[]{:S(2)}) collective-permute-start(bf16[2,32,768]{2,1,0:T(8,128)(2,1)S(1)} %get-tuple-element.28), channel_id=1, source_target_pairs={{0,16},{2,18},{4,20},{6,22},{8,24},{10,26},{12,28},{14,30},{16,0},... | collective-permute-start | bytes 294920 | tf_op jit(solution)/shard_map/ppermute | solution.py:524

commit v10 on v9

--- a/solution.py
+++ b/solution.py
@@ -268,25 +268,32 @@
     ready_ref = refs[0] if n_ready else None
     keep_ref, send_ref, raw, held, sums, f_by, k_parts, sems, sem = refs[bool(n_ready) :]
     n_chunks, _, block_c, m = held.shape
-    n_raw, n_parts = n_chunks - n_ready, sems.shape[1]
+    n_subs, n_parts = sems.shape
+    n_raw, sub = n_subs - n_ready, block_c * n_chunks // n_subs
     width = m // n_parts
     step = 256 if width % 256 == 0 else width
-    tall = block_c * local
+    tall = sub * local
     rows = f_ref.shape[0] // 4
     half = n_blocks // 2
 
-    def copy(b, i):
+    def spot(s):
+        return s * sub // block_c, slice(s * sub % block_c, s * sub % block_c + sub)
+
+    def copy(s, i):
         at = slice(i * width, (i + 1) * width)
-        if b < n_raw:
-            return pltpu.make_async_copy(d_ref.at[pl.ds(b * tall, tall), at], raw.at[b, :, at], sems.at[b, i])
-        source = ready_ref.at[:, pl.ds((b - n_raw) * block_c, block_c), at]
-        return pltpu.make_async_copy(source, held.at[b, :, :, at], sems.at[b, i])
+        if s < n_raw:
+            return pltpu.make_async_copy(d_ref.at[pl.ds(s * tall, tall), at], raw.at[s, :, at], sems.at[s, i])
+        b, columns = spot(s)
+        source = ready_ref.at[:, pl.ds((s - n_raw) * sub, sub), at]
+        return pltpu.make_async_copy(source, held.at[b, :, columns, at], sems.at[s, i])
 
     tables = pltpu.make_async_copy(k_ref, k_parts, sem)
-    order = (*range(n_raw, n_chunks), *range(n_raw))
+    per = n_subs // n_chunks
+    order = sorted(range(n_chunks), key=lambda b: (b * per < n_raw, b))
     for i in range(n_parts):
         for b in order:
-            copy(b, i).start()
+            for s in range(b * per, (b + 1) * per):
+                copy(s, i).start()
     tables.start()
 
     swap = place(rows, rows, lambda r, c: (r % 8 * 2 + r // 8 % 2) * local + r // 16 == c).astype(BF16)
@@ -298,11 +305,14 @@
     for i in range(n_parts):
         at = slice(i * width, (i + 1) * width)
         for b in order:
-            copy(b, i).wait()
-            for p in range(i * width, (i + 1) * width, step) if b < n_raw else ():
-                for c in range(0, block_c, 16):
-                    piece = raw[b, c * local : (c + 16) * local, p : p + step]
-                    held[b, :, c : c + 16, p : p + step] = separate(piece, local)
+            for s in range(b * per, (b + 1) * per):
+                copy(s, i).wait()
+            for s in range(b * per, min((b + 1) * per, n_raw)):
+                base = spot(s)[1].start
+                for p in range(i * width, (i + 1) * width, step):
+                    for c in range(0, sub, 16):
+                        piece = raw[s, c * local : (c + 16) * local, p : p + step]
+                        held[b, :, base + c : base + c + 16, p : p + step] = separate(piece, local)
             for k in range(local):
                 part = lax.dot_general(f_by[k, :, at], held[b, k, :, at], NT, preferred_element_type=F32)
                 sums[b, k] = part if i == 0 else sums[b, k] + part
@@ -413,7 +423,7 @@
         compiler_params=large,
         cost_estimate=pl.CostEstimate(flops=64 * work, bytes_accessed=work, transcendentals=0),
         name="forward",
-    )(block_seeds, flat)
+    )(pltpu.with_memory_space_constraint(block_seeds, pltpu.HBM), flat)
     n_grp = n_dev // 2
     n_p = math.gcd(P_SIZE, n_grp)
     n_r = n_grp // n_p
@@ -443,8 +453,10 @@
     )(jnp.asarray(merge), t)
     send, flat = lax.optimization_barrier((send, flat))
     got = lax.ppermute(send, "row", across)
-    n_ready = (cols // block_c) // 2 if m % 256 == 0 else 0
-    n_raw = cols // block_c - n_ready
+    sub = block_c // 2
+    n_subs = cols // sub
+    n_ready = n_subs // 2 if m % 256 == 0 and n_subs > 2 else 0
+    n_raw = n_subs - n_ready
     k_tables = pl.pallas_call(
         lambda *refs: blocks_kernel(local, n_row, n_blocks, amp, *refs),
         out_shape=jax.ShapeDtypeStruct((2, n_blocks * 16, channels * 16), BF16),
@@ -459,10 +471,10 @@
         ready.append(
             pl.pallas_call(
                 lambda *refs: separate_kernel(local, *refs),
-                grid=(2 * n_ready,),
-                out_shape=jax.ShapeDtypeStruct((local, n_ready * block_c, m), BF16),
-                in_specs=[pl.BlockSpec((block_c // 2 * local, m), lambda i: (i + 2 * n_raw, 0))],
-                out_specs=pl.BlockSpec((local, block_c // 2, m), lambda i: (0, i, 0)),
+                grid=(n_ready,),
+                out_shape=jax.ShapeDtypeStruct((local, n_ready * sub, m), BF16),
+                in_specs=[pl.BlockSpec((sub * local, m), lambda i: (i + n_raw, 0))],
+                out_specs=pl.BlockSpec((local, sub, m), lambda i: (0, i, 0)),
                 compiler_params=most,
                 cost_estimate=pl.CostEstimate(flops=work, bytes_accessed=2 * work, transcendentals=0),
                 name="separate",
@@ -482,8 +494,7 @@
     f = f.reshape(n_p, n_r, p_own * channels, lanes).transpose(0, 2, 1, 3).reshape(n_rows, m)
 
     n_parts = 3 if m % 768 == 0 else 1
-    n_chunks = n_raw + n_ready
-    deep = cols // n_chunks
+    n_chunks = cols // block_c
     keep, send = pl.pallas_call(
         lambda *refs: backward_kernel(local, n_blocks, n_ready, *refs),
         out_shape=(
@@ -493,12 +504,12 @@
         in_specs=vmem(1) + [pl.BlockSpec(memory_space=pl.ANY)] * (2 + len(ready)),
         out_specs=tuple(vmem(2)),
         scratch_shapes=[
-            pltpu.VMEM((n_raw, deep * local, m), BF16),
-            pltpu.VMEM((n_chunks, local, deep, m), BF16),
-            pltpu.VMEM((n_chunks, local, 2 * P_SIZE, deep), F32),
+            pltpu.VMEM((n_raw, sub * local, m), BF16),
+            pltpu.VMEM((n_chunks, local, block_c, m), BF16),
+            pltpu.VMEM((n_chunks, local, 2 * P_SIZE, block_c), F32),
             pltpu.VMEM((local, 2 * P_SIZE, m), BF16),
             pltpu.VMEM((2, n_blocks * 16, channels * 16), BF16),
-            pltpu.SemaphoreType.DMA((n_chunks, n_parts)),
+            pltpu.SemaphoreType.DMA((n_subs, n_parts)),
             pltpu.SemaphoreType.DMA,
         ],
         compiler_params=large,

time: 126 us -> 125 us (level)
  waiting for transfers between devices: 9.93 us -> 6.11 us
  Pallas kernels: 32.1 us -> 35.8 us
    pallas_call x1, Pallas kernels: 5.24 us -> 9.27 us  [shards(): pl.pallas_call(lambda *refs: separate_kernel(local, *refs), grid=(n_ready...]
    ppermute x2, waiting for transfers between devices: 8.02 us -> 4.19 us  [shards(): got = lax.ppermute(send, 'row', across)]
  transfers between devices with their start and end apart: 3 -> 3, of which waited for: 3 -> 2; matrix products, arithmetic and copies ran while one was open for 0% -> 0% of each run, Pallas kernels for 5% -> 8%
where the time goes in v10:
time: 125 us
  blocking collectives  77.1 us (62%)
  Pallas kernels  35.8 us (29%)
  waiting for transfers between devices  6.11 us (5%)
  starting transfers between devices  5.65 us (5%)
    all_to_all x1, blocking collectives, shards(): lax.all_to_all(t, ('row', 'col'), 0, 0, axis_index_groups=halves, tiled=T...  26.6 us
    all_to_all x1, blocking collectives, shards(): lax.all_to_all(f, ('row', 'col'), 0, 0, axis_index_groups=halves, tiled=T...  23.2 us
    all_to_all x1, blocking collectives, shards(): lax.all_to_all(summed, 'row', 0, 0, axis_index_groups=groups, tiled=True)  14.6 us
    all_to_all x1, blocking collectives, shards(): gram = lax.all_to_all(gram, ('row', 'col'), 0, 0, tiled=True)  12.7 us
    pallas_call x1, Pallas kernels, shards(): pl.pallas_call(lambda *refs: forward_kernel(local, n_freq, *refs), out_sh...  10.6 us
    pallas_call x1, Pallas kernels, shards(): pl.pallas_call(lambda *refs: backward_kernel(local, n_blocks, n_ready, *r...  9.67 us
    pallas_call x1, Pallas kernels, shards(): pl.pallas_call(lambda *refs: separate_kernel(local, *refs), grid=(n_ready...  9.27 us
    ppermute x2, starting transfers between devices, shards(): got = lax.ppermute(send, 'row', across)  5.12 us
  transfers between devices with their start and end apart: 3, of which 2 were waited for; matrix products, arithmetic and copies ran while one was open for 0% of the time, Pallas kernels for 8%

profile of v10, /device:TPU:0, one launch (start us, length us, event | category | flops | bytes accessed | tf_op | source)
XLA Modules:
  0.0 124.9 jit_solution(1976201100636775384)
XLA Ops:
  0.0 10.6 %forward.1 = bf16[32,16,1536]{2,1,0:T(8,128)(2,1)S(1)} custom-call(s32[32]{0:T(128)} %refs_0_.3, bf16[6144,1536]{1,0:T(8,128)(2,1)} %bitcast.12), custom_call_target="tpu_custom_call" | custom-call | flops 1207959552 | bytes 18874368 | tf_op jit(solution)/shard_map/forward/pallas_call | solution.py:404
  10.6 0.0 copy-start.1
  10.6 26.6 %all_to_all.20 = bf16[16,32,1536]{2,1,0:T(8,128)(2,1)S(1)} all-to-all(bf16[16,32,1536]{2,1,0:T(8,128)(2,1)S(1)} %bitcast.9), channel_id=1, replica_groups={{0,1,2,3,4,5,6,7,8,9,10,11,12,13,14,15},{16,17,18,19,20,21,22,23,24,25,..., dimensions={0} | all-to-all | bytes 3145728 | tf_op jit(solution)/shard_map/all_to_all | solution.py:435
  37.2 0.0 copy-done.1
  37.2 0.4 gather.1
  37.6 2.6 %collective-permute-start = (bf16[2,32,1536]{2,1,0:T(8,128)(2,1)S(1)}, bf16[2,32,1536]{2,1,0:T(8,128)(2,1)S(1)}, u32[]{:S(2)}, u32[]{:S(2)}) collective-permute-start(bf16[2,32,1536]{2,1,0:T(8,128)(2,1)S(1)} %get-tuple-element.20), channel_id=1, source_target_pairs={{0,16},{2,18},{4,20},{6,22},{8,24},{10,26},{12,28},{14,30},{16,0},... | collective-permute-start | bytes 589832 | tf_op jit(solution)/shard_map/ppermute | solution.py:455
  40.2 0.5 blocks.1.refs_1_
  40.7 0.0 copy-start
  40.7 9.3 %separate.1.refs_3_ = bf16[8,384,1536]{2,1,0:T(8,128)(2,1)} custom-call(bf16[6144,1536]{1,0:T(8,128)(2,1)} %bitcast.13), custom_call_target="tpu_custom_call" | custom-call | flops 18874368 | bytes 37748736 | tf_op jit(solution)/shard_map/separate/pallas_call | solution.py:472
  50.0 0.0 collective-permute-done.refs_2_
  50.0 0.0 copy-done
  50.0 0.4 scatter.1
  50.4 23.2 %all_to_all.21 = bf16[16,32,1536]{2,1,0:T(8,128)(2,1)S(1)} all-to-all(bf16[16,32,1536]{2,1,0:T(8,128)(2,1)S(1)} %bitcast.8), channel_id=1, replica_groups={{0,1,2,3,4,5,6,7,8,9,10,11,12,13,14,15},{16,17,18,19,20,21,22,23,24,25,..., dimensions={0} | all-to-all | bytes 3145728 | tf_op jit(solution)/shard_map/all_to_all | solution.py:493
  73.6 9.7 %backward.1 = (f32[16,32,768]{2,1,0:T(8,128)S(1)}, bf16[16,32,768]{2,1,0:T(8,128)(2,1)S(1)}) custom-call(bf16[512,1536]{1,0:T(8,128)(2,1)S(1)} %bitcast.10, bf16[2,512,256]{2,1,0:T(8,128)(2,1)S(1)} %blocks.1.refs_1_, bf16[6144,1536]{1,0:T(8,128)(2,1)} %bitcast.14, bf16[8,384,1536]{2,1,0:T(8,128)(2,1)} %separate.1.refs_3_), custom_call_target="tpu_custom_call" | custom-call | flops 1207959552 | bytes 18874368 | tf_op jit(solution)/shard_map/backward/pallas_call | solution.py:498
  83.3 0.5 collective-permute-start.1
  83.8 1.9 %collective-permute-done.1 = bf16[16,32,768]{2,1,0:T(8,128)(2,1)S(1)} collective-permute-done((bf16[16,32,768]{2,1,0:T(8,128)(2,1)S(1)}, bf16[16,32,768]{2,1,0:T(8,128)(2,1)S(1)}, u32[]{:S(2)}, u32[]{:S(2)}) %collective-permute-start.1) | collective-permute-done | bytes 786464 | tf_op jit(solution)/shard_map/ppermute | solution.py:519
  85.7 0.2 add_convert_fusion
  86.0 14.6 %all_to_all.22 = bf16[16,32,768]{2,1,0:T(8,128)(2,1)S(1)} all-to-all(bf16[16,32,768]{2,1,0:T(8,128)(2,1)S(1)} %add_convert_fusion), channel_id=1, replica_groups={{0,4,8,12},{2,6,10,14},{16,20,24,28},{18,22,26,30},{1,5,9,13},{3,7,11,1..., dimensions={0} | all-to-all | bytes 1572864 | tf_op jit(solution)/shard_map/all_to_all | solution.py:522
  100.5 0.1 join.1
  100.6 2.5 %collective-permute-start.2 = (bf16[2,32,768]{2,1,0:T(8,128)(2,1)S(1)}, bf16[2,32,768]{2,1,0:T(8,128)(2,1)S(1)}, u32[]{:S(2)}, u32[]{:S(2)}) collective-permute-start(bf16[2,32,768]{2,1,0:T(8,128)(2,1)S(1)} %get-tuple-element.28), channel_id=1, source_target_pairs={{0,16},{2,18},{4,20},{6,22},{8,24},{10,26},{12,28},{14,30},{16,0},... | collective-permute-start | bytes 294920 | tf_op jit(solution)/shard_map/ppermute | solution.py:535
  103.1 4.1 %collective-permute-done.2.got_ref = bf16[2,32,768]{2,1,0:T(8,128)(2,1)S(1)} collective-permute-done((bf16[2,32,768]{2,1,0:T(8,128)(2,1)S(1)}, bf16[2,32,768]{2,1,0:T(8,128)(2,1)S(1)}, u32[]{:S(2)}, u32[]{:S(2)}) %collective-permute-start.2) | collective-permute-done | bytes 98336 | tf_op jit(solution)/shard_map/ppermute | solution.py:535
  107.3 0.4 gram.1
  107.6 12.7 %all_to_all.23.refs_0_ = f32[32,8,128]{2,1,0:T(8,128)S(1)} all-to-all(f32[32,8,128]{2,1,0:T(8,128)S(1)} %get-tuple-element.29), channel_id=1, replica_groups=mesh['row'=16,'col'=2] {'row','col'}, dimensions={0} | all-to-all | bytes 262144 | tf_op jit(solution)/shard_map/all_to_all | solution.py:548
  120.3 4.6 %last.1 = f32[2,32,768]{2,1,0:T(8,128)} custom-call(f32[32,8,128]{2,1,0:T(8,128)S(1)} %all_to_all.23.refs_0_, f32[2,32,768]{2,1,0:T(8,128)S(1)} %get-tuple-element.30.refs_1_), custom_call_target="tpu_custom_call" | custom-call | tf_op jit(solution)/shard_map/last/pallas_call | solution.py:549
Async XLA Ops:
  10.6 26.6 %copy-start.1 = (bf16[2,64,256]{2,1,0:T(8,128)(2,1)S(1)}, bf16[2,64,256]{2,1,0:T(8,128)(2,1)}, u32[]{:S(2)}) copy-start(bf16[2,64,256]{2,1,0:T(8,128)(2,1)} %constant.4.clone.refs_0_) | copy-start | bytes 196612
  37.6 12.4 %collective-permute-start = (bf16[2,32,1536]{2,1,0:T(8,128)(2,1)S(1)}, bf16[2,32,1536]{2,1,0:T(8,128)(2,1)S(1)}, u32[]{:S(2)}, u32[]{:S(2)}) collective-permute-start(bf16[2,32,1536]{2,1,0:T(8,128)(2,1)S(1)} %get-tuple-element.20), channel_id=1, source_target_pairs={{0,16},{2,18},{4,20},{6,22},{8,24},{10,26},{12,28},{14,30},{16,0},... | collective-permute-start | bytes 589832 | tf_op jit(solution)/shard_map/ppermute | solution.py:455
  40.7 9.3 %copy-start = (bf16[2,128,96]{2,1,0:T(8,128)(2,1)S(1)}, bf16[2,128,96]{2,1,0:T(8,128)(2,1)}, u32[]{:S(2)}) copy-start(bf16[2,128,96]{2,1,0:T(8,128)(2,1)} %constant.5.clone.refs_0_) | copy-start | bytes 147460
  83.3 2.4 %collective-permute-start.1 = (bf16[16,32,768]{2,1,0:T(8,128)(2,1)S(1)}, bf16[16,32,768]{2,1,0:T(8,128)(2,1)S(1)}, u32[]{:S(2)}, u32[]{:S(2)}) collective-permute-start(bf16[16,32,768]{2,1,0:T(8,128)(2,1)S(1)} %get-tuple-element.26), channel_id=1, source_target_pairs={{0,2},{2,0},{4,6},{6,4},{8,10},{10,8},{12,14},{14,12},{16,18},{18,... | collective-permute-start | bytes 2359304 | tf_op jit(solution)/shard_map/ppermute | solution.py:519
  100.6 6.6 %collective-permute-start.2 = (bf16[2,32,768]{2,1,0:T(8,128)(2,1)S(1)}, bf16[2,32,768]{2,1,0:T(8,128)(2,1)S(1)}, u32[]{:S(2)}, u32[]{:S(2)}) collective-permute-start(bf16[2,32,768]{2,1,0:T(8,128)(2,1)S(1)} %get-tuple-element.28), channel_id=1, source_target_pairs={{0,16},{2,18},{4,20},{6,22},{8,24},{10,26},{12,28},{14,30},{16,0},... | collective-permute-start | bytes 294920 | tf_op jit(solution)/shard_map/ppermute | solution.py:535

commit v11 on v10

--- a/solution.py
+++ b/solution.py
@@ -289,7 +289,7 @@
 
     tables = pltpu.make_async_copy(k_ref, k_parts, sem)
     per = n_subs // n_chunks
-    order = sorted(range(n_chunks), key=lambda b: (b * per < n_raw, b))
+    order = range(n_chunks)
     for i in range(n_parts):
         for b in order:
             for s in range(b * per, (b + 1) * per):

time: 125 us -> 125 us (level)
  no operation moved by 1% of the time
where the time goes in v11:
time: 125 us
  blocking collectives  77.1 us (62%)
  Pallas kernels  35.7 us (29%)
  waiting for transfers between devices  6.09 us (5%)
  starting transfers between devices  5.65 us (5%)
    all_to_all x1, blocking collectives, shards(): lax.all_to_all(t, ('row', 'col'), 0, 0, axis_index_groups=halves, tiled=T...  26.6 us
    all_to_all x1, blocking collectives, shards(): lax.all_to_all(f, ('row', 'col'), 0, 0, axis_index_groups=halves, tiled=T...  23.2 us
    all_to_all x1, blocking collectives, shards(): lax.all_to_all(summed, 'row', 0, 0, axis_index_groups=groups, tiled=True)  14.6 us
    all_to_all x1, blocking collectives, shards(): gram = lax.all_to_all(gram, ('row', 'col'), 0, 0, tiled=True)  12.7 us
    pallas_call x1, Pallas kernels, shards(): pl.pallas_call(lambda *refs: forward_kernel(local, n_freq, *refs), out_sh...  10.6 us
    pallas_call x1, Pallas kernels, shards(): pl.pallas_call(lambda *refs: backward_kernel(local, n_blocks, n_ready, *r...  9.62 us
    pallas_call x1, Pallas kernels, shards(): pl.pallas_call(lambda *refs: separate_kernel(local, *refs), grid=(n_ready...  9.27 us
    ppermute x2, starting transfers between devices, shards(): got = lax.ppermute(send, 'row', across)  5.13 us
  transfers between devices with their start and end apart: 3, of which 2 were waited for; matrix products, arithmetic and copies ran while one was open for 0% of the time, Pallas kernels for 8%

profile of v11, /device:TPU:0, one launch (start us, length us, event | category | flops | bytes accessed | tf_op | source)
XLA Modules:
  0.0 124.8 jit_solution(16318906714320317181)
XLA Ops:
  0.0 10.6 %forward.1 = bf16[32,16,1536]{2,1,0:T(8,128)(2,1)S(1)} custom-call(s32[32]{0:T(128)} %refs_0_.3, bf16[6144,1536]{1,0:T(8,128)(2,1)} %bitcast.12), custom_call_target="tpu_custom_call" | custom-call | flops 1207959552 | bytes 18874368 | tf_op jit(solution)/shard_map/forward/pallas_call | solution.py:404
  10.6 0.0 copy-start.1
  10.6 26.6 %all_to_all.20 = bf16[16,32,1536]{2,1,0:T(8,128)(2,1)S(1)} all-to-all(bf16[16,32,1536]{2,1,0:T(8,128)(2,1)S(1)} %bitcast.9), channel_id=1, replica_groups={{0,1,2,3,4,5,6,7,8,9,10,11,12,13,14,15},{16,17,18,19,20,21,22,23,24,25,..., dimensions={0} | all-to-all | bytes 3145728 | tf_op jit(solution)/shard_map/all_to_all | solution.py:435
  37.2 0.0 copy-done.1
  37.2 0.4 gather.1
  37.6 2.6 %collective-permute-start = (bf16[2,32,1536]{2,1,0:T(8,128)(2,1)S(1)}, bf16[2,32,1536]{2,1,0:T(8,128)(2,1)S(1)}, u32[]{:S(2)}, u32[]{:S(2)}) collective-permute-start(bf16[2,32,1536]{2,1,0:T(8,128)(2,1)S(1)} %get-tuple-element.20), channel_id=1, source_target_pairs={{0,16},{2,18},{4,20},{6,22},{8,24},{10,26},{12,28},{14,30},{16,0},... | collective-permute-start | bytes 589832 | tf_op jit(solution)/shard_map/ppermute | solution.py:455
  40.2 0.5 blocks.1.refs_1_
  40.7 0.0 copy-start
  40.7 9.3 %separate.1.refs_3_ = bf16[8,384,1536]{2,1,0:T(8,128)(2,1)} custom-call(bf16[6144,1536]{1,0:T(8,128)(2,1)} %bitcast.13), custom_call_target="tpu_custom_call" | custom-call | flops 18874368 | bytes 37748736 | tf_op jit(solution)/shard_map/separate/pallas_call | solution.py:472
  50.0 0.0 collective-permute-done.refs_2_
  50.0 0.0 copy-done
  50.0 0.4 scatter.1
  50.4 23.2 %all_to_all.21 = bf16[16,32,1536]{2,1,0:T(8,128)(2,1)S(1)} all-to-all(bf16[16,32,1536]{2,1,0:T(8,128)(2,1)S(1)} %bitcast.8), channel_id=1, replica_groups={{0,1,2,3,4,5,6,7,8,9,10,11,12,13,14,15},{16,17,18,19,20,21,22,23,24,25,..., dimensions={0} | all-to-all | bytes 3145728 | tf_op jit(solution)/shard_map/all_to_all | solution.py:493
  73.6 9.6 %backward.1 = (f32[16,32,768]{2,1,0:T(8,128)S(1)}, bf16[16,32,768]{2,1,0:T(8,128)(2,1)S(1)}) custom-call(bf16[512,1536]{1,0:T(8,128)(2,1)S(1)} %bitcast.10, bf16[2,512,256]{2,1,0:T(8,128)(2,1)S(1)} %blocks.1.refs_1_, bf16[6144,1536]{1,0:T(8,128)(2,1)} %bitcast.14, bf16[8,384,1536]{2,1,0:T(8,128)(2,1)} %separate.1.refs_3_), custom_call_target="tpu_custom_call" | custom-call | flops 1207959552 | bytes 18874368 | tf_op jit(solution)/shard_map/backward/pallas_call | solution.py:498
  83.2 0.5 collective-permute-start.1
  83.8 1.9 %collective-permute-done.1 = bf16[16,32,768]{2,1,0:T(8,128)(2,1)S(1)} collective-permute-done((bf16[16,32,768]{2,1,0:T(8,128)(2,1)S(1)}, bf16[16,32,768]{2,1,0:T(8,128)(2,1)S(1)}, u32[]{:S(2)}, u32[]{:S(2)}) %collective-permute-start.1) | collective-permute-done | bytes 786464 | tf_op jit(solution)/shard_map/ppermute | solution.py:519
  85.7 0.2 add_convert_fusion
  85.9 14.6 %all_to_all.22 = bf16[16,32,768]{2,1,0:T(8,128)(2,1)S(1)} all-to-all(bf16[16,32,768]{2,1,0:T(8,128)(2,1)S(1)} %add_convert_fusion), channel_id=1, replica_groups={{0,4,8,12},{2,6,10,14},{16,20,24,28},{18,22,26,30},{1,5,9,13},{3,7,11,1..., dimensions={0} | all-to-all | bytes 1572864 | tf_op jit(solution)/shard_map/all_to_all | solution.py:522
  100.5 0.1 join.1
  100.6 2.5 %collective-permute-start.2 = (bf16[2,32,768]{2,1,0:T(8,128)(2,1)S(1)}, bf16[2,32,768]{2,1,0:T(8,128)(2,1)S(1)}, u32[]{:S(2)}, u32[]{:S(2)}) collective-permute-start(bf16[2,32,768]{2,1,0:T(8,128)(2,1)S(1)} %get-tuple-element.28), channel_id=1, source_target_pairs={{0,16},{2,18},{4,20},{6,22},{8,24},{10,26},{12,28},{14,30},{16,0},... | collective-permute-start | bytes 294920 | tf_op jit(solution)/shard_map/ppermute | solution.py:535
  103.1 4.1 %collective-permute-done.2.got_ref = bf16[2,32,768]{2,1,0:T(8,128)(2,1)S(1)} collective-permute-done((bf16[2,32,768]{2,1,0:T(8,128)(2,1)S(1)}, bf16[2,32,768]{2,1,0:T(8,128)(2,1)S(1)}, u32[]{:S(2)}, u32[]{:S(2)}) %collective-permute-start.2) | collective-permute-done | bytes 98336 | tf_op jit(solution)/shard_map/ppermute | solution.py:535
  107.2 0.4 gram.1
  107.6 12.7 %all_to_all.23.refs_0_ = f32[32,8,128]{2,1,0:T(8,128)S(1)} all-to-all(f32[32,8,128]{2,1,0:T(8,128)S(1)} %get-tuple-element.29), channel_id=1, replica_groups=mesh['row'=16,'col'=2] {'row','col'}, dimensions={0} | all-to-all | bytes 262144 | tf_op jit(solution)/shard_map/all_to_all | solution.py:548
  120.3 4.6 %last.1 = f32[2,32,768]{2,1,0:T(8,128)} custom-call(f32[32,8,128]{2,1,0:T(8,128)S(1)} %all_to_all.23.refs_0_, f32[2,32,768]{2,1,0:T(8,128)S(1)} %get-tuple-element.30.refs_1_), custom_call_target="tpu_custom_call" | custom-call | tf_op jit(solution)/shard_map/last/pallas_call | solution.py:549
Async XLA Ops:
  10.6 26.6 %copy-start.1 = (bf16[2,64,256]{2,1,0:T(8,128)(2,1)S(1)}, bf16[2,64,256]{2,1,0:T(8,128)(2,1)}, u32[]{:S(2)}) copy-start(bf16[2,64,256]{2,1,0:T(8,128)(2,1)} %constant.4.clone.refs_0_) | copy-start | bytes 196612
  37.6 12.4 %collective-permute-start = (bf16[2,32,1536]{2,1,0:T(8,128)(2,1)S(1)}, bf16[2,32,1536]{2,1,0:T(8,128)(2,1)S(1)}, u32[]{:S(2)}, u32[]{:S(2)}) collective-permute-start(bf16[2,32,1536]{2,1,0:T(8,128)(2,1)S(1)} %get-tuple-element.20), channel_id=1, source_target_pairs={{0,16},{2,18},{4,20},{6,22},{8,24},{10,26},{12,28},{14,30},{16,0},... | collective-permute-start | bytes 589832 | tf_op jit(solution)/shard_map/ppermute | solution.py:455
  40.7 9.3 %copy-start = (bf16[2,128,96]{2,1,0:T(8,128)(2,1)S(1)}, bf16[2,128,96]{2,1,0:T(8,128)(2,1)}, u32[]{:S(2)}) copy-start(bf16[2,128,96]{2,1,0:T(8,128)(2,1)} %constant.5.clone.refs_0_) | copy-start | bytes 147460
  83.2 2.4 %collective-permute-start.1 = (bf16[16,32,768]{2,1,0:T(8,128)(2,1)S(1)}, bf16[16,32,768]{2,1,0:T(8,128)(2,1)S(1)}, u32[]{:S(2)}, u32[]{:S(2)}) collective-permute-start(bf16[16,32,768]{2,1,0:T(8,128)(2,1)S(1)} %get-tuple-element.26), channel_id=1, source_target_pairs={{0,2},{2,0},{4,6},{6,4},{8,10},{10,8},{12,14},{14,12},{16,18},{18,... | collective-permute-start | bytes 2359304 | tf_op jit(solution)/shard_map/ppermute | solution.py:519
  100.6 6.6 %collective-permute-start.2 = (bf16[2,32,768]{2,1,0:T(8,128)(2,1)S(1)}, bf16[2,32,768]{2,1,0:T(8,128)(2,1)S(1)}, u32[]{:S(2)}, u32[]{:S(2)}) collective-permute-start(bf16[2,32,768]{2,1,0:T(8,128)(2,1)S(1)} %get-tuple-element.28), channel_id=1, source_target_pairs={{0,16},{2,18},{4,20},{6,22},{8,24},{10,26},{12,28},{14,30},{16,0},... | collective-permute-start | bytes 294920 | tf_op jit(solution)/shard_map/ppermute | solution.py:535

commit v12 on v8

--- a/solution.py
+++ b/solution.py
@@ -410,7 +410,7 @@
         compiler_params=large,
         cost_estimate=pl.CostEstimate(flops=64 * work, bytes_accessed=work, transcendentals=0),
         name="forward",
-    )(block_seeds, flat)
+    )(pltpu.with_memory_space_constraint(block_seeds, pltpu.HBM), flat)
     n_grp = n_dev // 2
     n_p = math.gcd(P_SIZE, n_grp)
     n_r = n_grp // n_p

time: 125 us -> 125 us (level)
  no operation moved by 1% of the time
where the time goes in v12:
time: 125 us; the launch traced here: 124 us
  blocking collectives  76.2 us (61%)
  Pallas kernels  36.2 us (29%)
  waiting for transfers between devices  6.99 us (6%)
  starting transfers between devices  4.71 us (4%)
    all_to_all x1, blocking collectives, shards(): lax.all_to_all(t, ('row', 'col'), 0, 0, axis_index_groups=halves, tiled=T...  26.6 us
    all_to_all x1, blocking collectives, shards(): lax.all_to_all(f, ('row', 'col'), 0, 0, axis_index_groups=halves, tiled=T...  23.3 us
    all_to_all x1, blocking collectives, shards(): lax.all_to_all(summed, 'row', 0, 0, axis_index_groups=groups, tiled=True)  14.6 us
    all_to_all x1, blocking collectives, shards(): gram = lax.all_to_all(gram, ('row', 'col'), 0, 0, tiled=True)  11.7 us
    pallas_call x1, Pallas kernels, shards(): pl.pallas_call(lambda *refs: forward_kernel(local, n_freq, *refs), out_sh...  10.6 us
    pallas_call x1, Pallas kernels, shards(): pl.pallas_call(lambda *refs: separate_kernel(local, *refs), grid=(2 * n_r...  10.2 us
    pallas_call x1, Pallas kernels, shards(): pl.pallas_call(lambda *refs: backward_kernel(local, n_blocks, n_ready, *r...  9.13 us
    ppermute x2, waiting for transfers between devices, shards(): got = lax.ppermute(send, 'row', across)  5.08 us
  transfers between devices with their start and end apart: 3, of which 2 were waited for; matrix products, arithmetic and copies ran while one was open for 0% of the time, Pallas kernels for 9%

profile of v12, /device:TPU:0, one launch (start us, length us, event | category | flops | bytes accessed | tf_op | source)
XLA Modules:
  0.0 124.4 jit_solution(17216392355262280686)
XLA Ops:
  0.0 10.6 %forward.1 = bf16[32,16,1536]{2,1,0:T(8,128)(2,1)S(1)} custom-call(s32[32]{0:T(128)} %refs_0_.3, bf16[6144,1536]{1,0:T(8,128)(2,1)} %bitcast.12), custom_call_target="tpu_custom_call" | custom-call | flops 1207959552 | bytes 18874368 | tf_op jit(solution)/shard_map/forward/pallas_call | solution.py:391
  10.6 0.0 copy-start.1
  10.6 26.6 %all_to_all.20 = bf16[16,32,1536]{2,1,0:T(8,128)(2,1)S(1)} all-to-all(bf16[16,32,1536]{2,1,0:T(8,128)(2,1)S(1)} %bitcast.10), channel_id=1, replica_groups={{0,1,2,3,4,5,6,7,8,9,10,11,12,13,14,15},{16,17,18,19,20,21,22,23,24,25,..., dimensions={0} | all-to-all | bytes 3145728 | tf_op jit(solution)/shard_map/all_to_all | solution.py:422
  37.2 0.0 copy-done.1
  37.2 0.4 gather.1
  37.6 2.6 %collective-permute-start = (bf16[2,32,1536]{2,1,0:T(8,128)(2,1)S(1)}, bf16[2,32,1536]{2,1,0:T(8,128)(2,1)S(1)}, u32[]{:S(2)}, u32[]{:S(2)}) collective-permute-start(bf16[2,32,1536]{2,1,0:T(8,128)(2,1)S(1)} %get-tuple-element.20), channel_id=1, source_target_pairs={{0,16},{2,18},{4,20},{6,22},{8,24},{10,26},{12,28},{14,30},{16,0},... | collective-permute-start | bytes 589832 | tf_op jit(solution)/shard_map/ppermute | solution.py:442
  40.2 0.5 blocks.1.refs_1_
  40.7 0.0 copy-start
  40.7 10.2 %separate.1.refs_3_ = bf16[8,512,1536]{2,1,0:T(8,128)(2,1)} custom-call(bf16[6144,1536]{1,0:T(8,128)(2,1)} %bitcast.13), custom_call_target="tpu_custom_call" | custom-call | flops 18874368 | bytes 37748736 | tf_op jit(solution)/shard_map/separate/pallas_call | solution.py:456
  50.9 0.0 collective-permute-done.refs_2_
  50.9 0.0 copy-done
  50.9 0.4 scatter.1
  51.3 23.3 %all_to_all.21 = bf16[16,32,1536]{2,1,0:T(8,128)(2,1)S(1)} all-to-all(bf16[16,32,1536]{2,1,0:T(8,128)(2,1)S(1)} %bitcast.9), channel_id=1, replica_groups={{0,1,2,3,4,5,6,7,8,9,10,11,12,13,14,15},{16,17,18,19,20,21,22,23,24,25,..., dimensions={0} | all-to-all | bytes 3145728 | tf_op jit(solution)/shard_map/all_to_all | solution.py:477
  74.5 9.1 %backward.1 = (f32[16,32,768]{2,1,0:T(8,128)S(1)}, bf16[16,32,768]{2,1,0:T(8,128)(2,1)S(1)}) custom-call(bf16[512,1536]{1,0:T(8,128)(2,1)S(1)} %bitcast.7, bf16[2,512,256]{2,1,0:T(8,128)(2,1)S(1)} %blocks.1.refs_1_, bf16[6144,1536]{1,0:T(8,128)(2,1)} %bitcast.14, bf16[8,512,1536]{2,1,0:T(8,128)(2,1)} %separate.1.refs_3_), custom_call_target="tpu_custom_call" | custom-call | flops 1207959552 | bytes 18874368 | tf_op jit(solution)/shard_map/backward/pallas_call | solution.py:483
  83.7 0.5 collective-permute-start.1
  84.2 1.9 %collective-permute-done.1 = bf16[16,32,768]{2,1,0:T(8,128)(2,1)S(1)} collective-permute-done((bf16[16,32,768]{2,1,0:T(8,128)(2,1)S(1)}, bf16[16,32,768]{2,1,0:T(8,128)(2,1)S(1)}, u32[]{:S(2)}, u32[]{:S(2)}) %collective-permute-start.1) | collective-permute-done | bytes 786464 | tf_op jit(solution)/shard_map/ppermute | solution.py:504
  86.1 0.2 add_convert_fusion
  86.4 14.6 %all_to_all.22 = bf16[16,32,768]{2,1,0:T(8,128)(2,1)S(1)} all-to-all(bf16[16,32,768]{2,1,0:T(8,128)(2,1)S(1)} %add_convert_fusion), channel_id=1, replica_groups={{0,4,8,12},{2,6,10,14},{16,20,24,28},{18,22,26,30},{1,5,9,13},{3,7,11,1..., dimensions={0} | all-to-all | bytes 1572864 | tf_op jit(solution)/shard_map/all_to_all | solution.py:507
  100.9 0.1 join.1
  101.0 1.6 %collective-permute-start.2 = (bf16[2,32,768]{2,1,0:T(8,128)(2,1)S(1)}, bf16[2,32,768]{2,1,0:T(8,128)(2,1)S(1)}, u32[]{:S(2)}, u32[]{:S(2)}) collective-permute-start(bf16[2,32,768]{2,1,0:T(8,128)(2,1)S(1)} %get-tuple-element.28), channel_id=1, source_target_pairs={{0,16},{2,18},{4,20},{6,22},{8,24},{10,26},{12,28},{14,30},{16,0},... | collective-permute-start | bytes 294920 | tf_op jit(solution)/shard_map/ppermute | solution.py:520
  102.6 5.1 %collective-permute-done.2.got_ref = bf16[2,32,768]{2,1,0:T(8,128)(2,1)S(1)} collective-permute-done((bf16[2,32,768]{2,1,0:T(8,128)(2,1)S(1)}, bf16[2,32,768]{2,1,0:T(8,128)(2,1)S(1)}, u32[]{:S(2)}, u32[]{:S(2)}) %collective-permute-start.2) | collective-permute-done | bytes 98336 | tf_op jit(solution)/shard_map/ppermute | solution.py:520
  107.7 0.4 gram.1
  108.0 11.7 %all_to_all.23.refs_0_ = f32[32,8,128]{2,1,0:T(8,128)S(1)} all-to-all(f32[32,8,128]{2,1,0:T(8,128)S(1)} %get-tuple-element.29), channel_id=1, replica_groups=mesh['row'=16,'col'=2] {'row','col'}, dimensions={0} | all-to-all | bytes 262144 | tf_op jit(solution)/shard_map/all_to_all | solution.py:533
  119.8 4.6 %last.1 = f32[2,32,768]{2,1,0:T(8,128)} custom-call(f32[32,8,128]{2,1,0:T(8,128)S(1)} %all_to_all.23.refs_0_, f32[2,32,768]{2,1,0:T(8,128)S(1)} %get-tuple-element.30.refs_1_), custom_call_target="tpu_custom_call" | custom-call | tf_op jit(solution)/shard_map/last/pallas_call | solution.py:534
Async XLA Ops:
  10.6 26.6 %copy-start.1 = (bf16[2,64,256]{2,1,0:T(8,128)(2,1)S(1)}, bf16[2,64,256]{2,1,0:T(8,128)(2,1)}, u32[]{:S(2)}) copy-start(bf16[2,64,256]{2,1,0:T(8,128)(2,1)} %constant.4.clone.refs_0_) | copy-start | bytes 196612
  37.6 13.3 %collective-permute-start = (bf16[2,32,1536]{2,1,0:T(8,128)(2,1)S(1)}, bf16[2,32,1536]{2,1,0:T(8,128)(2,1)S(1)}, u32[]{:S(2)}, u32[]{:S(2)}) collective-permute-start(bf16[2,32,1536]{2,1,0:T(8,128)(2,1)S(1)} %get-tuple-element.20), channel_id=1, source_target_pairs={{0,16},{2,18},{4,20},{6,22},{8,24},{10,26},{12,28},{14,30},{16,0},... | collective-permute-start | bytes 589832 | tf_op jit(solution)/shard_map/ppermute | solution.py:442
  40.7 10.2 %copy-start = (bf16[2,128,96]{2,1,0:T(8,128)(2,1)S(1)}, bf16[2,128,96]{2,1,0:T(8,128)(2,1)}, u32[]{:S(2)}) copy-start(bf16[2,128,96]{2,1,0:T(8,128)(2,1)} %constant.5.clone.refs_0_) | copy-start | bytes 147460
  83.7 2.4 %collective-permute-start.1 = (bf16[16,32,768]{2,1,0:T(8,128)(2,1)S(1)}, bf16[16,32,768]{2,1,0:T(8,128)(2,1)S(1)}, u32[]{:S(2)}, u32[]{:S(2)}) collective-permute-start(bf16[16,32,768]{2,1,0:T(8,128)(2,1)S(1)} %get-tuple-element.26), channel_id=1, source_target_pairs={{0,2},{2,0},{4,6},{6,4},{8,10},{10,8},{12,14},{14,12},{16,18},{18,... | collective-permute-start | bytes 2359304 | tf_op jit(solution)/shard_map/ppermute | solution.py:504
  101.0 6.6 %collective-permute-start.2 = (bf16[2,32,768]{2,1,0:T(8,128)(2,1)S(1)}, bf16[2,32,768]{2,1,0:T(8,128)(2,1)S(1)}, u32[]{:S(2)}, u32[]{:S(2)}) collective-permute-start(bf16[2,32,768]{2,1,0:T(8,128)(2,1)S(1)} %get-tuple-element.28), channel_id=1, source_target_pairs={{0,16},{2,18},{4,20},{6,22},{8,24},{10,26},{12,28},{14,30},{16,0},... | collective-permute-start | bytes 294920 | tf_op jit(solution)/shard_map/ppermute | solution.py:520
